TPU v7x, 32 devices: a whole 2x2x4 slice. The times are simulated.
32 devices in a mesh: rep: 8 (over z, core), slab: 4 (over y, x).
Axes of the slice: x: 2, y: 2, z: 4, core: 2. Of those that a mesh axis runs over, the one named last changes fastest.
Arguments:
- inputs: bfloat16 [8, 32, 32, 16, 128], P('rep', 'slab'), may hold values from -6 to 6
- pre_act: bfloat16 [8, 32, 32, 16, 128], P('rep', 'slab'), may hold values from -8 to 8
- cotangent: bfloat16 [8, 32, 32, 16, 128], P('rep', 'slab'), may hold values from -6 to 6
- weight_one: bfloat16 [27, 128, 128], replicated, may hold values from -0.109375 to 0.109375
- weight_two: bfloat16 [27, 128, 128], replicated, may hold values from -0.109375 to 0.109375
Outputs:
- input_grad: bfloat16 [8, 32, 32, 16, 128], P('rep', 'slab')
- grad_one: float32 [27, 128, 128], P(None, 'rep')
- grad_two: float32 [27, 128, 128], P(None, 'rep')
All inputs are finite; a program needn't handle non-finite values.
Results may differ from a plain program's by a relative error of at most 0.0049.
Values may be sent and summed in bfloat16 or wider, within the bound.
No kernel may reach another device: no remote copies, remote signals or barrier semaphores. Data moves between devices by JAX's collectives and lax.ppermute only.
A program may use at most 128 MiB of HBM per device.

v0:
```python
import functools
import math

import jax
import jax.numpy as jnp
from jax import lax
from jax.experimental import pallas as pl
from jax.experimental.pallas import tpu as pltpu
from jax.sharding import PartitionSpec as P

F32 = jnp.float32
BF16 = jnp.bfloat16
MIB = 2**20
VMEM = pl.BlockSpec(memory_space=pltpu.VMEM)
SMEM = pl.BlockSpec(memory_space=pltpu.SMEM)


def sigmoid(value):
    return 1.0 / (1.0 + jnp.exp(-value))


def clear_rows(var):
    shape = (var.shape[0], var.shape[1]) + var.shape[3:]
    zeros = jnp.zeros(shape, var.dtype)
    var[:, :, 0] = zeros
    var[:, :, var.shape[2] - 1] = zeros


def fill_plane(var, plane, x):
    height, width, _ = x.shape
    wide = x.astype(F32)
    place = lax.broadcasted_iota(jnp.int32, x.shape, 1)
    rows = slice(1, height + 1)
    later = pltpu.roll(wide, width - 1, 1)
    var[0, plane, rows] = jnp.where(place < width - 1, later, 0.0).astype(x.dtype)
    var[1, plane, rows] = x
    earlier = pltpu.roll(wide, 1, 1)
    var[2, plane, rows] = jnp.where(place > 0, earlier, 0.0).astype(x.dtype)


def fill_weights(tiles, w_ref):
    ch = w_ref.shape[1]
    zero = jnp.zeros((ch, ch), tiles.dtype)

    def one(j, carry):
        a, c = j // 3, j % 3
        low, mid, high = (w_ref[9 * a + 3 * b + c].T for b in range(3))
        tiles[j, 0, :ch, :ch] = mid
        tiles[j, 0, :ch, ch:] = high
        tiles[j, 0, ch:, :ch] = low
        tiles[j, 0, ch:, ch:] = mid
        tiles[j, 1, :ch, :ch] = high
        tiles[j, 1, :ch, ch:] = zero
        tiles[j, 1, ch:, :ch] = zero
        tiles[j, 1, ch:, ch:] = low
        return carry

    lax.fori_loop(0, 9, one, 0)


def back_plane(var, tiles, d):
    half = (var.shape[2] - 2) // 2
    width, ch = var.shape[3:]
    flat = lambda u: u.reshape(half * width, ch)
    acc = jnp.zeros((half * width, 2 * ch), F32)
    for j in range(9):
        a, c = j // 3, j % 3
        x = var[c, d + 2 - a].reshape(half + 1, 2, width, ch)
        inner = jnp.concatenate([flat(x[:half, 1]), flat(x[1:, 0])], 1)
        outer = jnp.concatenate([flat(x[:half, 0]), flat(x[1:, 1])], 1)
        acc += jnp.dot(inner, tiles[j, 0], preferred_element_type=F32)
        acc += jnp.dot(outer, tiles[j, 1], preferred_element_type=F32)
    return acc


def paired(x):
    height, width, ch = x.shape
    x = x.reshape(height // 2, 2, width, ch)
    return jnp.concatenate([x[:, i].reshape(height // 2 * width, ch) for i in range(2)], 1)


def unpaired(v, height, width):
    ch = v.shape[1] // 2
    parts = [v[:, i * ch : (i + 1) * ch].reshape(height // 2, width, ch) for i in range(2)]
    return jnp.stack(parts, axis=1).reshape(height, width, ch)


def transpose_plane(dst, plane, x):
    height, width, ch = x.shape
    n = height * width
    dst[:, pl.ds(pl.multiple_of(plane * n, n), n)] = x.reshape(n, ch).T


def store_tap(keep_ref, send_ref, core, tap, value, ranks):
    ch = value.shape[0]
    blocks = value.reshape(ranks // 2, 2, ch // ranks, value.shape[1])
    even = blocks[:, 0].reshape(ch // 2, value.shape[1])
    odd = blocks[:, 1].reshape(ch // 2, value.shape[1])
    keep_ref[tap] = jnp.where(core == 0, even, odd)
    send_ref[tap] = jnp.where(core == 0, odd, even).astype(send_ref.dtype)


def clear_tail(keep_ref, send_ref, taps):
    for t in range(taps, keep_ref.shape[0]):
        keep_ref[t] = jnp.zeros(keep_ref.shape[1:], keep_ref.dtype)
        send_ref[t] = jnp.zeros(send_ref.shape[1:], send_ref.dtype)


def prepare_kernel(pre_ref, w1_ref, w2_ref, act_t_ref, tiles1_ref, tiles2_ref):
    def plane(d, carry):
        v = pre_ref[d].astype(F32)
        transpose_plane(act_t_ref, d, (v * sigmoid(v)).astype(BF16))
        return carry

    lax.fori_loop(0, pre_ref.shape[0], plane, 0)
    fill_weights(tiles2_ref, w2_ref)
    fill_weights(tiles1_ref, w1_ref)


def second_kernel(
    ranks, taps, where_ref, cot_ref, far_a_ref, far_b_ref, pre_ref, act_t_ref, tiles_ref,
    hidden_ref, keep_ref, send_ref, var,
):
    depth, height, width, ch = cot_ref.shape
    even, core = where_ref[0] == 0, where_ref[1]
    clear_rows(var)
    far_a, far_b = far_a_ref[...], far_b_ref[...]
    fill_plane(var, 0, jnp.where(even, far_b, far_a))
    fill_plane(var, depth + 1, jnp.where(even, far_a, far_b))

    def prep(d, carry):
        fill_plane(var, d + 1, cot_ref[d])
        return carry

    lax.fori_loop(0, depth, prep, 0)

    def plane(d, carry):
        back = back_plane(var, tiles_ref, d)
        v = paired(pre_ref[d]).astype(F32)
        s = sigmoid(v)
        grad = back * (s * (1.0 + v * (1.0 - s)))
        hidden_ref[d] = unpaired(grad.astype(BF16), height, width)
        return carry

    lax.fori_loop(0, depth, plane, 0)
    voxels = depth * height * width

    def pair(i, carry):
        one, two = 2 * i, jnp.minimum(2 * i + 1, taps - 1)
        rights = []
        for t in (one, two):
            a, b, c = t // 9, (t // 3) % 3, t % 3
            rights.append(
                var[c, pl.ds(2 - a, depth), pl.ds(2 - b, height)].reshape(voxels, ch)
            )
        r = jnp.dot(act_t_ref[...], jnp.concatenate(rights, 1), preferred_element_type=F32)
        store_tap(keep_ref, send_ref, core, two, r[:, ch:], ranks)
        store_tap(keep_ref, send_ref, core, one, r[:, :ch], ranks)
        return carry

    lax.fori_loop(0, (taps + 1) // 2, pair, 0)
    clear_tail(keep_ref, send_ref, taps)


def first_kernel(
    ranks, taps, where_ref, in_ref, far_a_ref, far_b_ref, hidden_ref, keep_ref, send_ref, var, in_t
):
    depth, height, width, ch = in_ref.shape
    even, core = where_ref[0] == 0, where_ref[1]
    clear_rows(var)
    far_a, far_b = far_a_ref[...], far_b_ref[...]
    transpose_plane(in_t, 0, jnp.where(even, far_b, far_a))
    transpose_plane(in_t, depth + 1, jnp.where(even, far_a, far_b))

    def prep(d, carry):
        fill_plane(var, d, hidden_ref[d])
        transpose_plane(in_t, d + 1, in_ref[d])
        return carry

    lax.fori_loop(0, depth, prep, 0)
    voxels, n = depth * height * width, height * width

    def pair(i, carry):
        a, j = i // 5, i % 5
        one, two = 2 * j, jnp.minimum(2 * j + 1, 8)
        rights = []
        for t in (one, two):
            b, c = t // 3, t % 3
            rights.append(var[c, :, pl.ds(2 - b, height)].reshape(voxels, ch))
        left = in_t[:, pl.ds(pl.multiple_of(a * n, n), voxels)]
        r = jnp.dot(left, jnp.concatenate(rights, 1), preferred_element_type=F32)
        store_tap(keep_ref, send_ref, core, 9 * a + two, r[:, ch:], ranks)
        store_tap(keep_ref, send_ref, core, 9 * a + one, r[:, :ch], ranks)
        return carry

    lax.fori_loop(0, 15, pair, 0)
    clear_tail(keep_ref, send_ref, taps)


def input_kernel(where_ref, hidden_ref, far_a_ref, far_b_ref, tiles_ref, out_ref, var):
    depth, height, width, _ = hidden_ref.shape
    even = where_ref[0] == 0
    clear_rows(var)
    far_a, far_b = far_a_ref[...], far_b_ref[...]
    fill_plane(var, 0, jnp.where(even, far_b, far_a))
    fill_plane(var, depth + 1, jnp.where(even, far_a, far_b))

    def prep(d, carry):
        fill_plane(var, d + 1, hidden_ref[d])
        return carry

    lax.fori_loop(0, depth, prep, 0)

    def plane(d, carry):
        out_ref[d] = unpaired(back_plane(var, tiles_ref, d).astype(BF16), height, width)
        return carry

    lax.fori_loop(0, depth, plane, 0)


def call(body, out_shape, operands, scratch, flops, n_smem=0):
    moved = sum(x.size * x.dtype.itemsize for x in operands)
    return pl.pallas_call(
        body,
        out_shape=out_shape,
        in_specs=[SMEM] * n_smem + [VMEM] * (len(operands) - n_smem),
        out_specs=jax.tree.map(lambda _: VMEM, out_shape),
        scratch_shapes=scratch,
        compiler_params=pltpu.CompilerParams(vmem_limit_bytes=24 * MIB),
        cost_estimate=pl.CostEstimate(flops=flops, bytes_accessed=moved, transcendentals=0),
    )(*operands)


def partner(i, k, n):
    return i ^ k if n & (n - 1) == 0 else (i + k) % n


def swap_faces(x, even):
    peers = lax.axis_size("slab")
    first, last = x[0], x[-1]
    a = [(i, i ^ 1) for i in range(peers) if i ^ 1 < peers]
    b = [(i, j) for i in range(peers) for j in [((i + 1) ^ 1) - 1] if 0 <= j < peers]
    to_a = jnp.where(even, last, first)
    to_b = jnp.where(even, first, last)
    return lax.ppermute(to_a, "slab", a), lax.ppermute(to_b, "slab", b)


def swap_cores(send):
    ranks = lax.axis_size("rep")
    return lax.ppermute(send, "rep", [(i, i ^ 1) for i in range(ranks)])


def scatter_slab(total):
    peers, me = lax.axis_size("slab"), lax.axis_index("slab")
    count = total.shape[0] // peers
    out = lax.dynamic_slice_in_dim(total, me * count, count, 0)
    for k in range(1, peers):
        other = partner(me, k, peers)
        piece = lax.dynamic_slice_in_dim(total, other * count, count, 0).astype(BF16)
        got = lax.ppermute(piece, "slab", [(i, partner(i, k, peers)) for i in range(peers)])
        out = out + got.astype(F32)
    return out


def scatter_ranks(total):
    ranks, me = lax.axis_size("rep"), lax.axis_index("rep")
    peers = ranks // 2
    dim = total.ndim - 2
    count = total.shape[dim] // peers
    out = lax.dynamic_slice_in_dim(total, me // 2 * count, count, dim)
    for k in range(1, peers):
        other = partner(me // 2, k, peers)
        piece = lax.dynamic_slice_in_dim(total, other * count, count, dim).astype(BF16)
        perm = [(i, 2 * partner(i // 2, k, peers) + i % 2) for i in range(ranks)]
        out = out + lax.ppermute(piece, "rep", perm).astype(F32)
    return out


def gather_slab(part):
    peers, me = lax.axis_size("slab"), lax.axis_index("slab")
    count = part.shape[1]
    shape = (part.shape[0], count * peers) + part.shape[2:]
    out = lax.dynamic_update_slice_in_dim(jnp.zeros(shape, part.dtype), part, me * count, 1)
    for k in range(1, peers):
        perm = [(i, partner(i, k, peers)) for i in range(peers)]
        got = lax.ppermute(part, "slab", perm)
        source = partner(me, k, peers) if peers & (peers - 1) == 0 else (me - k) % peers
        out = lax.dynamic_update_slice_in_dim(out, got, source * count, 1)
    return out


def shards(inputs, pre_act, cotangent, weight_one, weight_two):
    volume_in, pre, cot = inputs[0], pre_act[0], cotangent[0]
    depth, height, width, ch = cot.shape
    taps = weight_one.shape[0]
    ranks, slabs = lax.axis_size("rep"), lax.axis_size("slab")
    padded_taps = -(-taps // slabs) * slabs
    voxels = depth * height * width
    even = lax.axis_index("slab") % 2 == 0
    where = jnp.stack([lax.axis_index("slab") % 2, lax.axis_index("rep") % 2]).astype(jnp.int32)
    s = jax.ShapeDtypeStruct
    sweep = 2 * taps * voxels * ch * ch
    tile_shape = s((9, 2, 2 * ch, 2 * ch), BF16)
    padded = pltpu.VMEM((3, depth + 2, height + 2, width, ch), BF16)
    term_shapes = (
        s((padded_taps, ch // 2, ch), F32),
        s((padded_taps, ch // 2, ch), BF16),
    )

    cot_a, cot_b = swap_faces(cot, even)
    act_t, tiles1, tiles2 = call(
        prepare_kernel,
        (s((ch, voxels), BF16), tile_shape, tile_shape),
        (pre, weight_one, weight_two), [], sweep // 4,
    )
    in_a, in_b = swap_faces(volume_in, even)
    hidden, keep2, send2 = call(
        functools.partial(second_kernel, ranks, taps),
        (s(cot.shape, BF16),) + term_shapes,
        (where, cot, cot_a, cot_b, pre, act_t, tiles2), [padded], 2 * sweep, 1,
    )
    hid_a, hid_b = swap_faces(hidden, even)
    got2 = swap_cores(send2)
    keep1, send1 = call(
        functools.partial(first_kernel, ranks, taps),
        term_shapes,
        (where, volume_in, in_a, in_b, hidden),
        [
            pltpu.VMEM((3, depth, height + 2, width, ch), BF16),
            pltpu.VMEM((ch, (depth + 2) * height * width), BF16),
        ],
        sweep, 1,
    )
    got1 = swap_cores(send1)
    input_grad = call(
        input_kernel, s(cot.shape, BF16), (where, hidden, hid_a, hid_b, tiles1), [padded], sweep, 1
    )
    part2 = scatter_slab(keep2 + got2.astype(F32))
    part1 = scatter_slab(keep1 + got1.astype(F32))
    factor = 1.0 / math.sqrt(ranks * slabs * voxels)
    mine = scatter_ranks(jnp.stack([part1, part2])) * factor
    grads = gather_slab(mine)[:, :taps]
    return (input_grad[None], grads[0], grads[1])


def solution(mesh):
    volumes = P("rep", "slab", None, None, None)
    kernels = P(None, "rep", None)
    return jax.shard_map(
        shards,
        mesh=mesh,
        in_specs=(volumes, volumes, volumes, P(), P()),
        out_specs=(volumes, kernels, kernels),
        check_vma=False,
    )
```

profile of v0, /device:TPU:0, one launch (start us, length us, event | category | flops | bytes accessed | tf_op | source)
XLA Modules:
  0.0 98.1 jit_solution(4113523085778036768)
XLA Ops:
  0.7 1.1 %select_bitcast_fusion.4 = (bf16[32,16,128]{2,1,0:T(8,128)(2,1)S(1)}, bf16[32,16,128]{2,1,0:T(8,128)(2,1)S(1)}) fusion(pred[]{:T(512)S(6)} %eq.7, bf16[1,8,32,16,128]{4,3,2,1,0:T(8,128)(2,1)} %param.7), kind=kLoop, calls=%fused_computation.24 | loop fusion | flops 131072 | bytes 524289 | tf_op jit(solution)/shard_map/jit(_where)/select_n | solution.py:244
  1.7 3.0 %collective-permute-start = (bf16[32,16,128]{2,1,0:T(8,128)(2,1)S(1)}, bf16[32,16,128]{2,1,0:T(8,128)(2,1)S(1)}, u32[]{:S(2)}, u32[]{:S(2)}) collective-permute-start(bf16[32,16,128]{2,1,0:T(8,128)(2,1)S(1)} %get-tuple-element.26), channel_id=1, source_target_pairs={{0,1},{1,0},{2,3},{3,2},{4,5},{5,4},{6,7},{7,6},{8,9},{9,8},{10,11... | collective-permute-start | bytes 393224 | tf_op jit(solution)/shard_map/ppermute | solution.py:245
  4.8 0.7 collective-permute-start.1
  5.4 1.7 %select_bitcast_fusion = (bf16[32,16,128]{2,1,0:T(8,128)(2,1)}, bf16[32,16,128]{2,1,0:T(8,128)(2,1)}) fusion(pred[]{:T(512)S(6)} %eq.7, bf16[1,8,32,16,128]{4,3,2,1,0:T(8,128)(2,1)} %param.5), kind=kLoop, calls=%fused_computation.20 | loop fusion | flops 131072 | bytes 524289 | tf_op jit(solution)/shard_map/jit(_where)/select_n | solution.py:244
  7.1 4.2 %collective-permute-start.4 = (bf16[32,16,128]{2,1,0:T(8,128)(2,1)}, bf16[32,16,128]{2,1,0:T(8,128)(2,1)S(1)}, u32[]{:S(2)}, u32[]{:S(2)}) collective-permute-start(bf16[32,16,128]{2,1,0:T(8,128)(2,1)} %get-tuple-element.22), channel_id=1, source_target_pairs={{0,1},{1,0},{2,3},{3,2},{4,5},{5,4},{6,7},{7,6},{8,9},{9,8},{10,11... | collective-permute-start | bytes 393224 | tf_op jit(solution)/shard_map/ppermute | solution.py:245
  11.3 0.7 collective-permute-start.5
  12.0 1.2 %copy-done.4 = bf16[1,8,32,16,128]{4,3,2,1,0:T(8,128)(2,1)S(1)} copy-done((bf16[1,8,32,16,128]{4,3,2,1,0:T(8,128)(2,1)S(1)}, bf16[1,8,32,16,128]{4,3,2,1,0:T(8,128)(2,1)}, u32[]{:S(2)}) %copy-start.4) | copy-done | bytes 1048600
  13.2 1.2 %copy-done.6 = bf16[27,128,128]{2,1,0:T(8,128)(2,1)S(1)} copy-done((bf16[27,128,128]{2,1,0:T(8,128)(2,1)S(1)}, bf16[27,128,128]{2,1,0:T(8,128)(2,1)}, u32[]{:S(2)}) %copy-start.6) | copy-done | bytes 884760
  14.4 1.2 %copy-done.7 = bf16[27,128,128]{2,1,0:T(8,128)(2,1)S(1)} copy-done((bf16[27,128,128]{2,1,0:T(8,128)(2,1)S(1)}, bf16[27,128,128]{2,1,0:T(8,128)(2,1)}, u32[]{:S(2)}) %copy-start.7) | copy-done | bytes 884760
  15.6 2.8 %shard_map.76 = (bf16[128,4096]{1,0:T(8,128)(2,1)S(1)}, bf16[9,2,256,256]{3,2,1,0:T(8,128)(2,1)S(1)}, bf16[9,2,256,256]{3,2,1,0:T(8,128)(2,1)S(1)}) custom-call(bf16[8,32,16,128]{3,2,1,0:T(8,128)(2,1)S(1)} %bitcast.28, bf16[27,128,128]{2,1,0:T(8,128)(2,1)S(1)} %copy-done.6, bf16[27,128,128]{2,1,0:T(8,128)(2,1)S(1)} %copy-done.7), custom_call_target="tpu_custom_call" | custom-call | flops 905969664 | bytes 2818048 | tf_op jit(solution)/shard_map/pallas_call | solution.py:223
  18.4 1.4 %copy-done.10 = bf16[9,2,256,256]{3,2,1,0:T(8,128)(2,1)} copy-done((bf16[9,2,256,256]{3,2,1,0:T(8,128)(2,1)}, bf16[9,2,256,256]{3,2,1,0:T(8,128)(2,1)S(1)}, u32[]{:S(2)}) %copy-start.10) | copy-done | bytes 2359320
  19.8 1.4 %copy-done.12 = bf16[9,2,256,256]{3,2,1,0:T(8,128)(2,1)} copy-done((bf16[9,2,256,256]{3,2,1,0:T(8,128)(2,1)}, bf16[9,2,256,256]{3,2,1,0:T(8,128)(2,1)S(1)}, u32[]{:S(2)}) %copy-start.12) | copy-done | bytes 2359320
  21.3 1.0 copy-done.14
  22.2 0.1 pad_add_fusion.where_ref
  22.3 1.2 %copy-done.5 = bf16[1,8,32,16,128]{4,3,2,1,0:T(8,128)(2,1)S(1)} copy-done((bf16[1,8,32,16,128]{4,3,2,1,0:T(8,128)(2,1)S(1)}, bf16[1,8,32,16,128]{4,3,2,1,0:T(8,128)(2,1)}, u32[]{:S(2)}) %copy-start.5) | copy-done | bytes 1048600
  23.6 1.7 %copy-done.13 = bf16[9,2,256,256]{3,2,1,0:T(8,128)(2,1)S(1)} copy-done((bf16[9,2,256,256]{3,2,1,0:T(8,128)(2,1)S(1)}, bf16[9,2,256,256]{3,2,1,0:T(8,128)(2,1)}, u32[]{:S(2)}) %copy-start.13) | copy-done | bytes 2359320
  25.2 1.2 %copy-done.15 = bf16[128,4096]{1,0:T(8,128)(2,1)S(1)} copy-done((bf16[128,4096]{1,0:T(8,128)(2,1)S(1)}, bf16[128,4096]{1,0:T(8,128)(2,1)}, u32[]{:S(2)}) %copy-start.15) | copy-done | bytes 1048600
  26.5 14.8 %shard_map.77 = (bf16[8,32,16,128]{3,2,1,0:T(8,128)(2,1)S(1)}, f32[28,64,128]{2,1,0:T(8,128)S(1)}, bf16[28,64,128]{2,1,0:T(8,128)(2,1)S(1)}) custom-call(s32[2]{0:T(128)S(1)} %pad_add_fusion.where_ref, bf16[8,32,16,128]{3,2,1,0:T(8,128)(2,1)S(1)} %bitcast.26, bf16[32,16,128]{2,1,0:T(8,128)(2,1)S(1)} %collective-permute-done.far_a_ref, ...), custom_call_target="tpu_custom_call" | custom-call | flops 7247757312 | bytes 5767176 | tf_op jit(solution)/shard_map/pallas_call | solution.py:223
  41.4 0.8 copy-done.8
  42.2 0.9 copy-done.9
  43.1 9.3 %shard_map.79 = (f32[28,64,128]{2,1,0:T(8,128)S(1)}, bf16[28,64,128]{2,1,0:T(8,128)(2,1)S(1)}) custom-call(s32[2]{0:T(128)S(1)} %pad_add_fusion.where_ref, bf16[8,32,16,128]{3,2,1,0:T(8,128)(2,1)S(1)} %bitcast.27, bf16[32,16,128]{2,1,0:T(8,128)(2,1)S(1)} %collective-permute-done.4.far_a_ref, bf16[32,16,128]{2,1,0:T(8,128)(2,1)S(1)} %copy-done.9, ...), custom_call_target="tpu_custom_call" | custom-call | flops 3623878656 | bytes 2359304 | tf_op jit(solution)/shard_map/pallas_call | solution.py:223
  52.4 0.4 collective-permute-start.6
  52.8 0.1 convert_add_fusion
  53.0 1.3 %collective-permute-start.11 = (bf16[7,64,128]{2,1,0:T(8,128)(2,1)S(1)}, bf16[7,64,128]{2,1,0:T(8,128)(2,1)S(1)}, u32[]{:S(2)}, u32[]{:S(2)}) collective-permute-start(bf16[7,64,128]{2,1,0:T(8,128)(2,1)S(1)} %get-tuple-element.27), channel_id=1, source_target_pairs={{0,1},{1,0},{2,3},{3,2},{4,5},{5,4},{6,7},{7,6},{8,9},{9,8},{10,11... | collective-permute-start | bytes 344072 | tf_op jit(solution)/shard_map/ppermute | solution.py:260
  54.3 1.5 %collective-permute-start.12 = (bf16[7,64,128]{2,1,0:T(8,128)(2,1)S(1)}, bf16[7,64,128]{2,1,0:T(8,128)(2,1)S(1)}, u32[]{:S(2)}, u32[]{:S(2)}) collective-permute-start(bf16[7,64,128]{2,1,0:T(8,128)(2,1)S(1)} %get-tuple-element.29), channel_id=1, source_target_pairs={{0,2},{1,3},{2,0},{3,1},{4,6},{5,7},{6,4},{7,5},{8,10},{9,11},{10,... | collective-permute-start | bytes 344072 | tf_op jit(solution)/shard_map/ppermute | solution.py:260
  55.8 1.4 %collective-permute-start.13 = (bf16[7,64,128]{2,1,0:T(8,128)(2,1)S(1)}, bf16[7,64,128]{2,1,0:T(8,128)(2,1)S(1)}, u32[]{:S(2)}, u32[]{:S(2)}) collective-permute-start(bf16[7,64,128]{2,1,0:T(8,128)(2,1)S(1)} %get-tuple-element.28), channel_id=1, source_target_pairs={{0,3},{1,2},{2,1},{3,0},{4,7},{5,6},{6,5},{7,4},{8,11},{9,10},{10,... | collective-permute-start | bytes 344072 | tf_op jit(solution)/shard_map/ppermute | solution.py:260
  57.2 1.2 %convert_add_fusion.1 = f32[28,64,128]{2,1,0:T(8,128)S(1)} fusion(f32[28,64,128]{2,1,0:T(8,128)S(1)} %get-tuple-element.15, bf16[28,64,128]{2,1,0:T(8,128)(2,1)} %collective-permute-done.6), kind=kLoop, calls=%fused_computation.1 | loop fusion | flops 458752 | bytes 2293760 | tf_op jit(solution)/shard_map/add | solution.py:339
  58.6 0.6 collective-permute-start.7
  59.2 1.5 %collective-permute-start.8 = (bf16[7,64,128]{2,1,0:T(8,128)(2,1)S(1)}, bf16[7,64,128]{2,1,0:T(8,128)(2,1)S(1)}, u32[]{:S(2)}, u32[]{:S(2)}) collective-permute-start(bf16[7,64,128]{2,1,0:T(8,128)(2,1)S(1)} %get-tuple-element.32), channel_id=1, source_target_pairs={{0,2},{1,3},{2,0},{3,1},{4,6},{5,7},{6,4},{7,5},{8,10},{9,11},{10,... | collective-permute-start | bytes 344072 | tf_op jit(solution)/shard_map/ppermute | solution.py:260
  60.7 1.4 %collective-permute-start.9 = (bf16[7,64,128]{2,1,0:T(8,128)(2,1)S(1)}, bf16[7,64,128]{2,1,0:T(8,128)(2,1)S(1)}, u32[]{:S(2)}, u32[]{:S(2)}) collective-permute-start(bf16[7,64,128]{2,1,0:T(8,128)(2,1)S(1)} %get-tuple-element.31), channel_id=1, source_target_pairs={{0,3},{1,2},{2,1},{3,0},{4,7},{5,6},{6,5},{7,4},{8,11},{9,10},{10,... | collective-permute-start | bytes 344072 | tf_op jit(solution)/shard_map/ppermute | solution.py:260
  62.1 1.6 %collective-permute-done.13 = bf16[7,64,128]{2,1,0:T(8,128)(2,1)S(1)} collective-permute-done((bf16[7,64,128]{2,1,0:T(8,128)(2,1)S(1)}, bf16[7,64,128]{2,1,0:T(8,128)(2,1)S(1)}, u32[]{:S(2)}, u32[]{:S(2)}) %collective-permute-start.13) | collective-permute-done | bytes 114720 | tf_op jit(solution)/shard_map/ppermute | solution.py:260
  63.7 0.8 collective-permute-done.7
  64.6 1.4 %collective-permute-done.8 = bf16[7,64,128]{2,1,0:T(8,128)(2,1)S(1)} collective-permute-done((bf16[7,64,128]{2,1,0:T(8,128)(2,1)S(1)}, bf16[7,64,128]{2,1,0:T(8,128)(2,1)S(1)}, u32[]{:S(2)}, u32[]{:S(2)}) %collective-permute-start.8) | collective-permute-done | bytes 114720 | tf_op jit(solution)/shard_map/ppermute | solution.py:260
  66.0 1.8 %collective-permute-done.9 = bf16[7,64,128]{2,1,0:T(8,128)(2,1)S(1)} collective-permute-done((bf16[7,64,128]{2,1,0:T(8,128)(2,1)S(1)}, bf16[7,64,128]{2,1,0:T(8,128)(2,1)S(1)}, u32[]{:S(2)}, u32[]{:S(2)}) %collective-permute-start.9) | collective-permute-done | bytes 114720 | tf_op jit(solution)/shard_map/ppermute | solution.py:260
  67.9 1.6 %collective-permute-start.14 = (bf16[2,7,16,128]{3,2,1,0:T(8,128)(2,1)S(1)}, bf16[2,7,16,128]{3,2,1,0:T(8,128)(2,1)S(1)}, u32[]{:S(2)}, u32[]{:S(2)}) collective-permute-start(bf16[2,7,16,128]{3,2,1,0:T(8,128)(2,1)S(1)} %get-tuple-element.35), channel_id=1, source_target_pairs={{0,8},{4,12},{8,0},{12,4},{16,24},{20,28},{24,16},{28,20},{1,9},{5... | collective-permute-start | bytes 172040 | tf_op jit(solution)/shard_map/ppermute | solution.py:275
  69.5 2.6 %collective-permute-start.15 = (bf16[2,7,16,128]{3,2,1,0:T(8,128)(2,1)S(1)}, bf16[2,7,16,128]{3,2,1,0:T(8,128)(2,1)S(1)}, u32[]{:S(2)}, u32[]{:S(2)}) collective-permute-start(bf16[2,7,16,128]{3,2,1,0:T(8,128)(2,1)S(1)} %get-tuple-element.36), channel_id=1, source_target_pairs={{0,16},{4,20},{8,24},{12,28},{16,0},{20,4},{24,8},{28,12},{1,17},{... | collective-permute-start | bytes 172040 | tf_op jit(solution)/shard_map/ppermute | solution.py:275
  72.1 0.2 collective-permute-start.16
  72.4 0.8 collective-permute-start.2
  73.2 0.7 collective-permute-start.3
  73.8 1.4 %collective-permute-done.15 = bf16[2,7,16,128]{3,2,1,0:T(8,128)(2,1)S(1)} collective-permute-done((bf16[2,7,16,128]{3,2,1,0:T(8,128)(2,1)S(1)}, bf16[2,7,16,128]{3,2,1,0:T(8,128)(2,1)S(1)}, u32[]{:S(2)}, u32[]{:S(2)}) %collective-permute-start.15) | collective-permute-done | bytes 57376 | tf_op jit(solution)/shard_map/ppermute | solution.py:275
  75.2 2.9 %collective-permute-done.16 = bf16[2,7,16,128]{3,2,1,0:T(8,128)(2,1)S(1)} collective-permute-done((bf16[2,7,16,128]{3,2,1,0:T(8,128)(2,1)S(1)}, bf16[2,7,16,128]{3,2,1,0:T(8,128)(2,1)S(1)}, u32[]{:S(2)}, u32[]{:S(2)}) %collective-permute-start.16) | collective-permute-done | bytes 57376 | tf_op jit(solution)/shard_map/ppermute | solution.py:275
  78.2 0.8 collective-permute-start.17
  79.0 8.7 %shard_map.78 = bf16[8,32,16,128]{3,2,1,0:T(8,128)(2,1)} custom-call(s32[2]{0:T(128)S(1)} %pad_add_fusion.where_ref, bf16[8,32,16,128]{3,2,1,0:T(8,128)(2,1)S(1)} %copy-done.3, bf16[32,16,128]{2,1,0:T(8,128)(2,1)S(1)} %collective-permute-done.2.far_a_ref, bf16[32,16,128]{2,1,0:T(8,128)(2,1)S(1)} %collective-permute-done.3.far_b_ref, ...), custom_call_target="tpu_custom_call" | custom-call | flops 3623878656 | bytes 3670024 | tf_op jit(solution)/shard_map/pallas_call | solution.py:223
  87.7 3.9 %collective-permute-start.18 = (f32[2,7,16,128]{3,2,1,0:T(8,128)S(1)}, f32[2,7,16,128]{3,2,1,0:T(8,128)S(1)}, u32[]{:S(2)}, u32[]{:S(2)}) collective-permute-start(f32[2,7,16,128]{3,2,1,0:T(8,128)S(1)} %get-tuple-element.20), channel_id=1, source_target_pairs={{0,2},{1,3},{2,0},{3,1},{4,6},{5,7},{6,4},{7,5},{8,10},{9,11},{10,... | collective-permute-start | bytes 344072 | tf_op jit(solution)/shard_map/ppermute | solution.py:286
  91.6 1.8 %collective-permute-start.19 = (f32[2,7,16,128]{3,2,1,0:T(8,128)S(1)}, f32[2,7,16,128]{3,2,1,0:T(8,128)S(1)}, u32[]{:S(2)}, u32[]{:S(2)}) collective-permute-start(f32[2,7,16,128]{3,2,1,0:T(8,128)S(1)} %get-tuple-element.20), channel_id=1, source_target_pairs={{0,3},{1,2},{2,1},{3,0},{4,7},{5,6},{6,5},{7,4},{8,11},{9,10},{10,... | collective-permute-start | bytes 344072 | tf_op jit(solution)/shard_map/ppermute | solution.py:286
  93.4 1.8 %collective-permute-done.18 = f32[2,7,16,128]{3,2,1,0:T(8,128)S(1)} collective-permute-done((f32[2,7,16,128]{3,2,1,0:T(8,128)S(1)}, f32[2,7,16,128]{3,2,1,0:T(8,128)S(1)}, u32[]{:S(2)}, u32[]{:S(2)}) %collective-permute-start.18) | collective-permute-done | bytes 114720 | tf_op jit(solution)/shard_map/ppermute | solution.py:286
  95.2 2.1 %collective-permute-done.19 = f32[2,7,16,128]{3,2,1,0:T(8,128)S(1)} collective-permute-done((f32[2,7,16,128]{3,2,1,0:T(8,128)S(1)}, f32[2,7,16,128]{3,2,1,0:T(8,128)S(1)}, u32[]{:S(2)}, u32[]{:S(2)}) %collective-permute-start.19) | collective-permute-done | bytes 114720 | tf_op jit(solution)/shard_map/ppermute | solution.py:286
  97.3 0.8 slice_bitcast_fusion
  (45 shorter events, 0.6 us)
Async XLA Ops:
  0.6 21.7 %copy-start = (bf16[1,8,32,16,128]{4,3,2,1,0:T(8,128)(2,1)S(1)}, bf16[1,8,32,16,128]{4,3,2,1,0:T(8,128)(2,1)}, u32[]{:S(2)}) copy-start(bf16[1,8,32,16,128]{4,3,2,1,0:T(8,128)(2,1)} %param.7) | copy-start | bytes 3145732
  1.7 20.6 %collective-permute-start = (bf16[32,16,128]{2,1,0:T(8,128)(2,1)S(1)}, bf16[32,16,128]{2,1,0:T(8,128)(2,1)S(1)}, u32[]{:S(2)}, u32[]{:S(2)}) collective-permute-start(bf16[32,16,128]{2,1,0:T(8,128)(2,1)S(1)} %get-tuple-element.26), channel_id=1, source_target_pairs={{0,1},{1,0},{2,3},{3,2},{4,5},{5,4},{6,7},{7,6},{8,9},{9,8},{10,11... | collective-permute-start | bytes 393224 | tf_op jit(solution)/shard_map/ppermute | solution.py:245
  4.8 17.6 %collective-permute-start.1 = (bf16[32,16,128]{2,1,0:T(8,128)(2,1)S(1)}, bf16[32,16,128]{2,1,0:T(8,128)(2,1)S(1)}, u32[]{:S(2)}, u32[]{:S(2)}) collective-permute-start(bf16[32,16,128]{2,1,0:T(8,128)(2,1)S(1)} %get-tuple-element.25), channel_id=1, source_target_pairs={{1,2},{2,1},{5,6},{6,5},{9,10},{10,9},{13,14},{14,13},{17,18},{18,... | collective-permute-start | bytes 393224 | tf_op jit(solution)/shard_map/ppermute | solution.py:245
  7.1 34.3 %collective-permute-start.4 = (bf16[32,16,128]{2,1,0:T(8,128)(2,1)}, bf16[32,16,128]{2,1,0:T(8,128)(2,1)S(1)}, u32[]{:S(2)}, u32[]{:S(2)}) collective-permute-start(bf16[32,16,128]{2,1,0:T(8,128)(2,1)} %get-tuple-element.22), channel_id=1, source_target_pairs={{0,1},{1,0},{2,3},{3,2},{4,5},{5,4},{6,7},{7,6},{8,9},{9,8},{10,11... | collective-permute-start | bytes 393224 | tf_op jit(solution)/shard_map/ppermute | solution.py:245
  11.3 30.0 %collective-permute-start.5 = (bf16[32,16,128]{2,1,0:T(8,128)(2,1)}, bf16[32,16,128]{2,1,0:T(8,128)(2,1)S(1)}, u32[]{:S(2)}, u32[]{:S(2)}) collective-permute-start(bf16[32,16,128]{2,1,0:T(8,128)(2,1)} %get-tuple-element.21), channel_id=1, source_target_pairs={{1,2},{2,1},{5,6},{6,5},{9,10},{10,9},{13,14},{14,13},{17,18},{18,... | collective-permute-start | bytes 393224 | tf_op jit(solution)/shard_map/ppermute | solution.py:245
  12.0 1.2 %copy-start.4 = (bf16[1,8,32,16,128]{4,3,2,1,0:T(8,128)(2,1)S(1)}, bf16[1,8,32,16,128]{4,3,2,1,0:T(8,128)(2,1)}, u32[]{:S(2)}) copy-start(bf16[1,8,32,16,128]{4,3,2,1,0:T(8,128)(2,1)} %param.6) | copy-start | bytes 3145732
  13.2 1.2 %copy-start.6 = (bf16[27,128,128]{2,1,0:T(8,128)(2,1)S(1)}, bf16[27,128,128]{2,1,0:T(8,128)(2,1)}, u32[]{:S(2)}) copy-start(bf16[27,128,128]{2,1,0:T(8,128)(2,1)} %w1_ref.1) | copy-start | bytes 2654212
  14.4 1.2 %copy-start.7 = (bf16[27,128,128]{2,1,0:T(8,128)(2,1)S(1)}, bf16[27,128,128]{2,1,0:T(8,128)(2,1)}, u32[]{:S(2)}) copy-start(bf16[27,128,128]{2,1,0:T(8,128)(2,1)} %w2_ref.1) | copy-start | bytes 2654212
  18.4 1.4 %copy-start.10 = (bf16[9,2,256,256]{3,2,1,0:T(8,128)(2,1)}, bf16[9,2,256,256]{3,2,1,0:T(8,128)(2,1)S(1)}, u32[]{:S(2)}) copy-start(bf16[9,2,256,256]{3,2,1,0:T(8,128)(2,1)S(1)} %get-tuple-element.14.tiles_ref) | copy-start | bytes 7077892
  19.8 1.4 %copy-start.12 = (bf16[9,2,256,256]{3,2,1,0:T(8,128)(2,1)}, bf16[9,2,256,256]{3,2,1,0:T(8,128)(2,1)S(1)}, u32[]{:S(2)}) copy-start(bf16[9,2,256,256]{3,2,1,0:T(8,128)(2,1)S(1)} %get-tuple-element.12.tiles_ref) | copy-start | bytes 7077892
  21.3 1.0 copy-start.14
  22.3 1.2 %copy-start.5 = (bf16[1,8,32,16,128]{4,3,2,1,0:T(8,128)(2,1)S(1)}, bf16[1,8,32,16,128]{4,3,2,1,0:T(8,128)(2,1)}, u32[]{:S(2)}) copy-start(bf16[1,8,32,16,128]{4,3,2,1,0:T(8,128)(2,1)} %param.6) | copy-start | bytes 3145732
  23.6 1.7 %copy-start.13 = (bf16[9,2,256,256]{3,2,1,0:T(8,128)(2,1)S(1)}, bf16[9,2,256,256]{3,2,1,0:T(8,128)(2,1)}, u32[]{:S(2)}) copy-start(bf16[9,2,256,256]{3,2,1,0:T(8,128)(2,1)} %copy-done.12) | copy-start | bytes 7077892
  25.2 1.2 %copy-start.15 = (bf16[128,4096]{1,0:T(8,128)(2,1)S(1)}, bf16[128,4096]{1,0:T(8,128)(2,1)}, u32[]{:S(2)}) copy-start(bf16[128,4096]{1,0:T(8,128)(2,1)} %copy-done.14) | copy-start | bytes 3145732
  26.5 15.7 %copy-start.1 = (bf16[1,8,32,16,128]{4,3,2,1,0:T(8,128)(2,1)S(1)}, bf16[1,8,32,16,128]{4,3,2,1,0:T(8,128)(2,1)}, u32[]{:S(2)}) copy-start(bf16[1,8,32,16,128]{4,3,2,1,0:T(8,128)(2,1)} %param.5) | copy-start | bytes 3145732
  41.3 11.1 %copy-start.2 = (bf16[8,32,16,128]{3,2,1,0:T(8,128)(2,1)}, bf16[8,32,16,128]{3,2,1,0:T(8,128)(2,1)S(1)}, u32[]{:S(2)}) copy-start(bf16[8,32,16,128]{3,2,1,0:T(8,128)(2,1)S(1)} %get-tuple-element.13.hidden_ref) | copy-start | bytes 3145732
  41.3 11.5 %collective-permute-start.10 = (bf16[28,64,128]{2,1,0:T(8,128)(2,1)S(1)}, bf16[28,64,128]{2,1,0:T(8,128)(2,1)S(1)}, u32[]{:S(2)}, u32[]{:S(2)}) collective-permute-start(bf16[28,64,128]{2,1,0:T(8,128)(2,1)S(1)} %get-tuple-element.18), channel_id=1, source_target_pairs={{0,4},{4,0},{8,12},{12,8},{16,20},{20,16},{24,28},{28,24},{1,5},{5... | collective-permute-start | bytes 1376264 | tf_op jit(solution)/shard_map/ppermute | solution.py:250
  41.4 0.8 copy-start.8
  42.2 0.9 copy-start.9
  52.4 4.9 %collective-permute-start.6 = (bf16[28,64,128]{2,1,0:T(8,128)(2,1)S(1)}, bf16[28,64,128]{2,1,0:T(8,128)(2,1)}, u32[]{:S(2)}, u32[]{:S(2)}) collective-permute-start(bf16[28,64,128]{2,1,0:T(8,128)(2,1)S(1)} %get-tuple-element.16), channel_id=1, source_target_pairs={{0,4},{4,0},{8,12},{12,8},{16,20},{20,16},{24,28},{28,24},{1,5},{5... | collective-permute-start | bytes 1376264 | tf_op jit(solution)/shard_map/ppermute | solution.py:250
  53.0 7.7 %collective-permute-start.11 = (bf16[7,64,128]{2,1,0:T(8,128)(2,1)S(1)}, bf16[7,64,128]{2,1,0:T(8,128)(2,1)S(1)}, u32[]{:S(2)}, u32[]{:S(2)}) collective-permute-start(bf16[7,64,128]{2,1,0:T(8,128)(2,1)S(1)} %get-tuple-element.27), channel_id=1, source_target_pairs={{0,1},{1,0},{2,3},{3,2},{4,5},{5,4},{6,7},{7,6},{8,9},{9,8},{10,11... | collective-permute-start | bytes 344072 | tf_op jit(solution)/shard_map/ppermute | solution.py:260
  54.3 7.8 %collective-permute-start.12 = (bf16[7,64,128]{2,1,0:T(8,128)(2,1)S(1)}, bf16[7,64,128]{2,1,0:T(8,128)(2,1)S(1)}, u32[]{:S(2)}, u32[]{:S(2)}) collective-permute-start(bf16[7,64,128]{2,1,0:T(8,128)(2,1)S(1)} %get-tuple-element.29), channel_id=1, source_target_pairs={{0,2},{1,3},{2,0},{3,1},{4,6},{5,7},{6,4},{7,5},{8,10},{9,11},{10,... | collective-permute-start | bytes 344072 | tf_op jit(solution)/shard_map/ppermute | solution.py:260
  55.8 7.8 %collective-permute-start.13 = (bf16[7,64,128]{2,1,0:T(8,128)(2,1)S(1)}, bf16[7,64,128]{2,1,0:T(8,128)(2,1)S(1)}, u32[]{:S(2)}, u32[]{:S(2)}) collective-permute-start(bf16[7,64,128]{2,1,0:T(8,128)(2,1)S(1)} %get-tuple-element.28), channel_id=1, source_target_pairs={{0,3},{1,2},{2,1},{3,0},{4,7},{5,6},{6,5},{7,4},{8,11},{9,10},{10,... | collective-permute-start | bytes 344072 | tf_op jit(solution)/shard_map/ppermute | solution.py:260
  57.2 15.1 %copy-start.3 = (bf16[8,32,16,128]{3,2,1,0:T(8,128)(2,1)S(1)}, bf16[8,32,16,128]{3,2,1,0:T(8,128)(2,1)}, u32[]{:S(2)}) copy-start(bf16[8,32,16,128]{3,2,1,0:T(8,128)(2,1)} %copy-done.2) | copy-start | bytes 3145732
  58.5 20.5 %copy-start.11 = (bf16[9,2,256,256]{3,2,1,0:T(8,128)(2,1)S(1)}, bf16[9,2,256,256]{3,2,1,0:T(8,128)(2,1)}, u32[]{:S(2)}) copy-start(bf16[9,2,256,256]{3,2,1,0:T(8,128)(2,1)} %copy-done.10) | copy-start | bytes 7077892
  58.6 6.0 %collective-permute-start.7 = (bf16[7,64,128]{2,1,0:T(8,128)(2,1)S(1)}, bf16[7,64,128]{2,1,0:T(8,128)(2,1)S(1)}, u32[]{:S(2)}, u32[]{:S(2)}) collective-permute-start(bf16[7,64,128]{2,1,0:T(8,128)(2,1)S(1)} %get-tuple-element.30), channel_id=1, source_target_pairs={{0,1},{1,0},{2,3},{3,2},{4,5},{5,4},{6,7},{7,6},{8,9},{9,8},{10,11... | collective-permute-start | bytes 344072 | tf_op jit(solution)/shard_map/ppermute | solution.py:260
  59.2 6.8 %collective-permute-start.8 = (bf16[7,64,128]{2,1,0:T(8,128)(2,1)S(1)}, bf16[7,64,128]{2,1,0:T(8,128)(2,1)S(1)}, u32[]{:S(2)}, u32[]{:S(2)}) collective-permute-start(bf16[7,64,128]{2,1,0:T(8,128)(2,1)S(1)} %get-tuple-element.32), channel_id=1, source_target_pairs={{0,2},{1,3},{2,0},{3,1},{4,6},{5,7},{6,4},{7,5},{8,10},{9,11},{10,... | collective-permute-start | bytes 344072 | tf_op jit(solution)/shard_map/ppermute | solution.py:260
  60.7 7.0 %collective-permute-start.9 = (bf16[7,64,128]{2,1,0:T(8,128)(2,1)S(1)}, bf16[7,64,128]{2,1,0:T(8,128)(2,1)S(1)}, u32[]{:S(2)}, u32[]{:S(2)}) collective-permute-start(bf16[7,64,128]{2,1,0:T(8,128)(2,1)S(1)} %get-tuple-element.31), channel_id=1, source_target_pairs={{0,3},{1,2},{2,1},{3,0},{4,7},{5,6},{6,5},{7,4},{8,11},{9,10},{10,... | collective-permute-start | bytes 344072 | tf_op jit(solution)/shard_map/ppermute | solution.py:260
  67.9 6.0 %collective-permute-start.14 = (bf16[2,7,16,128]{3,2,1,0:T(8,128)(2,1)S(1)}, bf16[2,7,16,128]{3,2,1,0:T(8,128)(2,1)S(1)}, u32[]{:S(2)}, u32[]{:S(2)}) collective-permute-start(bf16[2,7,16,128]{3,2,1,0:T(8,128)(2,1)S(1)} %get-tuple-element.35), channel_id=1, source_target_pairs={{0,8},{4,12},{8,0},{12,4},{16,24},{20,28},{24,16},{28,20},{1,9},{5... | collective-permute-start | bytes 172040 | tf_op jit(solution)/shard_map/ppermute | solution.py:275
  69.5 5.7 %collective-permute-start.15 = (bf16[2,7,16,128]{3,2,1,0:T(8,128)(2,1)S(1)}, bf16[2,7,16,128]{3,2,1,0:T(8,128)(2,1)S(1)}, u32[]{:S(2)}, u32[]{:S(2)}) collective-permute-start(bf16[2,7,16,128]{3,2,1,0:T(8,128)(2,1)S(1)} %get-tuple-element.36), channel_id=1, source_target_pairs={{0,16},{4,20},{8,24},{12,28},{16,0},{20,4},{24,8},{28,12},{1,17},{... | collective-permute-start | bytes 172040 | tf_op jit(solution)/shard_map/ppermute | solution.py:275
  72.1 6.0 %collective-permute-start.16 = (bf16[2,7,16,128]{3,2,1,0:T(8,128)(2,1)S(1)}, bf16[2,7,16,128]{3,2,1,0:T(8,128)(2,1)S(1)}, u32[]{:S(2)}, u32[]{:S(2)}) collective-permute-start(bf16[2,7,16,128]{3,2,1,0:T(8,128)(2,1)S(1)} %get-tuple-element.37), channel_id=1, source_target_pairs={{0,24},{4,28},{8,16},{12,20},{16,8},{20,12},{24,0},{28,4},{1,25},{... | collective-permute-start | bytes 172040 | tf_op jit(solution)/shard_map/ppermute | solution.py:275
  72.4 6.6 %collective-permute-start.2 = (bf16[32,16,128]{2,1,0:T(8,128)(2,1)S(1)}, bf16[32,16,128]{2,1,0:T(8,128)(2,1)S(1)}, u32[]{:S(2)}, u32[]{:S(2)}) collective-permute-start(bf16[32,16,128]{2,1,0:T(8,128)(2,1)S(1)} %get-tuple-element.24), channel_id=1, source_target_pairs={{0,1},{1,0},{2,3},{3,2},{4,5},{5,4},{6,7},{7,6},{8,9},{9,8},{10,11... | collective-permute-start | bytes 393224 | tf_op jit(solution)/shard_map/ppermute | solution.py:245
  73.2 5.8 %collective-permute-start.3 = (bf16[32,16,128]{2,1,0:T(8,128)(2,1)S(1)}, bf16[32,16,128]{2,1,0:T(8,128)(2,1)S(1)}, u32[]{:S(2)}, u32[]{:S(2)}) collective-permute-start(bf16[32,16,128]{2,1,0:T(8,128)(2,1)S(1)} %get-tuple-element.23), channel_id=1, source_target_pairs={{1,2},{2,1},{5,6},{6,5},{9,10},{10,9},{13,14},{14,13},{17,18},{18,... | collective-permute-start | bytes 393224 | tf_op jit(solution)/shard_map/ppermute | solution.py:245
  78.2 15.2 %collective-permute-start.17 = (f32[2,7,16,128]{3,2,1,0:T(8,128)S(1)}, f32[2,7,16,128]{3,2,1,0:T(8,128)S(1)}, u32[]{:S(2)}, u32[]{:S(2)}) collective-permute-start(f32[2,7,16,128]{3,2,1,0:T(8,128)S(1)} %get-tuple-element.20), channel_id=1, source_target_pairs={{0,1},{1,0},{2,3},{3,2},{4,5},{5,4},{6,7},{7,6},{8,9},{9,8},{10,11... | collective-permute-start | bytes 344072 | tf_op jit(solution)/shard_map/ppermute | solution.py:286
  87.7 7.5 %collective-permute-start.18 = (f32[2,7,16,128]{3,2,1,0:T(8,128)S(1)}, f32[2,7,16,128]{3,2,1,0:T(8,128)S(1)}, u32[]{:S(2)}, u32[]{:S(2)}) collective-permute-start(f32[2,7,16,128]{3,2,1,0:T(8,128)S(1)} %get-tuple-element.20), channel_id=1, source_target_pairs={{0,2},{1,3},{2,0},{3,1},{4,6},{5,7},{6,4},{7,5},{8,10},{9,11},{10,... | collective-permute-start | bytes 344072 | tf_op jit(solution)/shard_map/ppermute | solution.py:286
  91.6 5.7 %collective-permute-start.19 = (f32[2,7,16,128]{3,2,1,0:T(8,128)S(1)}, f32[2,7,16,128]{3,2,1,0:T(8,128)S(1)}, u32[]{:S(2)}, u32[]{:S(2)}) collective-permute-start(f32[2,7,16,128]{3,2,1,0:T(8,128)S(1)} %get-tuple-element.20), channel_id=1, source_target_pairs={{0,3},{1,2},{2,1},{3,0},{4,7},{5,6},{6,5},{7,4},{8,11},{9,10},{10,... | collective-permute-start | bytes 344072 | tf_op jit(solution)/shard_map/ppermute | solution.py:286
where the time goes:
time: 98.6 us; the launch traced here: 98.1 us
  Pallas kernels  35.6 us (36%)
  starting transfers between devices  29.2 us (30%)
  local copies, waits for them, and re-layouts  14.2 us (14%)
  waiting for transfers between devices  13.8 us (14%)
  other arithmetic  4.39 us (4%)
    pallas_call x4, Pallas kernels, call(): pl.pallas_call(body, out_shape=out_shape, in_specs=[SMEM] * n_smem + [VME...  35.6 us
    unnamed x32, local copies, waits for them, and re-layouts  13.2 us
    ppermute x6, starting transfers between devices, swap_faces(): return (lax.ppermute(to_a, 'slab', a), lax.ppermute(to_b, 'slab', b))  10 us
    ppermute x6, starting transfers between devices, scatter_slab(): lax.ppermute(piece, 'slab', [(i, partner(i, k, peers)) for i in range(pee...  7.79 us
    ppermute x3, starting transfers between devices, gather_slab(): got = lax.ppermute(part, 'slab', perm)  6.47 us
    ppermute x6, waiting for transfers between devices, scatter_slab(): lax.ppermute(piece, 'slab', [(i, partner(i, k, peers)) for i in range(pee...  5.6 us
    ppermute x3, starting transfers between devices, scatter_ranks(): out = out + lax.ppermute(piece, 'rep', perm).astype(F32)  4.45 us
    ppermute x3, waiting for transfers between devices, scatter_ranks(): out = out + lax.ppermute(piece, 'rep', perm).astype(F32)  4.25 us
  transfers between devices with their start and end apart: 20, of which 8 were waited for; matrix products, arithmetic and copies ran while one was open for 3% of the time, Pallas kernels for 36%

commit v1 on v0

v1 whole, which is shorter than its diff:
```python
import functools
import math

import jax
import jax.numpy as jnp
from jax import lax
from jax.experimental import pallas as pl
from jax.experimental.pallas import tpu as pltpu
from jax.sharding import PartitionSpec as P

F32 = jnp.float32
BF16 = jnp.bfloat16
MIB = 2**20
ANY = pl.BlockSpec(memory_space=pl.ANY)
SMEM = pl.BlockSpec(memory_space=pltpu.SMEM)


def sigmoid(value):
    return 1.0 / (1.0 + jnp.exp(-value))


def clear_rows(var):
    shape = (var.shape[0], var.shape[1]) + var.shape[3:]
    zeros = jnp.zeros(shape, var.dtype)
    var[:, :, 0] = zeros
    var[:, :, var.shape[2] - 1] = zeros


def fill_plane(var, plane, x):
    height, width, _ = x.shape
    wide = x.astype(F32)
    place = lax.broadcasted_iota(jnp.int32, x.shape, 1)
    rows = slice(1, height + 1)
    later = pltpu.roll(wide, width - 1, 1)
    var[0, plane, rows] = jnp.where(place < width - 1, later, 0.0).astype(x.dtype)
    var[1, plane, rows] = x
    earlier = pltpu.roll(wide, 1, 1)
    var[2, plane, rows] = jnp.where(place > 0, earlier, 0.0).astype(x.dtype)


def fill_weights(tiles, w_ref):
    ch = w_ref.shape[1]
    zero = jnp.zeros((ch, ch), tiles.dtype)

    def one(j, carry):
        a, c = j // 3, j % 3
        low, mid, high = (w_ref[9 * a + 3 * b + c].T for b in range(3))
        tiles[j, 0, :ch, :ch] = mid
        tiles[j, 0, :ch, ch:] = high
        tiles[j, 0, ch:, :ch] = low
        tiles[j, 0, ch:, ch:] = mid
        tiles[j, 1, :ch, :ch] = high
        tiles[j, 1, :ch, ch:] = zero
        tiles[j, 1, ch:, :ch] = zero
        tiles[j, 1, ch:, ch:] = low
        return carry

    lax.fori_loop(0, 9, one, 0)


def back_planes(var, tiles, d, count):
    half = (var.shape[2] - 2) // 2
    width, ch = var.shape[3:]
    flat = lambda u: u.reshape(-1, ch)
    acc = jnp.zeros((count * half * width, 2 * ch), F32)
    for j in range(9):
        a, c = j // 3, j % 3
        x = var[c, pl.ds(d + 2 - a, count)].reshape(count, half + 1, 2, width, ch)
        inner = jnp.concatenate([flat(x[:, :half, 1]), flat(x[:, 1:, 0])], 1)
        outer = jnp.concatenate([flat(x[:, :half, 0]), flat(x[:, 1:, 1])], 1)
        acc += jnp.dot(inner, tiles[j, 0], preferred_element_type=F32)
        acc += jnp.dot(outer, tiles[j, 1], preferred_element_type=F32)
    return acc


def paired(x):
    planes, height, width, ch = x.shape
    x = x.reshape(planes, height // 2, 2, width, ch)
    return jnp.concatenate([x[:, :, i].reshape(-1, ch) for i in range(2)], 1)


def unpaired(v, height, width):
    ch = v.shape[1] // 2
    parts = [v[:, i * ch : (i + 1) * ch].reshape(-1, height // 2, width, ch) for i in range(2)]
    return jnp.stack(parts, axis=2).reshape(-1, height, width, ch)


def step_of(count):
    return max(k for k in range(1, 5) if count % k == 0)


def transpose_plane(dst, plane, x):
    height, width, ch = x.shape
    n = height * width
    dst[:, pl.ds(pl.multiple_of(plane * n, n), n)] = x.reshape(n, ch).T


def store_tap(keep_ref, send_ref, conv, core, tap, value, ranks):
    ch = value.shape[0]
    blocks = value.reshape(ranks // 2, 2, ch // ranks, value.shape[1])
    even = blocks[:, 0].reshape(ch // 2, value.shape[1])
    odd = blocks[:, 1].reshape(ch // 2, value.shape[1])
    keep_ref[conv, tap] = jnp.where(core == 0, even, odd)
    send_ref[conv, tap] = jnp.where(core == 0, odd, even).astype(send_ref.dtype)


def rights_of(var, plane, depth, taps):
    height, ch = var.shape[2] - 2, var.shape[4]
    views = [var[t % 3, pl.ds(plane, depth), pl.ds(2 - t // 3 % 3, height)] for t in taps]
    return jnp.concatenate([x.reshape(-1, ch) for x in views], 1)


def depth_terms(left, var, taps, depth):
    n = left.shape[1] // (depth + 2)
    lefts = jnp.concatenate([left[:, a * n : (a + depth) * n] for a in range(3)], 0)
    return jnp.dot(lefts, rights_of(var, 1, depth, taps), preferred_element_type=F32)


def edge_terms(left, var, first, last, taps):
    n = (var.shape[2] - 2) * var.shape[3]
    size = left.shape[1]
    low = jnp.dot(left[:, n : 2 * n], rights_of(var, first, 1, taps), preferred_element_type=F32)
    high = jnp.dot(
        left[:, size - 2 * n : size - n], rights_of(var, last, 1, taps), preferred_element_type=F32
    )
    return low, high


def grouped(body):
    @functools.partial(loop, 0, 2)
    def _(i):
        body([4 * i + k for k in range(4)])

    return lambda: body([8])


def hidden_plane(back, pre):
    v = paired(pre).astype(F32)
    s = sigmoid(v)
    return (back * (s * (1.0 + v * (1.0 - s)))).astype(BF16)


def loop(start, stop, body):
    def step(i, carry):
        body(i)
        return carry

    lax.fori_loop(start, stop, step, 0)


def clear_ends(left, depth):
    n = left.shape[1] // (depth + 2)
    zero = jnp.zeros((left.shape[0], n), left.dtype)
    left[:, :n] = zero
    left[:, (depth + 1) * n :] = zero


def inner_kernel(
    taps, cot_hbm, pre_hbm, w_hbm, hid_hbm, part_hbm, tiles_hbm,
    cot, pre, w, var, act_t, tiles, hid, part, sems,
):
    depth, height, width, ch = cot.shape
    copies = [
        pltpu.make_async_copy(a, b, sems.at[i])
        for i, (a, b) in enumerate(((w_hbm, w), (cot_hbm, cot), (pre_hbm, pre)))
    ]
    for c in copies:
        c.start()
    clear_rows(var)
    edge = jnp.zeros((3,) + var.shape[2:], BF16)
    var[:, 0] = edge
    var[:, depth + 1] = edge
    clear_ends(act_t, depth)
    copies[0].wait()
    fill_weights(tiles, w)
    tiles_out = pltpu.make_async_copy(tiles, tiles_hbm, sems.at[3])
    tiles_out.start()
    copies[1].wait()
    copies[2].wait()

    @functools.partial(loop, 0, depth)
    def _(d):
        fill_plane(var, d + 1, cot[d])
        transpose_plane(act_t, d + 1, silu_of(pre[d]))

    def terms(group):
        r = depth_terms(act_t, var, group, depth)
        for k, t in enumerate(group):
            for a in range(3):
                part[9 * a + t] = r[a * ch : (a + 1) * ch, k * ch : (k + 1) * ch]

    grouped(terms)()
    part_out = pltpu.make_async_copy(part, part_hbm, sems.at[5])
    part_out.start()
    step = step_of(depth - 2)

    @functools.partial(loop, 0, (depth - 2) // step)
    def _(i):
        d = 1 + i * step
        grad = hidden_plane(back_planes(var, tiles, d, step), pre[pl.ds(d, step)])
        hid[pl.ds(d - 1, step)] = unpaired(grad, height, width)

    hid_out = pltpu.make_async_copy(hid, hid_hbm, sems.at[4])
    hid_out.start()
    tiles_out.wait()
    part_out.wait()
    hid_out.wait()


def outer_kernel(
    ranks, taps, where_ref, far_a_hbm, far_b_hbm, cot_hbm, pre_hbm, in_hbm, hid_hbm, part_hbm,
    tiles_hbm, ext_hbm, keep_hbm, send_hbm,
    far_a, far_b, cot, pre, vol, ext, part, tiles, cvar, hvar, act_t, in_t, keep, send, sems,
):
    depth, height, width, ch = vol.shape
    n = height * width
    even, core = where_ref[0] == 0, where_ref[1]
    pairs = (
        (far_a_hbm, far_a), (far_b_hbm, far_b),
        (cot_hbm.at[pl.ds(0, 2)], cot.at[pl.ds(0, 2)]),
        (cot_hbm.at[pl.ds(depth - 2, 2)], cot.at[pl.ds(2, 2)]),
        (pre_hbm.at[0], pre.at[1]), (pre_hbm.at[depth - 1], pre.at[2]),
        (tiles_hbm, tiles), (in_hbm, vol),
        (hid_hbm, ext.at[pl.ds(2, depth - 2)]), (part_hbm, part),
    )
    copies = [pltpu.make_async_copy(a, b, sems.at[i]) for i, (a, b) in enumerate(pairs)]
    for c in copies:
        c.start()
    clear_rows(cvar)
    clear_rows(hvar)
    clear_ends(in_t, depth)
    for c in copies[:6]:
        c.wait()
    for i in range(2):
        fill_plane(cvar, i, jnp.where(even, far_b[i], far_a[i]))
        fill_plane(cvar, 2 + i, cot[i])
        fill_plane(cvar, 4 + i, cot[2 + i])
        fill_plane(cvar, 6 + i, jnp.where(even, far_a[i], far_b[i]))
        transpose_plane(act_t, 1 + i, silu_of(pre[1 + i]))
    pre[0] = jnp.where(even, far_b[2], far_a[2])
    pre[3] = jnp.where(even, far_a[2], far_b[2])
    copies[6].wait()
    copies[8].wait()

    for late in range(2):
        back = back_planes(cvar, tiles, 4 * late, 2)
        grad = hidden_plane(back, pre[2 * late : 2 * late + 2])
        planes = unpaired(grad, height, width)
        there = where_ref[2 + late] == 1
        outside = jnp.where(there, planes[late].astype(F32), 0.0).astype(BF16)
        ext[depth * late + late] = outside
        ext[(depth - 1) * late + 1] = planes[1 - late]

    ext_out = pltpu.make_async_copy(ext, ext_hbm, sems.at[10])
    ext_out.start()
    copies[7].wait()

    @functools.partial(loop, 0, depth)
    def _(d):
        fill_plane(hvar, d, ext[d])
        transpose_plane(in_t, d + 1, vol[d])

    fill_plane(hvar, depth, ext[depth])
    fill_plane(hvar, depth + 1, ext[depth + 1])
    copies[9].wait()

    def seconds(group):
        low, high = edge_terms(act_t, cvar, 1, 6, group)
        for k, t in enumerate(group):
            cols = slice(k * ch, (k + 1) * ch)
            store_tap(keep, send, 1, core, t, part[t] + high[:, cols], ranks)
            store_tap(keep, send, 1, core, 9 + t, part[9 + t], ranks)
            store_tap(keep, send, 1, core, 18 + t, part[18 + t] + low[:, cols], ranks)

    grouped(seconds)()
    for t in range(taps, keep.shape[1]):
        for conv in range(2):
            keep[conv, t] = jnp.zeros(keep.shape[2:], keep.dtype)
            send[conv, t] = jnp.zeros(send.shape[2:], send.dtype)
    outs = [
        pltpu.make_async_copy(a.at[1], b.at[1], sems.at[11 + i])
        for i, (a, b) in enumerate(((send, send_hbm), (keep, keep_hbm)))
    ]
    for c in outs:
        c.start()

    def firsts(group):
        r = depth_terms(in_t, hvar, group, depth)
        low, high = edge_terms(in_t, hvar, 0, depth + 1, group)
        for k, t in enumerate(group):
            cols = slice(k * ch, (k + 1) * ch)
            store_tap(keep, send, 0, core, t, r[:ch, cols] + high[:, cols], ranks)
            store_tap(keep, send, 0, core, 9 + t, r[ch : 2 * ch, cols], ranks)
            store_tap(keep, send, 0, core, 18 + t, r[2 * ch :, cols] + low[:, cols], ranks)

    finish = grouped(firsts)

    def leave(first, count, sem):
        moved = [
            pltpu.make_async_copy(
                x.at[0, pl.ds(first, count)], y.at[0, pl.ds(first, count)], sems.at[sem + i]
            )
            for i, (x, y) in enumerate(((send, send_hbm), (keep, keep_hbm)))
        ]
        for c in moved:
            c.start()
        return moved

    for a in range(3):
        outs += leave(9 * a, 8, 13 + 2 * a)
    finish()
    for a in range(3):
        outs += leave(9 * a + 8, 1 if a < 2 else keep.shape[1] - 26, 19 + 2 * a)
    ext_out.wait()
    for c in outs:
        c.wait()


def silu_of(x):
    v = x.astype(F32)
    return (v * sigmoid(v)).astype(BF16)


def input_kernel(ext_hbm, w_hbm, out_hbm, ext, w, tiles, out, var, sems):
    depth, height, width, _ = out.shape
    copies = [
        pltpu.make_async_copy(a, b, sems.at[i])
        for i, (a, b) in enumerate(((w_hbm, w), (ext_hbm, ext)))
    ]
    for c in copies:
        c.start()
    clear_rows(var)
    copies[0].wait()
    fill_weights(tiles, w)
    copies[1].wait()

    @functools.partial(loop, 0, depth + 2)
    def _(d):
        fill_plane(var, d, ext[d])

    step = step_of(depth)

    @functools.partial(loop, 0, depth // step)
    def _(i):
        grad = back_planes(var, tiles, i * step, step).astype(BF16)
        out[pl.ds(i * step, step)] = unpaired(grad, height, width)

    c = pltpu.make_async_copy(out, out_hbm, sems.at[2])
    c.start()
    c.wait()


def call(body, out_shape, operands, scratch, sems, flops, n_smem=0):
    moved = sum(x.size * x.dtype.itemsize for x in operands)
    return pl.pallas_call(
        body,
        out_shape=out_shape,
        in_specs=[SMEM] * n_smem + [ANY] * (len(operands) - n_smem),
        out_specs=jax.tree.map(lambda _: ANY, out_shape),
        scratch_shapes=[pltpu.VMEM(*x) for x in scratch] + [pltpu.SemaphoreType.DMA((sems,))],
        compiler_params=pltpu.CompilerParams(vmem_limit_bytes=60 * MIB),
        cost_estimate=pl.CostEstimate(flops=flops, bytes_accessed=moved, transcendentals=0),
    )(*operands)


def partner(i, k, n):
    return i ^ k if n & (n - 1) == 0 else (i + k) % n


def swap_faces(cot, pre, even):
    peers, depth = lax.axis_size("slab"), cot.shape[0]
    a = [(i, i ^ 1) for i in range(peers) if i ^ 1 < peers]
    b = [(i, j) for i in range(peers) for j in [((i + 1) ^ 1) - 1] if 0 <= j < peers]

    def face(last):
        cut = lambda x, count: lax.dynamic_slice_in_dim(
            x, jnp.where(last, depth - count, 0), count, 0
        )
        return jnp.concatenate([cut(cot, 2), cut(pre, 1)])

    return lax.ppermute(face(even), "slab", a), lax.ppermute(face(~even), "slab", b)


def swap_cores(send):
    ranks = lax.axis_size("rep")
    return lax.ppermute(send, "rep", [(i, i ^ 1) for i in range(ranks)])


def slab_pieces(keep, got):
    peers, me = lax.axis_size("slab"), lax.axis_index("slab")
    count = keep.shape[1] // peers

    def piece(i):
        cut = lambda x: lax.dynamic_slice_in_dim(x, i * count, count, 1)
        return cut(keep) + cut(got).astype(F32)

    others = [piece(partner(me, k, peers)).astype(BF16) for k in range(1, peers)]
    return piece(me), others


def trade_slab(others):
    peers = lax.axis_size("slab")
    return [
        lax.ppermute(x, "slab", [(i, partner(i, k + 1, peers)) for i in range(peers)])
        for k, x in enumerate(others)
    ]


def scatter_ranks(total):
    ranks, me = lax.axis_size("rep"), lax.axis_index("rep")
    peers = ranks // 2
    count = total.shape[2] // peers
    out = lax.dynamic_slice_in_dim(total, me // 2 * count, count, 2)
    for k in range(1, peers):
        other = partner(me // 2, k, peers)
        piece = lax.dynamic_slice_in_dim(total, other * count, count, 2).astype(BF16)
        perm = [(i, 2 * partner(i // 2, k, peers) + i % 2) for i in range(ranks)]
        out = out + lax.ppermute(piece, "rep", perm).astype(F32)
    return out


def gather_slab(part):
    peers, me = lax.axis_size("slab"), lax.axis_index("slab")
    count = part.shape[1]
    shape = (part.shape[0], count * peers) + part.shape[2:]
    out = lax.dynamic_update_slice_in_dim(jnp.zeros(shape, part.dtype), part, me * count, 1)
    for k in range(1, peers):
        perm = [(i, partner(i, k, peers)) for i in range(peers)]
        got = lax.ppermute(part, "slab", perm)
        source = partner(me, k, peers) if peers & (peers - 1) == 0 else (me - k) % peers
        out = lax.dynamic_update_slice_in_dim(out, got, source * count, 1)
    return out


def shards(inputs, pre_act, cotangent, weight_one, weight_two):
    volume_in, pre, cot = inputs[0], pre_act[0], cotangent[0]
    depth, height, width, ch = cot.shape
    taps = weight_one.shape[0]
    ranks, slabs = lax.axis_size("rep"), lax.axis_size("slab")
    padded_taps = -(-taps // slabs) * slabs
    n = height * width
    me = lax.axis_index("slab")
    even = me % 2 == 0
    where = jnp.stack([me % 2, lax.axis_index("rep") % 2, me > 0, me < slabs - 1]).astype(jnp.int32)
    s = jax.ShapeDtypeStruct
    sweep = 2 * taps * depth * n * ch * ch
    plane = (height, width, ch)
    many = lambda k: ((k,) + plane, BF16)
    shifted = lambda k: ((3, k, height + 2, width, ch), BF16)
    tiles_of = ((9, 2, 2 * ch, 2 * ch), BF16)
    weights_of = (weight_one.shape, BF16)
    part_of = ((taps, ch, ch), F32)
    keep_of = ((2, padded_taps, ch // 2, ch), F32)
    send_of = (keep_of[0], BF16)

    far_a, far_b = swap_faces(cot, pre, even)
    hid, part, tiles2 = call(
        functools.partial(inner_kernel, taps),
        (s(*many(depth - 2)), s(*part_of), s(*tiles_of)),
        (cot, pre, weight_two),
        [many(depth), many(depth), weights_of, shifted(depth + 2), ((ch, (depth + 2) * n), BF16),
         tiles_of, many(depth - 2), part_of],
        6, 2 * sweep,
    )
    ext, keep, send = call(
        functools.partial(outer_kernel, ranks, taps),
        (s(*many(depth + 2)), s(*keep_of), s(*send_of)),
        (where, far_a, far_b, cot, pre, volume_in, hid, part, tiles2),
        [many(3), many(3), many(4), many(4), many(depth), many(depth + 2), part_of, tiles_of,
         shifted(8), shifted(depth + 2), ((ch, 4 * n), BF16), ((ch, (depth + 2) * n), BF16),
         keep_of, send_of],
        25, 3 * sweep // 2, 1,
    )
    got = swap_cores(send)
    mine, others = slab_pieces(keep, got)
    ext, weight_one, mine, *others = lax.optimization_barrier((ext, weight_one, mine, *others))
    arrived = trade_slab(others)
    input_grad = call(
        input_kernel, s(*many(depth)), (ext, weight_one),
        [many(depth + 2), weights_of, tiles_of, many(depth), shifted(depth + 2)], 3, sweep,
    )
    input_grad, *arrived = lax.optimization_barrier((input_grad, *arrived))
    for x in arrived:
        mine = mine + x.astype(F32)
    factor = 1.0 / math.sqrt(ranks * slabs * depth * n)
    mine = scatter_ranks(mine) * factor
    grads = gather_slab(mine)[:, :taps]
    return (input_grad[None], grads[0], grads[1])


def solution(mesh):
    volumes = P("rep", "slab", None, None, None)
    kernels = P(None, "rep", None)
    return jax.shard_map(
        shards,
        mesh=mesh,
        in_specs=(volumes, volumes, volumes, P(), P()),
        out_specs=(volumes, kernels, kernels),
        check_vma=False,
    )
```

time: 98.6 us -> 77.8 us (0.79)
  starting transfers between devices: 29.2 us -> 18.1 us
  local copies, waits for them, and re-layouts: 14.2 us -> 3.76 us
  other arithmetic: 4.39 us -> 2.61 us
  waiting for transfers between devices: 13.8 us -> 15.4 us
  Pallas kernels: 35.6 us -> 36.9 us
    unnamed x32 -> x4, local copies, waits for them, and re-layouts: 13.2 us -> 0.8 us
    ppermute x12 -> x5, starting transfers between devices: 17.8 us -> 9.98 us  [the longest x1 5.75 us: swap_faces(): lax.ppermute(face(even), 'slab', a)]
    ppermute x3, starting transfers between devices: 6.47 us -> 3.55 us  [gather_slab(): got = lax.ppermute(part, 'slab', perm)]
    select_n x3 -> x0, other arithmetic: 2.79 us -> none  [swap_faces(): to_b = jnp.where(even, first, last)]
    ppermute x12 -> x5, waiting for transfers between devices: 5.61 us -> 2.9 us  [the longest x1 2.72 us: swap_faces(): lax.ppermute(face(even), 'slab', a)]
    ppermute x2 -> x1, waiting for transfers between devices: 0.01 us -> 2.61 us  [swap_cores(): return lax.ppermute(send, 'rep', [(i, i ^ 1) for i in range(ranks)])]
    dynamic_slice x0 -> x2, local copies, waits for them, and re-layouts: none -> 2.07 us  [face(): lax.dynamic_slice_in_dim(x, jnp.where(last, depth - count, 0), count, 0)]
    convert_element_type x1, other arithmetic: 0.04 us -> 1.72 us  [slab_pieces(): piece(partner(me, k, peers)).astype(BF16)]
  transfers between devices with their start and end apart: 20 -> 12, of which waited for: 8 -> 9; matrix products, arithmetic and copies ran while one was open for 3% -> 1% of each run, Pallas kernels for 36% -> 29%
where the time goes in v1:
time: 77.8 us; the launch traced here: 77.6 us
  Pallas kernels  36.9 us (47%)
  starting transfers between devices  18.1 us (23%)
  waiting for transfers between devices  15.4 us (20%)
  local copies, waits for them, and re-layouts  3.76 us (5%)
  other arithmetic  2.61 us (3%)
  between operations  0.87 us (1%)
    pallas_call x3, Pallas kernels, call(): pl.pallas_call(body, out_shape=out_shape, in_specs=[SMEM] * n_smem + [ANY...  36.9 us
    ppermute x3, waiting for transfers between devices, scatter_ranks(): out = out + lax.ppermute(piece, 'rep', perm).astype(F32)  5.76 us
    ppermute x1, starting transfers between devices, swap_faces(): lax.ppermute(face(even), 'slab', a)  5.75 us
    ppermute x3, starting transfers between devices, scatter_ranks(): out = out + lax.ppermute(piece, 'rep', perm).astype(F32)  4.45 us
    ppermute x3, waiting for transfers between devices, gather_slab(): got = lax.ppermute(part, 'slab', perm)  4.17 us
    ppermute x3, starting transfers between devices, gather_slab(): got = lax.ppermute(part, 'slab', perm)  3.55 us
    ppermute x3, starting transfers between devices, trade_slab(): lax.ppermute(x, 'slab', [(i, partner(i, k + 1, peers)) for i in range(pee...  3.55 us
    ppermute x1, waiting for transfers between devices, swap_faces(): lax.ppermute(face(even), 'slab', a)  2.72 us
  transfers between devices with their start and end apart: 12, of which 9 were waited for; matrix products, arithmetic and copies ran while one was open for 1% of the time, Pallas kernels for 29%

profile of v1, /device:TPU:0, one launch (start us, length us, event | category | flops | bytes accessed | tf_op | source)
XLA Modules:
  0.0 77.6 jit_solution(11867008201282824462)
XLA Ops:
  0.7 1.1 %dynamic-slice_bitcast_fusion = (bf16[2,32,16,128]{3,2,1,0:T(8,128)(2,1)S(1)}, bf16[2,32,16,128]{3,2,1,0:T(8,128)(2,1)S(1)}) fusion(bf16[1,8,32,16,128]{4,3,2,1,0:T(8,128)(2,1)} %param.7, s32[]{:T(128)S(6)} %select_n.73, s32[]{:T(128)S(6)} %select_n.71), kind=kLoop, calls=%fused_computation.7 | loop fusion | bytes 1048584 | tf_op jit(solution)/shard_map/dynamic_slice | solution.py:376
  1.7 1.0 %dynamic-slice_bitcast_fusion.2 = (bf16[1,32,16,128]{3,2,1,0:T(8,128)(2,1)S(1)}, bf16[1,32,16,128]{3,2,1,0:T(8,128)(2,1)S(1)}) fusion(bf16[1,8,32,16,128]{4,3,2,1,0:T(8,128)(2,1)} %param.6, s32[]{:T(128)S(6)} %select_n.74, s32[]{:T(128)S(6)} %select_n.72), kind=kLoop, calls=%fused_computation.11 | loop fusion | bytes 524296 | tf_op jit(solution)/shard_map/dynamic_slice | solution.py:376
  2.8 0.7 collective-permute-start.1
  3.5 5.7 %collective-permute-start = (bf16[3,32,16,128]{3,2,1,0:T(8,128)(2,1)S(1)}, bf16[3,32,16,128]{3,2,1,0:T(8,128)(2,1)S(1)}, u32[]{:S(2)}, u32[]{:S(2)}) collective-permute-start(bf16[3,32,16,128]{3,2,1,0:T(8,128)(2,1)S(1)} %pad_maximum_fusion), channel_id=1, source_target_pairs={{0,1},{1,0},{2,3},{3,2},{4,5},{5,4},{6,7},{7,6},{8,9},{9,8},{10,11... | collective-permute-start | bytes 1179656 | tf_op jit(solution)/shard_map/ppermute | solution.py:381
  9.3 13.7 %shard_map.76 = (bf16[6,32,16,128]{3,2,1,0:T(8,128)(2,1)}, f32[27,128,128]{2,1,0:T(8,128)}, bf16[9,2,256,256]{3,2,1,0:T(8,128)(2,1)}) custom-call(bf16[8,32,16,128]{3,2,1,0:T(8,128)(2,1)} %bitcast.20, bf16[8,32,16,128]{3,2,1,0:T(8,128)(2,1)} %bitcast.22, bf16[27,128,128]{2,1,0:T(8,128)(2,1)} %w_hbm.1), custom_call_target="tpu_custom_call" | custom-call | flops 7247757312 | bytes 2981888 | tf_op jit(solution)/shard_map/pallas_call | solution.py:355
  23.0 0.7 pad_add_fusion.where_ref
  23.7 0.0 collective-permute-done.1.far_b_hbm
  23.7 0.0 copy-start
  23.7 2.7 %collective-permute-done.far_a_hbm = bf16[3,32,16,128]{3,2,1,0:T(8,128)(2,1)S(1)} collective-permute-done((bf16[3,32,16,128]{3,2,1,0:T(8,128)(2,1)S(1)}, bf16[3,32,16,128]{3,2,1,0:T(8,128)(2,1)S(1)}, u32[]{:S(2)}, u32[]{:S(2)}) %collective-permute-start) | collective-permute-done | bytes 393248 | tf_op jit(solution)/shard_map/ppermute | solution.py:381
  26.4 0.0 copy-start.1
  26.4 0.0 copy-done
  26.4 0.8 %copy-done.1 = bf16[3,32,16,128]{3,2,1,0:T(8,128)(2,1)} copy-done((bf16[3,32,16,128]{3,2,1,0:T(8,128)(2,1)}, bf16[3,32,16,128]{3,2,1,0:T(8,128)(2,1)S(1)}, u32[]{:S(2)}) %copy-start.1) | copy-done | bytes 393240
  27.2 14.2 %shard_map.77 = (bf16[10,32,16,128]{3,2,1,0:T(8,128)(2,1)}, f32[2,28,64,128]{3,2,1,0:T(8,128)}, bf16[2,28,64,128]{3,2,1,0:T(8,128)(2,1)}) custom-call(s32[4]{0:T(128)} %pad_add_fusion.where_ref, bf16[3,32,16,128]{3,2,1,0:T(8,128)(2,1)} %copy-done.1, bf16[3,32,16,128]{3,2,1,0:T(8,128)(2,1)} %copy-done, bf16[8,32,16,128]{3,2,1,0:T(8,128)(2,1)} %bitcast.21, ...), custom_call_target="tpu_custom_call" | custom-call | flops 5435817984 | bytes 8847376 | tf_op jit(solution)/shard_map/pallas_call | solution.py:355
  41.4 0.1 collective-permute-start.2
  41.5 2.6 %collective-permute-done.2 = bf16[2,28,64,128]{3,2,1,0:T(8,128)(2,1)S(1)} collective-permute-done((bf16[2,28,64,128]{3,2,1,0:T(8,128)(2,1)}, bf16[2,28,64,128]{3,2,1,0:T(8,128)(2,1)S(1)}, u32[]{:S(2)}, u32[]{:S(2)}) %collective-permute-start.2) | collective-permute-done | bytes 917536 | tf_op jit(solution)/shard_map/ppermute | solution.py:386
  44.1 1.7 %add_convert_fusion = (bf16[2,7,64,128]{3,2,1,0:T(8,128)(2,1)S(1)}, bf16[2,7,64,128]{3,2,1,0:T(8,128)(2,1)S(1)}, bf16[2,7,64,128]{3,2,1,0:T(8,128)(2,1)S(1)}, f32[2,7,64,128]{3,2,1,0:T(8,128)S(1)}) fusion(f32[2,28,64,128]{3,2,1,0:T(8,128)} %get-tuple-element.23, s32[]{:T(128)S(6)} %select_n.78, bf16[2,28,64,128]{3,2,1,0:T(8,128)(2,1)S(1)} %collective-permute-done.2, ...), kind=kLoop, calls=%fused_computation.1 | loop fusion | flops 1261568 | bytes 3899408 | tf_op jit(solution)/shard_map/convert_element_type | solution.py:397
  45.9 0.1 collective-permute-start.3
  46.0 2.0 %collective-permute-start.4 = (bf16[2,7,64,128]{3,2,1,0:T(8,128)(2,1)S(1)}, bf16[2,7,64,128]{3,2,1,0:T(8,128)(2,1)S(1)}, u32[]{:S(2)}, u32[]{:S(2)}) collective-permute-start(bf16[2,7,64,128]{3,2,1,0:T(8,128)(2,1)S(1)} %get-tuple-element.28), channel_id=1, source_target_pairs={{0,2},{1,3},{2,0},{3,1},{4,6},{5,7},{6,4},{7,5},{8,10},{9,11},{10,... | collective-permute-start | bytes 688136 | tf_op jit(solution)/shard_map/ppermute | solution.py:404
  47.9 1.5 %collective-permute-start.5 = (bf16[2,7,64,128]{3,2,1,0:T(8,128)(2,1)S(1)}, bf16[2,7,64,128]{3,2,1,0:T(8,128)(2,1)S(1)}, u32[]{:S(2)}, u32[]{:S(2)}) collective-permute-start(bf16[2,7,64,128]{3,2,1,0:T(8,128)(2,1)S(1)} %get-tuple-element.29), channel_id=1, source_target_pairs={{0,3},{1,2},{2,1},{3,0},{4,7},{5,6},{6,5},{7,4},{8,11},{9,10},{10,... | collective-permute-start | bytes 688136 | tf_op jit(solution)/shard_map/ppermute | solution.py:404
  49.4 9.0 %shard_map.78 = bf16[8,32,16,128]{3,2,1,0:T(8,128)(2,1)} custom-call(bf16[10,32,16,128]{3,2,1,0:T(8,128)(2,1)} %get-tuple-element.25.ext_hbm, bf16[27,128,128]{2,1,0:T(8,128)(2,1)} %w_hbm.2), custom_call_target="tpu_custom_call" | custom-call | flops 3623878656 | bytes 2195456 | tf_op jit(solution)/shard_map/pallas_call | solution.py:355
  58.4 0.0 collective-permute-done.3
  58.4 0.2 collective-permute-done.4
  58.6 0.0 collective-permute-done.5
  58.6 0.1 convert_add_fusion
  58.7 1.6 %collective-permute-start.6 = (bf16[2,7,16,128]{3,2,1,0:T(8,128)(2,1)S(1)}, bf16[2,7,16,128]{3,2,1,0:T(8,128)(2,1)S(1)}, u32[]{:S(2)}, u32[]{:S(2)}) collective-permute-start(bf16[2,7,16,128]{3,2,1,0:T(8,128)(2,1)S(1)} %get-tuple-element.47), channel_id=1, source_target_pairs={{0,8},{4,12},{8,0},{12,4},{16,24},{20,28},{24,16},{28,20},{1,9},{5... | collective-permute-start | bytes 172040 | tf_op jit(solution)/shard_map/ppermute | solution.py:418
  60.4 2.6 %collective-permute-start.7 = (bf16[2,7,16,128]{3,2,1,0:T(8,128)(2,1)S(1)}, bf16[2,7,16,128]{3,2,1,0:T(8,128)(2,1)S(1)}, u32[]{:S(2)}, u32[]{:S(2)}) collective-permute-start(bf16[2,7,16,128]{3,2,1,0:T(8,128)(2,1)S(1)} %get-tuple-element.49), channel_id=1, source_target_pairs={{0,16},{4,20},{8,24},{12,28},{16,0},{20,4},{24,8},{28,12},{1,17},{... | collective-permute-start | bytes 172040 | tf_op jit(solution)/shard_map/ppermute | solution.py:418
  63.0 0.2 collective-permute-start.8
  63.2 0.3 collective-permute-done.6
  63.5 3.2 %collective-permute-done.7 = bf16[2,7,16,128]{3,2,1,0:T(8,128)(2,1)S(1)} collective-permute-done((bf16[2,7,16,128]{3,2,1,0:T(8,128)(2,1)S(1)}, bf16[2,7,16,128]{3,2,1,0:T(8,128)(2,1)S(1)}, u32[]{:S(2)}, u32[]{:S(2)}) %collective-permute-start.7) | collective-permute-done | bytes 57376 | tf_op jit(solution)/shard_map/ppermute | solution.py:418
  66.7 2.3 %collective-permute-done.8 = bf16[2,7,16,128]{3,2,1,0:T(8,128)(2,1)S(1)} collective-permute-done((bf16[2,7,16,128]{3,2,1,0:T(8,128)(2,1)S(1)}, bf16[2,7,16,128]{3,2,1,0:T(8,128)(2,1)S(1)}, u32[]{:S(2)}, u32[]{:S(2)}) %collective-permute-start.8) | collective-permute-done | bytes 57376 | tf_op jit(solution)/shard_map/ppermute | solution.py:418
  69.0 1.7 %collective-permute-start.9 = (f32[2,7,16,128]{3,2,1,0:T(8,128)S(1)}, f32[2,7,16,128]{3,2,1,0:T(8,128)S(1)}, u32[]{:S(2)}, u32[]{:S(2)}) collective-permute-start(f32[2,7,16,128]{3,2,1,0:T(8,128)S(1)} %get-tuple-element.36), channel_id=1, source_target_pairs={{0,1},{1,0},{2,3},{3,2},{4,5},{5,4},{6,7},{7,6},{8,9},{9,8},{10,11... | collective-permute-start | bytes 344072 | tf_op jit(solution)/shard_map/ppermute | solution.py:429
  70.8 0.3 collective-permute-start.10
  71.1 1.5 %collective-permute-start.11 = (f32[2,7,16,128]{3,2,1,0:T(8,128)S(1)}, f32[2,7,16,128]{3,2,1,0:T(8,128)S(1)}, u32[]{:S(2)}, u32[]{:S(2)}) collective-permute-start(f32[2,7,16,128]{3,2,1,0:T(8,128)S(1)} %get-tuple-element.36), channel_id=1, source_target_pairs={{0,3},{1,2},{2,1},{3,0},{4,7},{5,6},{6,5},{7,4},{8,11},{9,10},{10,... | collective-permute-start | bytes 344072 | tf_op jit(solution)/shard_map/ppermute | solution.py:429
  72.6 1.4 %collective-permute-done.9 = f32[2,7,16,128]{3,2,1,0:T(8,128)S(1)} collective-permute-done((f32[2,7,16,128]{3,2,1,0:T(8,128)S(1)}, f32[2,7,16,128]{3,2,1,0:T(8,128)S(1)}, u32[]{:S(2)}, u32[]{:S(2)}) %collective-permute-start.9) | collective-permute-done | bytes 114720 | tf_op jit(solution)/shard_map/ppermute | solution.py:429
  74.0 1.5 %collective-permute-done.10 = f32[2,7,16,128]{3,2,1,0:T(8,128)S(1)} collective-permute-done((f32[2,7,16,128]{3,2,1,0:T(8,128)S(1)}, f32[2,7,16,128]{3,2,1,0:T(8,128)S(1)}, u32[]{:S(2)}, u32[]{:S(2)}) %collective-permute-start.10) | collective-permute-done | bytes 114720 | tf_op jit(solution)/shard_map/ppermute | solution.py:429
  75.6 1.2 %collective-permute-done.11 = f32[2,7,16,128]{3,2,1,0:T(8,128)S(1)} collective-permute-done((f32[2,7,16,128]{3,2,1,0:T(8,128)S(1)}, f32[2,7,16,128]{3,2,1,0:T(8,128)S(1)}, u32[]{:S(2)}, u32[]{:S(2)}) %collective-permute-start.11) | collective-permute-done | bytes 114720 | tf_op jit(solution)/shard_map/ppermute | solution.py:429
  76.8 0.8 %slice_bitcast_fusion = (f32[27,16,128]{2,1,0:T(8,128)}, f32[27,16,128]{2,1,0:T(8,128)}) fusion(f32[2,28,16,128]{3,2,1,0:T(8,128)S(1)} %constant_dynamic-update-slice_fusion), kind=kLoop, calls=%fused_computation.9 | loop fusion | bytes 884736 | tf_op jit(solution)/shard_map/squeeze | solution.py:488
  (8 shorter events, 0.2 us)
Async XLA Ops:
  2.8 20.9 %collective-permute-start.1 = (bf16[3,32,16,128]{3,2,1,0:T(8,128)(2,1)S(1)}, bf16[3,32,16,128]{3,2,1,0:T(8,128)(2,1)S(1)}, u32[]{:S(2)}, u32[]{:S(2)}) collective-permute-start(bf16[3,32,16,128]{3,2,1,0:T(8,128)(2,1)S(1)} %pad_maximum_fusion.1), channel_id=1, source_target_pairs={{1,2},{2,1},{5,6},{6,5},{9,10},{10,9},{13,14},{14,13},{17,18},{18,... | collective-permute-start | bytes 1179656 | tf_op jit(solution)/shard_map/ppermute | solution.py:381
  3.5 22.9 %collective-permute-start = (bf16[3,32,16,128]{3,2,1,0:T(8,128)(2,1)S(1)}, bf16[3,32,16,128]{3,2,1,0:T(8,128)(2,1)S(1)}, u32[]{:S(2)}, u32[]{:S(2)}) collective-permute-start(bf16[3,32,16,128]{3,2,1,0:T(8,128)(2,1)S(1)} %pad_maximum_fusion), channel_id=1, source_target_pairs={{0,1},{1,0},{2,3},{3,2},{4,5},{5,4},{6,7},{7,6},{8,9},{9,8},{10,11... | collective-permute-start | bytes 1179656 | tf_op jit(solution)/shard_map/ppermute | solution.py:381
  23.7 2.7 %copy-start = (bf16[3,32,16,128]{3,2,1,0:T(8,128)(2,1)}, bf16[3,32,16,128]{3,2,1,0:T(8,128)(2,1)S(1)}, u32[]{:S(2)}) copy-start(bf16[3,32,16,128]{3,2,1,0:T(8,128)(2,1)S(1)} %collective-permute-done.1.far_b_hbm) | copy-start | bytes 1179652
  26.4 0.8 %copy-start.1 = (bf16[3,32,16,128]{3,2,1,0:T(8,128)(2,1)}, bf16[3,32,16,128]{3,2,1,0:T(8,128)(2,1)S(1)}, u32[]{:S(2)}) copy-start(bf16[3,32,16,128]{3,2,1,0:T(8,128)(2,1)S(1)} %collective-permute-done.far_a_hbm) | copy-start | bytes 1179652
  41.4 2.7 %collective-permute-start.2 = (bf16[2,28,64,128]{3,2,1,0:T(8,128)(2,1)}, bf16[2,28,64,128]{3,2,1,0:T(8,128)(2,1)S(1)}, u32[]{:S(2)}, u32[]{:S(2)}) collective-permute-start(bf16[2,28,64,128]{3,2,1,0:T(8,128)(2,1)} %get-tuple-element.24), channel_id=1, source_target_pairs={{0,4},{4,0},{8,12},{12,8},{16,20},{20,16},{24,28},{28,24},{1,5},{5... | collective-permute-start | bytes 2752520 | tf_op jit(solution)/shard_map/ppermute | solution.py:386
  45.9 12.5 %collective-permute-start.3 = (bf16[2,7,64,128]{3,2,1,0:T(8,128)(2,1)S(1)}, bf16[2,7,64,128]{3,2,1,0:T(8,128)(2,1)S(1)}, u32[]{:S(2)}, u32[]{:S(2)}) collective-permute-start(bf16[2,7,64,128]{3,2,1,0:T(8,128)(2,1)S(1)} %get-tuple-element.27), channel_id=1, source_target_pairs={{0,1},{1,0},{2,3},{3,2},{4,5},{5,4},{6,7},{7,6},{8,9},{9,8},{10,11... | collective-permute-start | bytes 688136 | tf_op jit(solution)/shard_map/ppermute | solution.py:404
  46.0 12.6 %collective-permute-start.4 = (bf16[2,7,64,128]{3,2,1,0:T(8,128)(2,1)S(1)}, bf16[2,7,64,128]{3,2,1,0:T(8,128)(2,1)S(1)}, u32[]{:S(2)}, u32[]{:S(2)}) collective-permute-start(bf16[2,7,64,128]{3,2,1,0:T(8,128)(2,1)S(1)} %get-tuple-element.28), channel_id=1, source_target_pairs={{0,2},{1,3},{2,0},{3,1},{4,6},{5,7},{6,4},{7,5},{8,10},{9,11},{10,... | collective-permute-start | bytes 688136 | tf_op jit(solution)/shard_map/ppermute | solution.py:404
  47.9 10.6 %collective-permute-start.5 = (bf16[2,7,64,128]{3,2,1,0:T(8,128)(2,1)S(1)}, bf16[2,7,64,128]{3,2,1,0:T(8,128)(2,1)S(1)}, u32[]{:S(2)}, u32[]{:S(2)}) collective-permute-start(bf16[2,7,64,128]{3,2,1,0:T(8,128)(2,1)S(1)} %get-tuple-element.29), channel_id=1, source_target_pairs={{0,3},{1,2},{2,1},{3,0},{4,7},{5,6},{6,5},{7,4},{8,11},{9,10},{10,... | collective-permute-start | bytes 688136 | tf_op jit(solution)/shard_map/ppermute | solution.py:404
  58.7 4.8 %collective-permute-start.6 = (bf16[2,7,16,128]{3,2,1,0:T(8,128)(2,1)S(1)}, bf16[2,7,16,128]{3,2,1,0:T(8,128)(2,1)S(1)}, u32[]{:S(2)}, u32[]{:S(2)}) collective-permute-start(bf16[2,7,16,128]{3,2,1,0:T(8,128)(2,1)S(1)} %get-tuple-element.47), channel_id=1, source_target_pairs={{0,8},{4,12},{8,0},{12,4},{16,24},{20,28},{24,16},{28,20},{1,9},{5... | collective-permute-start | bytes 172040 | tf_op jit(solution)/shard_map/ppermute | solution.py:418
  60.4 6.3 %collective-permute-start.7 = (bf16[2,7,16,128]{3,2,1,0:T(8,128)(2,1)S(1)}, bf16[2,7,16,128]{3,2,1,0:T(8,128)(2,1)S(1)}, u32[]{:S(2)}, u32[]{:S(2)}) collective-permute-start(bf16[2,7,16,128]{3,2,1,0:T(8,128)(2,1)S(1)} %get-tuple-element.49), channel_id=1, source_target_pairs={{0,16},{4,20},{8,24},{12,28},{16,0},{20,4},{24,8},{28,12},{1,17},{... | collective-permute-start | bytes 172040 | tf_op jit(solution)/shard_map/ppermute | solution.py:418
  63.0 6.0 %collective-permute-start.8 = (bf16[2,7,16,128]{3,2,1,0:T(8,128)(2,1)S(1)}, bf16[2,7,16,128]{3,2,1,0:T(8,128)(2,1)S(1)}, u32[]{:S(2)}, u32[]{:S(2)}) collective-permute-start(bf16[2,7,16,128]{3,2,1,0:T(8,128)(2,1)S(1)} %get-tuple-element.48), channel_id=1, source_target_pairs={{0,24},{4,28},{8,16},{12,20},{16,8},{20,12},{24,0},{28,4},{1,25},{... | collective-permute-start | bytes 172040 | tf_op jit(solution)/shard_map/ppermute | solution.py:418
  69.0 5.0 %collective-permute-start.9 = (f32[2,7,16,128]{3,2,1,0:T(8,128)S(1)}, f32[2,7,16,128]{3,2,1,0:T(8,128)S(1)}, u32[]{:S(2)}, u32[]{:S(2)}) collective-permute-start(f32[2,7,16,128]{3,2,1,0:T(8,128)S(1)} %get-tuple-element.36), channel_id=1, source_target_pairs={{0,1},{1,0},{2,3},{3,2},{4,5},{5,4},{6,7},{7,6},{8,9},{9,8},{10,11... | collective-permute-start | bytes 344072 | tf_op jit(solution)/shard_map/ppermute | solution.py:429
  70.8 4.8 %collective-permute-start.10 = (f32[2,7,16,128]{3,2,1,0:T(8,128)S(1)}, f32[2,7,16,128]{3,2,1,0:T(8,128)S(1)}, u32[]{:S(2)}, u32[]{:S(2)}) collective-permute-start(f32[2,7,16,128]{3,2,1,0:T(8,128)S(1)} %get-tuple-element.36), channel_id=1, source_target_pairs={{0,2},{1,3},{2,0},{3,1},{4,6},{5,7},{6,4},{7,5},{8,10},{9,11},{10,... | collective-permute-start | bytes 344072 | tf_op jit(solution)/shard_map/ppermute | solution.py:429
  71.1 5.7 %collective-permute-start.11 = (f32[2,7,16,128]{3,2,1,0:T(8,128)S(1)}, f32[2,7,16,128]{3,2,1,0:T(8,128)S(1)}, u32[]{:S(2)}, u32[]{:S(2)}) collective-permute-start(f32[2,7,16,128]{3,2,1,0:T(8,128)S(1)} %get-tuple-element.36), channel_id=1, source_target_pairs={{0,3},{1,2},{2,1},{3,0},{4,7},{5,6},{6,5},{7,4},{8,11},{9,10},{10,... | collective-permute-start | bytes 344072 | tf_op jit(solution)/shard_map/ppermute | solution.py:429

commit v2 on v1

--- a/solution.py
+++ b/solution.py
@@ -11,7 +11,10 @@
 F32 = jnp.float32
 BF16 = jnp.bfloat16
 MIB = 2**20
+LIMIT = 60 * MIB
+OUTER_LIMIT = 52 * MIB
 ANY = pl.BlockSpec(memory_space=pl.ANY)
+HBM = pl.BlockSpec(memory_space=pltpu.HBM)
 SMEM = pl.BlockSpec(memory_space=pltpu.SMEM)
 
 
@@ -38,24 +41,19 @@
     var[2, plane, rows] = jnp.where(place > 0, earlier, 0.0).astype(x.dtype)
 
 
-def fill_weights(tiles, w_ref):
+def fill_tile(tiles, w_ref, j):
     ch = w_ref.shape[1]
     zero = jnp.zeros((ch, ch), tiles.dtype)
-
-    def one(j, carry):
-        a, c = j // 3, j % 3
-        low, mid, high = (w_ref[9 * a + 3 * b + c].T for b in range(3))
-        tiles[j, 0, :ch, :ch] = mid
-        tiles[j, 0, :ch, ch:] = high
-        tiles[j, 0, ch:, :ch] = low
-        tiles[j, 0, ch:, ch:] = mid
-        tiles[j, 1, :ch, :ch] = high
-        tiles[j, 1, :ch, ch:] = zero
-        tiles[j, 1, ch:, :ch] = zero
-        tiles[j, 1, ch:, ch:] = low
-        return carry
-
-    lax.fori_loop(0, 9, one, 0)
+    a, c = j // 3, j % 3
+    low, mid, high = (w_ref[9 * a + 3 * b + c].T for b in range(3))
+    tiles[j, 0, :ch, :ch] = mid
+    tiles[j, 0, :ch, ch:] = high
+    tiles[j, 0, ch:, :ch] = low
+    tiles[j, 0, ch:, ch:] = mid
+    tiles[j, 1, :ch, :ch] = high
+    tiles[j, 1, :ch, ch:] = zero
+    tiles[j, 1, ch:, :ch] = zero
+    tiles[j, 1, ch:, ch:] = low
 
 
 def back_planes(var, tiles, d, count):
@@ -129,9 +127,9 @@
 def grouped(body):
     @functools.partial(loop, 0, 2)
     def _(i):
-        body([4 * i + k for k in range(4)])
-
-    return lambda: body([8])
+        body([4 * i + k for k in range(4)], i)
+
+    return lambda: body([8], None)
 
 
 def hidden_plane(back, pre):
@@ -156,13 +154,13 @@
 
 
 def inner_kernel(
-    taps, cot_hbm, pre_hbm, w_hbm, hid_hbm, part_hbm, tiles_hbm,
-    cot, pre, w, var, act_t, tiles, hid, part, sems,
+    cot_hbm, pre_hbm, vol_hbm, w_hbm, hid_hbm, part_hbm, tiles_hbm, in_t_hbm,
+    cot, pre, vol, w, var, act_t, in_t, tiles, hid, part, sems,
 ):
     depth, height, width, ch = cot.shape
     copies = [
         pltpu.make_async_copy(a, b, sems.at[i])
-        for i, (a, b) in enumerate(((w_hbm, w), (cot_hbm, cot), (pre_hbm, pre)))
+        for i, (a, b) in enumerate(((cot_hbm, cot), (pre_hbm, pre), (w_hbm, w), (vol_hbm, vol)))
     ]
     for c in copies:
         c.start()
@@ -171,27 +169,34 @@
     var[:, 0] = edge
     var[:, depth + 1] = edge
     clear_ends(act_t, depth)
-    copies[0].wait()
-    fill_weights(tiles, w)
-    tiles_out = pltpu.make_async_copy(tiles, tiles_hbm, sems.at[3])
-    tiles_out.start()
-    copies[1].wait()
-    copies[2].wait()
+    clear_ends(in_t, depth)
+    for c in copies:
+        c.wait()
 
     @functools.partial(loop, 0, depth)
     def _(d):
         fill_plane(var, d + 1, cot[d])
         transpose_plane(act_t, d + 1, silu_of(pre[d]))
 
-    def terms(group):
+    def terms(group, half):
         r = depth_terms(act_t, var, group, depth)
+        for t in group:
+            fill_tile(tiles, w, t)
+        if half is not None:
+            for k in range(depth // 2):
+                d = half * (depth // 2) + k
+                transpose_plane(in_t, d + 1, vol[d])
         for k, t in enumerate(group):
             for a in range(3):
                 part[9 * a + t] = r[a * ch : (a + 1) * ch, k * ch : (k + 1) * ch]
 
     grouped(terms)()
-    part_out = pltpu.make_async_copy(part, part_hbm, sems.at[5])
-    part_out.start()
+    outs = [
+        pltpu.make_async_copy(a, b, sems.at[4 + i])
+        for i, (a, b) in enumerate(((tiles, tiles_hbm), (part, part_hbm), (in_t, in_t_hbm)))
+    ]
+    for c in outs:
+        c.start()
     step = step_of(depth - 2)
 
     @functools.partial(loop, 0, (depth - 2) // step)
@@ -200,35 +205,38 @@
         grad = hidden_plane(back_planes(var, tiles, d, step), pre[pl.ds(d, step)])
         hid[pl.ds(d - 1, step)] = unpaired(grad, height, width)
 
-    hid_out = pltpu.make_async_copy(hid, hid_hbm, sems.at[4])
+    inner = hid_hbm.at[pl.ds(2, depth - 2)]
+    hid_out = pltpu.make_async_copy(hid, inner, sems.at[7])
     hid_out.start()
-    tiles_out.wait()
-    part_out.wait()
-    hid_out.wait()
+    for c in outs + [hid_out]:
+        c.wait()
+
+
+def bit(code, place):
+    return lax.rem(lax.div(code, 2**place), 2)
 
 
 def outer_kernel(
-    ranks, taps, where_ref, far_a_hbm, far_b_hbm, cot_hbm, pre_hbm, in_hbm, hid_hbm, part_hbm,
-    tiles_hbm, ext_hbm, keep_hbm, send_hbm,
-    far_a, far_b, cot, pre, vol, ext, part, tiles, cvar, hvar, act_t, in_t, keep, send, sems,
+    ranks, taps, where_ref, far_a_hbm, far_b_hbm, cot_hbm, pre_hbm, hid_hbm, part_hbm,
+    tiles_hbm, in_t_hbm, ext_hbm, keep_hbm, send_hbm,
+    far_a, far_b, cot, pre, ext, part, tiles, cvar, hvar, act_t, in_t, keep, send, sems,
 ):
-    depth, height, width, ch = vol.shape
-    n = height * width
-    even, core = where_ref[0] == 0, where_ref[1]
+    depth, height, width, ch = ext.shape[0] - 2, *ext.shape[1:]
+    code = where_ref[0]
+    even, core = bit(code, 0) == 0, bit(code, 1)
     pairs = (
         (far_a_hbm, far_a), (far_b_hbm, far_b),
         (cot_hbm.at[pl.ds(0, 2)], cot.at[pl.ds(0, 2)]),
         (cot_hbm.at[pl.ds(depth - 2, 2)], cot.at[pl.ds(2, 2)]),
         (pre_hbm.at[0], pre.at[1]), (pre_hbm.at[depth - 1], pre.at[2]),
-        (tiles_hbm, tiles), (in_hbm, vol),
-        (hid_hbm, ext.at[pl.ds(2, depth - 2)]), (part_hbm, part),
+        (tiles_hbm, tiles), (hid_hbm.at[pl.ds(2, depth - 2)], ext.at[pl.ds(2, depth - 2)]),
+        (part_hbm, part), (in_t_hbm, in_t),
     )
     copies = [pltpu.make_async_copy(a, b, sems.at[i]) for i, (a, b) in enumerate(pairs)]
     for c in copies:
         c.start()
     clear_rows(cvar)
     clear_rows(hvar)
-    clear_ends(in_t, depth)
     for c in copies[:6]:
         c.wait()
     for i in range(2):
@@ -240,31 +248,26 @@
     pre[0] = jnp.where(even, far_b[2], far_a[2])
     pre[3] = jnp.where(even, far_a[2], far_b[2])
     copies[6].wait()
-    copies[8].wait()
-
+    copies[7].wait()
+    inner = depth - 2
     for late in range(2):
         back = back_planes(cvar, tiles, 4 * late, 2)
+        for d in range(inner // 2 * late, inner if late else inner // 2):
+            fill_plane(hvar, 2 + d, ext[2 + d])
         grad = hidden_plane(back, pre[2 * late : 2 * late + 2])
         planes = unpaired(grad, height, width)
-        there = where_ref[2 + late] == 1
+        there = bit(code, 2 + late) == 1
         outside = jnp.where(there, planes[late].astype(F32), 0.0).astype(BF16)
         ext[depth * late + late] = outside
+        fill_plane(hvar, depth * late + late, outside)
         ext[(depth - 1) * late + 1] = planes[1 - late]
+        fill_plane(hvar, (depth - 1) * late + 1, planes[1 - late])
 
     ext_out = pltpu.make_async_copy(ext, ext_hbm, sems.at[10])
     ext_out.start()
-    copies[7].wait()
-
-    @functools.partial(loop, 0, depth)
-    def _(d):
-        fill_plane(hvar, d, ext[d])
-        transpose_plane(in_t, d + 1, vol[d])
-
-    fill_plane(hvar, depth, ext[depth])
-    fill_plane(hvar, depth + 1, ext[depth + 1])
-    copies[9].wait()
-
-    def seconds(group):
+    copies[8].wait()
+
+    def seconds(group, _):
         low, high = edge_terms(act_t, cvar, 1, 6, group)
         for k, t in enumerate(group):
             cols = slice(k * ch, (k + 1) * ch)
@@ -284,7 +287,7 @@
     for c in outs:
         c.start()
 
-    def firsts(group):
+    def firsts(group, _):
         r = depth_terms(in_t, hvar, group, depth)
         low, high = edge_terms(in_t, hvar, 0, depth + 1, group)
         for k, t in enumerate(group):
@@ -293,6 +296,7 @@
             store_tap(keep, send, 0, core, 9 + t, r[ch : 2 * ch, cols], ranks)
             store_tap(keep, send, 0, core, 18 + t, r[2 * ch :, cols] + low[:, cols], ranks)
 
+    copies[9].wait()
     finish = grouped(firsts)
 
     def leave(first, count, sem):
@@ -331,7 +335,7 @@
         c.start()
     clear_rows(var)
     copies[0].wait()
-    fill_weights(tiles, w)
+    loop(0, 9, functools.partial(fill_tile, tiles, w))
     copies[1].wait()
 
     @functools.partial(loop, 0, depth + 2)
@@ -350,35 +354,60 @@
     c.wait()
 
 
-def call(body, out_shape, operands, scratch, sems, flops, n_smem=0):
+def call(body, out_shape, operands, scratch, sems, flops, n_smem=0, limit=LIMIT, n_any=0):
     moved = sum(x.size * x.dtype.itemsize for x in operands)
     return pl.pallas_call(
         body,
         out_shape=out_shape,
-        in_specs=[SMEM] * n_smem + [ANY] * (len(operands) - n_smem),
-        out_specs=jax.tree.map(lambda _: ANY, out_shape),
+        in_specs=[SMEM] * n_smem + [ANY] * n_any + [HBM] * (len(operands) - n_smem - n_any),
+        out_specs=jax.tree.map(lambda _: HBM, out_shape),
         scratch_shapes=[pltpu.VMEM(*x) for x in scratch] + [pltpu.SemaphoreType.DMA((sems,))],
-        compiler_params=pltpu.CompilerParams(vmem_limit_bytes=60 * MIB),
+        compiler_params=pltpu.CompilerParams(vmem_limit_bytes=limit),
         cost_estimate=pl.CostEstimate(flops=flops, bytes_accessed=moved, transcendentals=0),
     )(*operands)
 
 
+def farthest_first(n):
+    return range(n - 1, 0, -1)
+
+
 def partner(i, k, n):
     return i ^ k if n & (n - 1) == 0 else (i + k) % n
 
 
-def swap_faces(cot, pre, even):
-    peers, depth = lax.axis_size("slab"), cot.shape[0]
+def faces_kernel(where_ref, cot_hbm, pre_hbm, a_ref, b_ref, sems):
+    depth = cot_hbm.shape[0]
+    first = bit(where_ref[0], 0)
+    copies = []
+    for i, (out, low) in enumerate(((a_ref, first), (b_ref, 1 - first))):
+        for k, (x, count) in enumerate(((cot_hbm, 2), (pre_hbm, 1))):
+            start = (1 - low) * (depth - count)
+            copies.append(
+                pltpu.make_async_copy(
+                    x.at[pl.ds(start, count)], out.at[pl.ds(2 * k, count)], sems.at[2 * i + k]
+                )
+            )
+    for c in copies:
+        c.start()
+    for c in copies:
+        c.wait()
+
+
+def swap_faces(where, cot, pre):
+    peers = lax.axis_size("slab")
     a = [(i, i ^ 1) for i in range(peers) if i ^ 1 < peers]
     b = [(i, j) for i in range(peers) for j in [((i + 1) ^ 1) - 1] if 0 <= j < peers]
-
-    def face(last):
-        cut = lambda x, count: lax.dynamic_slice_in_dim(
-            x, jnp.where(last, depth - count, 0), count, 0
-        )
-        return jnp.concatenate([cut(cot, 2), cut(pre, 1)])
-
-    return lax.ppermute(face(even), "slab", a), lax.ppermute(face(~even), "slab", b)
+    face = jax.ShapeDtypeStruct((3,) + cot.shape[1:], cot.dtype)
+    vmem = pl.BlockSpec(memory_space=pltpu.VMEM)
+    to_a, to_b = pl.pallas_call(
+        faces_kernel,
+        out_shape=(face, face),
+        in_specs=[SMEM, HBM, HBM],
+        out_specs=(vmem, vmem),
+        scratch_shapes=[pltpu.SemaphoreType.DMA((4,))],
+        compiler_params=pltpu.CompilerParams(vmem_limit_bytes=LIMIT),
+    )(where, cot, pre)
+    return lax.ppermute(to_a, "slab", a), lax.ppermute(to_b, "slab", b)
 
 
 def swap_cores(send):
@@ -394,15 +423,15 @@
         cut = lambda x: lax.dynamic_slice_in_dim(x, i * count, count, 1)
         return cut(keep) + cut(got).astype(F32)
 
-    others = [piece(partner(me, k, peers)).astype(BF16) for k in range(1, peers)]
+    others = [piece(partner(me, k, peers)).astype(BF16) for k in farthest_first(peers)]
     return piece(me), others
 
 
 def trade_slab(others):
     peers = lax.axis_size("slab")
     return [
-        lax.ppermute(x, "slab", [(i, partner(i, k + 1, peers)) for i in range(peers)])
-        for k, x in enumerate(others)
+        lax.ppermute(x, "slab", [(i, partner(i, k, peers)) for i in range(peers)])
+        for k, x in zip(farthest_first(peers), others)
     ]
 
 
@@ -410,12 +439,14 @@
     ranks, me = lax.axis_size("rep"), lax.axis_index("rep")
     peers = ranks // 2
     count = total.shape[2] // peers
-    out = lax.dynamic_slice_in_dim(total, me // 2 * count, count, 2)
-    for k in range(1, peers):
-        other = partner(me // 2, k, peers)
-        piece = lax.dynamic_slice_in_dim(total, other * count, count, 2).astype(BF16)
+    cut = lambda i: lax.dynamic_slice_in_dim(total, i * count, count, 2)
+    order = farthest_first(peers)
+    pieces = [cut(partner(me // 2, k, peers)).astype(BF16) for k in order]
+    pieces = lax.optimization_barrier(pieces)
+    out = cut(me // 2)
+    for k, x in zip(order, pieces):
         perm = [(i, 2 * partner(i // 2, k, peers) + i % 2) for i in range(ranks)]
-        out = out + lax.ppermute(piece, "rep", perm).astype(F32)
+        out = out + lax.ppermute(x, "rep", perm).astype(F32)
     return out
 
 
@@ -424,7 +455,7 @@
     count = part.shape[1]
     shape = (part.shape[0], count * peers) + part.shape[2:]
     out = lax.dynamic_update_slice_in_dim(jnp.zeros(shape, part.dtype), part, me * count, 1)
-    for k in range(1, peers):
+    for k in farthest_first(peers):
         perm = [(i, partner(i, k, peers)) for i in range(peers)]
         got = lax.ppermute(part, "slab", perm)
         source = partner(me, k, peers) if peers & (peers - 1) == 0 else (me - k) % peers
@@ -440,8 +471,9 @@
     padded_taps = -(-taps // slabs) * slabs
     n = height * width
     me = lax.axis_index("slab")
-    even = me % 2 == 0
-    where = jnp.stack([me % 2, lax.axis_index("rep") % 2, me > 0, me < slabs - 1]).astype(jnp.int32)
+    core = lax.axis_index("rep") % 2
+    code = me % 2 + 2 * core + 4 * (me > 0) + 8 * (me < slabs - 1)
+    where = code.astype(jnp.int32).reshape(1)
     s = jax.ShapeDtypeStruct
     sweep = 2 * taps * depth * n * ch * ch
     plane = (height, width, ch)
@@ -453,23 +485,23 @@
     keep_of = ((2, padded_taps, ch // 2, ch), F32)
     send_of = (keep_of[0], BF16)
 
-    far_a, far_b = swap_faces(cot, pre, even)
-    hid, part, tiles2 = call(
-        functools.partial(inner_kernel, taps),
-        (s(*many(depth - 2)), s(*part_of), s(*tiles_of)),
-        (cot, pre, weight_two),
-        [many(depth), many(depth), weights_of, shifted(depth + 2), ((ch, (depth + 2) * n), BF16),
+    turned = ((ch, (depth + 2) * n), BF16)
+    far_a, far_b = swap_faces(where, cot, pre)
+    hid, part, tiles2, in_t = call(
+        inner_kernel,
+        (s(*many(depth + 2)), s(*part_of), s(*tiles_of), s(*turned)),
+        (cot, pre, volume_in, weight_two),
+        [many(depth), many(depth), many(depth), weights_of, shifted(depth + 2), turned, turned,
          tiles_of, many(depth - 2), part_of],
-        6, 2 * sweep,
+        8, 2 * sweep,
     )
     ext, keep, send = call(
         functools.partial(outer_kernel, ranks, taps),
         (s(*many(depth + 2)), s(*keep_of), s(*send_of)),
-        (where, far_a, far_b, cot, pre, volume_in, hid, part, tiles2),
-        [many(3), many(3), many(4), many(4), many(depth), many(depth + 2), part_of, tiles_of,
-         shifted(8), shifted(depth + 2), ((ch, 4 * n), BF16), ((ch, (depth + 2) * n), BF16),
-         keep_of, send_of],
-        25, 3 * sweep // 2, 1,
+        (where, far_a, far_b, cot, pre, hid, part, tiles2, in_t),
+        [many(3), many(3), many(4), many(4), many(depth + 2), part_of, tiles_of,
+         shifted(8), shifted(depth + 2), ((ch, 4 * n), BF16), turned, keep_of, send_of],
+        25, 3 * sweep // 2, 1, OUTER_LIMIT, 2,
     )
     got = swap_cores(send)
     mine, others = slab_pieces(keep, got)

time: 77.8 us -> 73.6 us (0.946)
  waiting for transfers between devices: 15.4 us -> 11.8 us
  local copies, waits for them, and re-layouts: 3.76 us -> 0.89 us
  Pallas kernels: 36.9 us -> 38.6 us
  starting transfers between devices: 18.1 us -> 19.3 us
    ppermute x8, waiting for transfers between devices: 8.65 us -> 4.85 us  [the longest x3 4.44 us: scatter_ranks(): out = out + lax.ppermute(x, 'rep', perm).astype(F32)]
    dynamic_slice x2 -> x0, local copies, waits for them, and re-layouts: 2.07 us -> none  [face(): lax.dynamic_slice_in_dim(x, jnp.where(last, depth - count, 0), count, 0)]
    pallas_call x0 -> x1, Pallas kernels: none -> 2.04 us  [swap_faces(): pl.pallas_call(faces_kernel, out_shape=(face, face), in_specs=[SMEM, HBM,...]
    ppermute x8, starting transfers between devices: 14.4 us -> 15.6 us  [the longest x3 7.42 us: trade_slab(): lax.ppermute(x, 'slab', [(i, partner(i, k, peers)) for i in range(peers)])]
    unnamed x4 -> x0, local copies, waits for them, and re-layouts: 0.8 us -> none
  transfers between devices with their start and end apart: 12 -> 12, of which waited for: 9 -> 7; matrix products, arithmetic and copies ran while one was open for 1% -> 0% of each run, Pallas kernels for 29% -> 31%
where the time goes in v2:
time: 73.6 us; the launch traced here: 73.3 us
  Pallas kernels  38.6 us (52%)
  starting transfers between devices  19.3 us (26%)
  waiting for transfers between devices  11.8 us (16%)
  other arithmetic  1.86 us (3%)
  local copies, waits for them, and re-layouts  0.89 us (1%)
  between operations  0.85 us (1%)
    pallas_call x3, Pallas kernels, call(): pl.pallas_call(body, out_shape=out_shape, in_specs=[SMEM] * n_smem + [ANY...  36.6 us
    ppermute x3, starting transfers between devices, trade_slab(): lax.ppermute(x, 'slab', [(i, partner(i, k, peers)) for i in range(peers)])  7.42 us
    ppermute x3, waiting for transfers between devices, gather_slab(): got = lax.ppermute(part, 'slab', perm)  4.58 us
    ppermute x3, starting transfers between devices, scatter_ranks(): out = out + lax.ppermute(x, 'rep', perm).astype(F32)  4.5 us
    ppermute x3, waiting for transfers between devices, scatter_ranks(): out = out + lax.ppermute(x, 'rep', perm).astype(F32)  4.44 us
    ppermute x2, starting transfers between devices, swap_faces(): return (lax.ppermute(to_a, 'slab', a), lax.ppermute(to_b, 'slab', b))  3.71 us
    ppermute x3, starting transfers between devices, gather_slab(): got = lax.ppermute(part, 'slab', perm)  3.55 us
    ppermute x1, waiting for transfers between devices, swap_cores(): return lax.ppermute(send, 'rep', [(i, i ^ 1) for i in range(ranks)])  2.4 us
  transfers between devices with their start and end apart: 12, of which 7 were waited for; matrix products, arithmetic and copies ran while one was open for 0% of the time, Pallas kernels for 31%

profile of v2, /device:TPU:0, one launch (start us, length us, event | category | flops | bytes accessed | tf_op | source)
XLA Modules:
  0.0 73.3 jit_solution(16366060775267610903)
XLA Ops:
  0.7 2.0 %shard_map.76 = (bf16[3,32,16,128]{3,2,1,0:T(8,128)(2,1)}, bf16[3,32,16,128]{3,2,1,0:T(8,128)(2,1)}) custom-call(s32[1]{0:T(128)} %bitcast.where_ref, bf16[8,32,16,128]{3,2,1,0:T(8,128)(2,1)} %bitcast.9, bf16[8,32,16,128]{3,2,1,0:T(8,128)(2,1)} %bitcast.12), custom_call_target="tpu_custom_call" | custom-call | tf_op jit(solution)/shard_map/pallas_call | solution.py:402
  2.7 3.0 %collective-permute-start = (bf16[3,32,16,128]{3,2,1,0:T(8,128)(2,1)}, bf16[3,32,16,128]{3,2,1,0:T(8,128)(2,1)S(1)}, u32[]{:S(2)}, u32[]{:S(2)}) collective-permute-start(bf16[3,32,16,128]{3,2,1,0:T(8,128)(2,1)} %get-tuple-element.25), channel_id=1, source_target_pairs={{0,1},{1,0},{2,3},{3,2},{4,5},{5,4},{6,7},{7,6},{8,9},{9,8},{10,11... | collective-permute-start | bytes 1179656 | tf_op jit(solution)/shard_map/ppermute | solution.py:410
  5.7 0.7 collective-permute-start.1
  6.4 13.8 %shard_map.77 = (bf16[10,32,16,128]{3,2,1,0:T(8,128)(2,1)}, f32[27,128,128]{2,1,0:T(8,128)}, bf16[9,2,256,256]{3,2,1,0:T(8,128)(2,1)}, bf16[128,5120]{1,0:T(8,128)(2,1)}) custom-call(bf16[8,32,16,128]{3,2,1,0:T(8,128)(2,1)} %bitcast.10, bf16[8,32,16,128]{3,2,1,0:T(8,128)(2,1)} %bitcast.13, bf16[8,32,16,128]{3,2,1,0:T(8,128)(2,1)} %bitcast.15, ...), custom_call_target="tpu_custom_call" | custom-call | flops 7247757312 | bytes 4030464 | tf_op jit(solution)/shard_map/pallas_call | solution.py:359
  20.3 0.0 collective-permute-done.far_a_hbm
  20.3 0.0 collective-permute-done.1.far_b_hbm
  20.3 13.8 %shard_map.78 = (bf16[10,32,16,128]{3,2,1,0:T(8,128)(2,1)}, f32[2,28,64,128]{3,2,1,0:T(8,128)}, bf16[2,28,64,128]{3,2,1,0:T(8,128)(2,1)S(1)}) custom-call(s32[1]{0:T(128)} %bitcast.where_ref, bf16[3,32,16,128]{3,2,1,0:T(8,128)(2,1)S(1)} %collective-permute-done.far_a_hbm, bf16[3,32,16,128]{3,2,1,0:T(8,128)(2,1)S(1)} %collective-permute-done.1.far_b_hbm, ...), custom_call_target="tpu_custom_call" | custom-call | flops 5435817984 | bytes 9633796 | tf_op jit(solution)/shard_map/pallas_call | solution.py:359
  34.1 0.1 collective-permute-start.2
  34.2 2.4 %collective-permute-done.2 = bf16[2,28,64,128]{3,2,1,0:T(8,128)(2,1)S(1)} collective-permute-done((bf16[2,28,64,128]{3,2,1,0:T(8,128)(2,1)S(1)}, bf16[2,28,64,128]{3,2,1,0:T(8,128)(2,1)S(1)}, u32[]{:S(2)}, u32[]{:S(2)}) %collective-permute-start.2) | collective-permute-done | bytes 917536 | tf_op jit(solution)/shard_map/ppermute | solution.py:415
  36.6 1.7 %add_convert_fusion = (bf16[2,7,64,128]{3,2,1,0:T(8,128)(2,1)S(1)}, bf16[2,7,64,128]{3,2,1,0:T(8,128)(2,1)S(1)}, bf16[2,7,64,128]{3,2,1,0:T(8,128)(2,1)S(1)}, f32[2,7,64,128]{3,2,1,0:T(8,128)S(1)}) fusion(f32[2,28,64,128]{3,2,1,0:T(8,128)} %get-tuple-element.32, s32[]{:T(128)S(6)} %select_n.55, bf16[2,28,64,128]{3,2,1,0:T(8,128)(2,1)S(1)} %collective-permute-done.2, ...), kind=kLoop, calls=%fused_computation.1 | loop fusion | flops 1261568 | bytes 3899408 | tf_op jit(solution)/shard_map/convert_element_type | solution.py:426
  38.4 1.6 %collective-permute-start.3 = (bf16[2,7,64,128]{3,2,1,0:T(8,128)(2,1)S(1)}, bf16[2,7,64,128]{3,2,1,0:T(8,128)(2,1)S(1)}, u32[]{:S(2)}, u32[]{:S(2)}) collective-permute-start(bf16[2,7,64,128]{3,2,1,0:T(8,128)(2,1)S(1)} %get-tuple-element.36), channel_id=1, source_target_pairs={{0,3},{1,2},{2,1},{3,0},{4,7},{5,6},{6,5},{7,4},{8,11},{9,10},{10,... | collective-permute-start | bytes 688136 | tf_op jit(solution)/shard_map/ppermute | solution.py:433
  39.9 5.9 %collective-permute-start.4 = (bf16[2,7,64,128]{3,2,1,0:T(8,128)(2,1)S(1)}, bf16[2,7,64,128]{3,2,1,0:T(8,128)(2,1)S(1)}, u32[]{:S(2)}, u32[]{:S(2)}) collective-permute-start(bf16[2,7,64,128]{3,2,1,0:T(8,128)(2,1)S(1)} %get-tuple-element.37), channel_id=1, source_target_pairs={{0,2},{1,3},{2,0},{3,1},{4,6},{5,7},{6,4},{7,5},{8,10},{9,11},{10,... | collective-permute-start | bytes 688136 | tf_op jit(solution)/shard_map/ppermute | solution.py:433
  45.8 0.0 collective-permute-start.5
  45.8 9.0 %shard_map.79 = bf16[8,32,16,128]{3,2,1,0:T(8,128)(2,1)} custom-call(bf16[10,32,16,128]{3,2,1,0:T(8,128)(2,1)} %get-tuple-element.34.ext_hbm, bf16[27,128,128]{2,1,0:T(8,128)(2,1)} %w_hbm.2), custom_call_target="tpu_custom_call" | custom-call | flops 3623878656 | bytes 2195456 | tf_op jit(solution)/shard_map/pallas_call | solution.py:359
  54.8 0.0 collective-permute-done.3
  54.8 0.0 collective-permute-done.4
  54.8 0.4 collective-permute-done.5
  55.2 0.1 convert_add_fusion
  55.3 3.9 %collective-permute-start.6 = (bf16[2,7,16,128]{3,2,1,0:T(8,128)(2,1)S(1)}, bf16[2,7,16,128]{3,2,1,0:T(8,128)(2,1)S(1)}, u32[]{:S(2)}, u32[]{:S(2)}) collective-permute-start(bf16[2,7,16,128]{3,2,1,0:T(8,128)(2,1)S(1)} %get-tuple-element.44), channel_id=1, source_target_pairs={{0,24},{4,28},{8,16},{12,20},{16,8},{20,12},{24,0},{28,4},{1,25},{... | collective-permute-start | bytes 172040 | tf_op jit(solution)/shard_map/ppermute | solution.py:449
  59.2 0.0 collective-permute-start.7
  59.2 0.6 collective-permute-start.8
  59.9 2.2 %collective-permute-done.6 = bf16[2,7,16,128]{3,2,1,0:T(8,128)(2,1)S(1)} collective-permute-done((bf16[2,7,16,128]{3,2,1,0:T(8,128)(2,1)S(1)}, bf16[2,7,16,128]{3,2,1,0:T(8,128)(2,1)S(1)}, u32[]{:S(2)}, u32[]{:S(2)}) %collective-permute-start.6) | collective-permute-done | bytes 57376 | tf_op jit(solution)/shard_map/ppermute | solution.py:449
  62.0 2.2 %collective-permute-done.7 = bf16[2,7,16,128]{3,2,1,0:T(8,128)(2,1)S(1)} collective-permute-done((bf16[2,7,16,128]{3,2,1,0:T(8,128)(2,1)S(1)}, bf16[2,7,16,128]{3,2,1,0:T(8,128)(2,1)S(1)}, u32[]{:S(2)}, u32[]{:S(2)}) %collective-permute-start.7) | collective-permute-done | bytes 57376 | tf_op jit(solution)/shard_map/ppermute | solution.py:449
  64.3 0.0 collective-permute-done.8
  64.4 2.5 %collective-permute-start.9 = (f32[2,7,16,128]{3,2,1,0:T(8,128)S(1)}, f32[2,7,16,128]{3,2,1,0:T(8,128)S(1)}, u32[]{:S(2)}, u32[]{:S(2)}) collective-permute-start(f32[2,7,16,128]{3,2,1,0:T(8,128)S(1)} %get-tuple-element.48), channel_id=1, source_target_pairs={{0,3},{1,2},{2,1},{3,0},{4,7},{5,6},{6,5},{7,4},{8,11},{9,10},{10,... | collective-permute-start | bytes 344072 | tf_op jit(solution)/shard_map/ppermute | solution.py:460
  66.9 0.7 collective-permute-start.10
  67.6 0.3 collective-permute-start.11
  67.9 3.4 %collective-permute-done.9 = f32[2,7,16,128]{3,2,1,0:T(8,128)S(1)} collective-permute-done((f32[2,7,16,128]{3,2,1,0:T(8,128)S(1)}, f32[2,7,16,128]{3,2,1,0:T(8,128)S(1)}, u32[]{:S(2)}, u32[]{:S(2)}) %collective-permute-start.9) | collective-permute-done | bytes 114720 | tf_op jit(solution)/shard_map/ppermute | solution.py:460
  71.3 0.8 %collective-permute-done.10 = f32[2,7,16,128]{3,2,1,0:T(8,128)S(1)} collective-permute-done((f32[2,7,16,128]{3,2,1,0:T(8,128)S(1)}, f32[2,7,16,128]{3,2,1,0:T(8,128)S(1)}, u32[]{:S(2)}, u32[]{:S(2)}) %collective-permute-start.10) | collective-permute-done | bytes 114720 | tf_op jit(solution)/shard_map/ppermute | solution.py:460
  72.1 0.4 collective-permute-done.11
  72.6 0.8 %slice_bitcast_fusion = (f32[27,16,128]{2,1,0:T(8,128)}, f32[27,16,128]{2,1,0:T(8,128)}) fusion(f32[2,28,16,128]{3,2,1,0:T(8,128)S(1)} %constant_dynamic-update-slice_fusion), kind=kLoop, calls=%fused_computation.5 | loop fusion | bytes 884736 | tf_op jit(solution)/shard_map/squeeze | solution.py:520
  (6 shorter events, 0.1 us)
Async XLA Ops:
  2.7 17.6 %collective-permute-start = (bf16[3,32,16,128]{3,2,1,0:T(8,128)(2,1)}, bf16[3,32,16,128]{3,2,1,0:T(8,128)(2,1)S(1)}, u32[]{:S(2)}, u32[]{:S(2)}) collective-permute-start(bf16[3,32,16,128]{3,2,1,0:T(8,128)(2,1)} %get-tuple-element.25), channel_id=1, source_target_pairs={{0,1},{1,0},{2,3},{3,2},{4,5},{5,4},{6,7},{7,6},{8,9},{9,8},{10,11... | collective-permute-start | bytes 1179656 | tf_op jit(solution)/shard_map/ppermute | solution.py:410
  5.7 14.5 %collective-permute-start.1 = (bf16[3,32,16,128]{3,2,1,0:T(8,128)(2,1)}, bf16[3,32,16,128]{3,2,1,0:T(8,128)(2,1)S(1)}, u32[]{:S(2)}, u32[]{:S(2)}) collective-permute-start(bf16[3,32,16,128]{3,2,1,0:T(8,128)(2,1)} %get-tuple-element.26), channel_id=1, source_target_pairs={{1,2},{2,1},{5,6},{6,5},{9,10},{10,9},{13,14},{14,13},{17,18},{18,... | collective-permute-start | bytes 1179656 | tf_op jit(solution)/shard_map/ppermute | solution.py:410
  34.1 2.5 %collective-permute-start.2 = (bf16[2,28,64,128]{3,2,1,0:T(8,128)(2,1)S(1)}, bf16[2,28,64,128]{3,2,1,0:T(8,128)(2,1)S(1)}, u32[]{:S(2)}, u32[]{:S(2)}) collective-permute-start(bf16[2,28,64,128]{3,2,1,0:T(8,128)(2,1)S(1)} %get-tuple-element.33), channel_id=1, source_target_pairs={{0,4},{4,0},{8,12},{12,8},{16,20},{20,16},{24,28},{28,24},{1,5},{5... | collective-permute-start | bytes 2752520 | tf_op jit(solution)/shard_map/ppermute | solution.py:415
  38.4 16.4 %collective-permute-start.3 = (bf16[2,7,64,128]{3,2,1,0:T(8,128)(2,1)S(1)}, bf16[2,7,64,128]{3,2,1,0:T(8,128)(2,1)S(1)}, u32[]{:S(2)}, u32[]{:S(2)}) collective-permute-start(bf16[2,7,64,128]{3,2,1,0:T(8,128)(2,1)S(1)} %get-tuple-element.36), channel_id=1, source_target_pairs={{0,3},{1,2},{2,1},{3,0},{4,7},{5,6},{6,5},{7,4},{8,11},{9,10},{10,... | collective-permute-start | bytes 688136 | tf_op jit(solution)/shard_map/ppermute | solution.py:433
  39.9 14.9 %collective-permute-start.4 = (bf16[2,7,64,128]{3,2,1,0:T(8,128)(2,1)S(1)}, bf16[2,7,64,128]{3,2,1,0:T(8,128)(2,1)S(1)}, u32[]{:S(2)}, u32[]{:S(2)}) collective-permute-start(bf16[2,7,64,128]{3,2,1,0:T(8,128)(2,1)S(1)} %get-tuple-element.37), channel_id=1, source_target_pairs={{0,2},{1,3},{2,0},{3,1},{4,6},{5,7},{6,4},{7,5},{8,10},{9,11},{10,... | collective-permute-start | bytes 688136 | tf_op jit(solution)/shard_map/ppermute | solution.py:433
  45.8 9.4 %collective-permute-start.5 = (bf16[2,7,64,128]{3,2,1,0:T(8,128)(2,1)S(1)}, bf16[2,7,64,128]{3,2,1,0:T(8,128)(2,1)S(1)}, u32[]{:S(2)}, u32[]{:S(2)}) collective-permute-start(bf16[2,7,64,128]{3,2,1,0:T(8,128)(2,1)S(1)} %get-tuple-element.38), channel_id=1, source_target_pairs={{0,1},{1,0},{2,3},{3,2},{4,5},{5,4},{6,7},{7,6},{8,9},{9,8},{10,11... | collective-permute-start | bytes 688136 | tf_op jit(solution)/shard_map/ppermute | solution.py:433
  55.3 6.7 %collective-permute-start.6 = (bf16[2,7,16,128]{3,2,1,0:T(8,128)(2,1)S(1)}, bf16[2,7,16,128]{3,2,1,0:T(8,128)(2,1)S(1)}, u32[]{:S(2)}, u32[]{:S(2)}) collective-permute-start(bf16[2,7,16,128]{3,2,1,0:T(8,128)(2,1)S(1)} %get-tuple-element.44), channel_id=1, source_target_pairs={{0,24},{4,28},{8,16},{12,20},{16,8},{20,12},{24,0},{28,4},{1,25},{... | collective-permute-start | bytes 172040 | tf_op jit(solution)/shard_map/ppermute | solution.py:449
  59.2 5.1 %collective-permute-start.7 = (bf16[2,7,16,128]{3,2,1,0:T(8,128)(2,1)S(1)}, bf16[2,7,16,128]{3,2,1,0:T(8,128)(2,1)S(1)}, u32[]{:S(2)}, u32[]{:S(2)}) collective-permute-start(bf16[2,7,16,128]{3,2,1,0:T(8,128)(2,1)S(1)} %get-tuple-element.45), channel_id=1, source_target_pairs={{0,16},{4,20},{8,24},{12,28},{16,0},{20,4},{24,8},{28,12},{1,17},{... | collective-permute-start | bytes 172040 | tf_op jit(solution)/shard_map/ppermute | solution.py:449
  59.2 5.1 %collective-permute-start.8 = (bf16[2,7,16,128]{3,2,1,0:T(8,128)(2,1)S(1)}, bf16[2,7,16,128]{3,2,1,0:T(8,128)(2,1)S(1)}, u32[]{:S(2)}, u32[]{:S(2)}) collective-permute-start(bf16[2,7,16,128]{3,2,1,0:T(8,128)(2,1)S(1)} %get-tuple-element.46), channel_id=1, source_target_pairs={{0,8},{4,12},{8,0},{12,4},{16,24},{20,28},{24,16},{28,20},{1,9},{5... | collective-permute-start | bytes 172040 | tf_op jit(solution)/shard_map/ppermute | solution.py:449
  64.4 6.9 %collective-permute-start.9 = (f32[2,7,16,128]{3,2,1,0:T(8,128)S(1)}, f32[2,7,16,128]{3,2,1,0:T(8,128)S(1)}, u32[]{:S(2)}, u32[]{:S(2)}) collective-permute-start(f32[2,7,16,128]{3,2,1,0:T(8,128)S(1)} %get-tuple-element.48), channel_id=1, source_target_pairs={{0,3},{1,2},{2,1},{3,0},{4,7},{5,6},{6,5},{7,4},{8,11},{9,10},{10,... | collective-permute-start | bytes 344072 | tf_op jit(solution)/shard_map/ppermute | solution.py:460
  66.9 5.2 %collective-permute-start.10 = (f32[2,7,16,128]{3,2,1,0:T(8,128)S(1)}, f32[2,7,16,128]{3,2,1,0:T(8,128)S(1)}, u32[]{:S(2)}, u32[]{:S(2)}) collective-permute-start(f32[2,7,16,128]{3,2,1,0:T(8,128)S(1)} %get-tuple-element.48), channel_id=1, source_target_pairs={{0,2},{1,3},{2,0},{3,1},{4,6},{5,7},{6,4},{7,5},{8,10},{9,11},{10,... | collective-permute-start | bytes 344072 | tf_op jit(solution)/shard_map/ppermute | solution.py:460
  67.6 4.9 %collective-permute-start.11 = (f32[2,7,16,128]{3,2,1,0:T(8,128)S(1)}, f32[2,7,16,128]{3,2,1,0:T(8,128)S(1)}, u32[]{:S(2)}, u32[]{:S(2)}) collective-permute-start(f32[2,7,16,128]{3,2,1,0:T(8,128)S(1)} %get-tuple-element.48), channel_id=1, source_target_pairs={{0,1},{1,0},{2,3},{3,2},{4,5},{5,4},{6,7},{7,6},{8,9},{9,8},{10,11... | collective-permute-start | bytes 344072 | tf_op jit(solution)/shard_map/ppermute | solution.py:460

commit v3 on v2

--- a/solution.py
+++ b/solution.py
@@ -41,34 +41,60 @@
     var[2, plane, rows] = jnp.where(place > 0, earlier, 0.0).astype(x.dtype)
 
 
-def fill_tile(tiles, w_ref, j):
+def fill_tiles(tiles, w_ref, c):
     ch = w_ref.shape[1]
     zero = jnp.zeros((ch, ch), tiles.dtype)
-    a, c = j // 3, j % 3
-    low, mid, high = (w_ref[9 * a + 3 * b + c].T for b in range(3))
-    tiles[j, 0, :ch, :ch] = mid
-    tiles[j, 0, :ch, ch:] = high
-    tiles[j, 0, ch:, :ch] = low
-    tiles[j, 0, ch:, ch:] = mid
-    tiles[j, 1, :ch, :ch] = high
-    tiles[j, 1, :ch, ch:] = zero
-    tiles[j, 1, ch:, :ch] = zero
-    tiles[j, 1, ch:, ch:] = low
-
-
-def back_planes(var, tiles, d, count):
+    taps = [[w_ref[9 * a + 3 * b + c].T for b in range(3)] for a in range(3)]
+
+    def put(at, top_left, top_right, low_left, low_right):
+        tiles[at, :ch, :ch] = top_left
+        tiles[at, :ch, ch:] = top_right
+        tiles[at, ch:, :ch] = low_left
+        tiles[at, ch:, ch:] = low_right
+
+    for a in range(3):
+        low, mid, high = taps[a]
+        put(3 * a + c, mid, high, low, mid)
+        if a != 1:
+            put(9 + 3 * (a // 2) + c, high, zero, zero, low)
+    for odd, b in ((0, 2), (1, 0)):
+        put(15 + 3 * odd + c, taps[1][b], taps[2][b], taps[0][b], taps[1][b])
+
+
+def back_planes(var, tiles, d, pairs):
     half = (var.shape[2] - 2) // 2
     width, ch = var.shape[3:]
-    flat = lambda u: u.reshape(-1, ch)
-    acc = jnp.zeros((count * half * width, 2 * ch), F32)
-    for j in range(9):
-        a, c = j // 3, j % 3
-        x = var[c, pl.ds(d + 2 - a, count)].reshape(count, half + 1, 2, width, ch)
-        inner = jnp.concatenate([flat(x[:, :half, 1]), flat(x[:, 1:, 0])], 1)
-        outer = jnp.concatenate([flat(x[:, :half, 0]), flat(x[:, 1:, 1])], 1)
-        acc += jnp.dot(inner, tiles[j, 0], preferred_element_type=F32)
-        acc += jnp.dot(outer, tiles[j, 1], preferred_element_type=F32)
-    return acc
+
+    def side_by_side(*views):
+        return jnp.concatenate([v.reshape(-1, ch) for v in views], 1)
+
+    def dot(left, at):
+        return jnp.dot(left, tiles[at], preferred_element_type=F32)
+
+    def rows(c, ahead):
+        skip = min(ahead, 1)
+        x = var[c, pl.ds(d + ahead - skip, 2 * pairs)]
+        x = x.reshape(pairs, 2, half + 1, 2, width, ch)[:, skip]
+        return x[:, :half, 0], x[:, :half, 1], x[:, 1:, 0], x[:, 1:, 1]
+
+    size = pairs * half * width
+    sums = [jnp.zeros((size, 2 * ch), F32) for _ in range(2)]
+    reach = [jnp.zeros((size, 2 * ch), F32) for _ in range(2)]
+    for c in range(3):
+        for k in range(2):
+            for a in range(3):
+                _, even, odd, _ = rows(c, k + 2 - a)
+                sums[k] += dot(side_by_side(even, odd), 3 * a + c)
+            before, _, _, after = rows(c, 3 * k)
+            sums[k] += dot(side_by_side(before, after), 9 + 3 * (1 - k) + c)
+        low, high = rows(c, 1), rows(c, 2)
+        reach[0] += dot(side_by_side(low[0], high[0]), 15 + c)
+        reach[1] += dot(side_by_side(low[3], high[3]), 18 + c)
+    shape = (pairs, half * width, 2 * ch)
+    planes = [
+        sums[k] + jnp.concatenate([r[:, k * ch : (k + 1) * ch] for r in reach], 1) for k in range(2)
+    ]
+    return jnp.stack([p.reshape(shape) for p in planes], axis=1).reshape(2 * size, 2 * ch)
 
 
 def paired(x):
@@ -81,10 +107,6 @@
     ch = v.shape[1] // 2
     parts = [v[:, i * ch : (i + 1) * ch].reshape(-1, height // 2, width, ch) for i in range(2)]
     return jnp.stack(parts, axis=2).reshape(-1, height, width, ch)
-
-
-def step_of(count):
-    return max(k for k in range(1, 5) if count % k == 0)
 
 
 def transpose_plane(dst, plane, x):
@@ -108,10 +130,17 @@
     return jnp.concatenate([x.reshape(-1, ch) for x in views], 1)
 
 
-def depth_terms(left, var, taps, depth):
+def depth_terms(left, depth, var, spans, taps):
     n = left.shape[1] // (depth + 2)
-    lefts = jnp.concatenate([left[:, a * n : (a + depth) * n] for a in range(3)], 0)
-    return jnp.dot(lefts, rights_of(var, 1, depth, taps), preferred_element_type=F32)
+    lefts = jnp.concatenate(
+        [
+            jnp.concatenate([left[:, (p + a) * n : (p + a + k) * n] for p, _, k in spans], 1)
+            for a in range(3)
+        ],
+        0,
+    )
+    rights = jnp.concatenate([rights_of(var, at, k, taps) for _, at, k in spans], 0)
+    return jnp.dot(lefts, rights, preferred_element_type=F32)
 
 
 def edge_terms(left, var, first, last, taps):
@@ -155,7 +184,7 @@
 
 def inner_kernel(
     cot_hbm, pre_hbm, vol_hbm, w_hbm, hid_hbm, part_hbm, tiles_hbm, in_t_hbm,
-    cot, pre, vol, w, var, act_t, in_t, tiles, hid, part, sems,
+    cot, pre, vol, w, var, hvar, act_t, in_t, tiles, hid, part, sems,
 ):
     depth, height, width, ch = cot.shape
     copies = [
@@ -164,13 +193,14 @@
     ]
     for c in copies:
         c.start()
+    clear_rows(hvar)
     clear_rows(var)
     edge = jnp.zeros((3,) + var.shape[2:], BF16)
     var[:, 0] = edge
     var[:, depth + 1] = edge
     clear_ends(act_t, depth)
     clear_ends(in_t, depth)
-    for c in copies:
+    for c in copies[:2]:
         c.wait()
 
     @functools.partial(loop, 0, depth)
@@ -178,37 +208,49 @@
         fill_plane(var, d + 1, cot[d])
         transpose_plane(act_t, d + 1, silu_of(pre[d]))
 
+    for c in copies[2:]:
+        c.wait()
+
     def terms(group, half):
-        r = depth_terms(act_t, var, group, depth)
-        for t in group:
-            fill_tile(tiles, w, t)
+        r = depth_terms(act_t, depth, var, [(0, 1, depth)], group)
+        fill_tiles(tiles, w, 2 if half is None else half)
         if half is not None:
             for k in range(depth // 2):
                 d = half * (depth // 2) + k
                 transpose_plane(in_t, d + 1, vol[d])
         for k, t in enumerate(group):
             for a in range(3):
-                part[9 * a + t] = r[a * ch : (a + 1) * ch, k * ch : (k + 1) * ch]
+                part[1, 9 * a + t] = r[a * ch : (a + 1) * ch, k * ch : (k + 1) * ch]
 
     grouped(terms)()
     outs = [
         pltpu.make_async_copy(a, b, sems.at[4 + i])
-        for i, (a, b) in enumerate(((tiles, tiles_hbm), (part, part_hbm), (in_t, in_t_hbm)))
+        for i, (a, b) in enumerate(
+            ((tiles, tiles_hbm), (part.at[1], part_hbm.at[1]), (in_t, in_t_hbm))
+        )
     ]
     for c in outs:
         c.start()
-    step = step_of(depth - 2)
-
-    @functools.partial(loop, 0, (depth - 2) // step)
-    def _(i):
-        d = 1 + i * step
-        grad = hidden_plane(back_planes(var, tiles, d, step), pre[pl.ds(d, step)])
-        hid[pl.ds(d - 1, step)] = unpaired(grad, height, width)
-
-    inner = hid_hbm.at[pl.ds(2, depth - 2)]
-    hid_out = pltpu.make_async_copy(hid, inner, sems.at[7])
-    hid_out.start()
-    for c in outs + [hid_out]:
+    middle = depth - 2
+    grad = hidden_plane(back_planes(var, tiles, 1, middle // 2), pre[1 : depth - 1])
+    hid[...] = unpaired(grad, height, width)
+    outs.append(pltpu.make_async_copy(hid, hid_hbm.at[pl.ds(2, middle)], sems.at[7]))
+    outs[-1].start()
+
+    @functools.partial(loop, 0, middle)
+    def _(d):
+        fill_plane(hvar, d, hid[d])
+
+    def firsts(group, _):
+        r = depth_terms(in_t, depth, hvar, [(1, 0, middle)], group)
+        for k, t in enumerate(group):
+            for a in range(3):
+                part[0, 9 * a + t] = r[a * ch : (a + 1) * ch, k * ch : (k + 1) * ch]
+
+    grouped(firsts)()
+    outs.append(pltpu.make_async_copy(part.at[0], part_hbm.at[0], sems.at[8]))
+    outs[-1].start()
+    for c in outs:
         c.wait()
 
 
@@ -217,11 +259,11 @@
 
 
 def outer_kernel(
-    ranks, taps, where_ref, far_a_hbm, far_b_hbm, cot_hbm, pre_hbm, hid_hbm, part_hbm,
-    tiles_hbm, in_t_hbm, ext_hbm, keep_hbm, send_hbm,
-    far_a, far_b, cot, pre, ext, part, tiles, cvar, hvar, act_t, in_t, keep, send, sems,
+    ranks, taps, where_ref, far_a_hbm, far_b_hbm, cot_hbm, pre_hbm, part_hbm,
+    tiles_hbm, in_t_hbm, rim_hbm, keep_hbm, send_hbm,
+    far_a, far_b, cot, pre, rim, part, tiles, cvar, hvar, act_t, in_t, keep, send, sems,
 ):
-    depth, height, width, ch = ext.shape[0] - 2, *ext.shape[1:]
+    depth, height, width, ch = cot_hbm.shape
     code = where_ref[0]
     even, core = bit(code, 0) == 0, bit(code, 1)
     pairs = (
@@ -229,8 +271,7 @@
         (cot_hbm.at[pl.ds(0, 2)], cot.at[pl.ds(0, 2)]),
         (cot_hbm.at[pl.ds(depth - 2, 2)], cot.at[pl.ds(2, 2)]),
         (pre_hbm.at[0], pre.at[1]), (pre_hbm.at[depth - 1], pre.at[2]),
-        (tiles_hbm, tiles), (hid_hbm.at[pl.ds(2, depth - 2)], ext.at[pl.ds(2, depth - 2)]),
-        (part_hbm, part), (in_t_hbm, in_t),
+        (tiles_hbm, tiles), (part_hbm.at[1], part.at[1]), (in_t_hbm, in_t), (part_hbm.at[0], part.at[0]),
     )
     copies = [pltpu.make_async_copy(a, b, sems.at[i]) for i, (a, b) in enumerate(pairs)]
     for c in copies:
@@ -248,32 +289,27 @@
     pre[0] = jnp.where(even, far_b[2], far_a[2])
     pre[3] = jnp.where(even, far_a[2], far_b[2])
     copies[6].wait()
-    copies[7].wait()
-    inner = depth - 2
     for late in range(2):
-        back = back_planes(cvar, tiles, 4 * late, 2)
-        for d in range(inner // 2 * late, inner if late else inner // 2):
-            fill_plane(hvar, 2 + d, ext[2 + d])
+        back = back_planes(cvar, tiles, 4 * late, 1)
         grad = hidden_plane(back, pre[2 * late : 2 * late + 2])
         planes = unpaired(grad, height, width)
         there = bit(code, 2 + late) == 1
         outside = jnp.where(there, planes[late].astype(F32), 0.0).astype(BF16)
-        ext[depth * late + late] = outside
-        fill_plane(hvar, depth * late + late, outside)
-        ext[(depth - 1) * late + 1] = planes[1 - late]
-        fill_plane(hvar, (depth - 1) * late + 1, planes[1 - late])
-
-    ext_out = pltpu.make_async_copy(ext, ext_hbm, sems.at[10])
-    ext_out.start()
-    copies[8].wait()
+        for at, value in ((3 * late, outside), (1 + late, planes[1 - late])):
+            rim[at] = value
+            fill_plane(hvar, at, value)
+
+    rim_out = pltpu.make_async_copy(rim, rim_hbm.at[pl.ds(0, 4)], sems.at[10])
+    rim_out.start()
+    copies[7].wait()
 
     def seconds(group, _):
         low, high = edge_terms(act_t, cvar, 1, 6, group)
         for k, t in enumerate(group):
             cols = slice(k * ch, (k + 1) * ch)
-            store_tap(keep, send, 1, core, t, part[t] + high[:, cols], ranks)
-            store_tap(keep, send, 1, core, 9 + t, part[9 + t], ranks)
-            store_tap(keep, send, 1, core, 18 + t, part[18 + t] + low[:, cols], ranks)
+            store_tap(keep, send, 1, core, t, part[1, t] + high[:, cols], ranks)
+            store_tap(keep, send, 1, core, 9 + t, part[1, 9 + t], ranks)
+            store_tap(keep, send, 1, core, 18 + t, part[1, 18 + t] + low[:, cols], ranks)
 
     grouped(seconds)()
     for t in range(taps, keep.shape[1]):
@@ -288,14 +324,16 @@
         c.start()
 
     def firsts(group, _):
-        r = depth_terms(in_t, hvar, group, depth)
-        low, high = edge_terms(in_t, hvar, 0, depth + 1, group)
+        r = depth_terms(in_t, depth, hvar, [(0, 1, 1), (depth - 1, 2, 1)], group)
+        low, high = edge_terms(in_t, hvar, 0, 3, group)
         for k, t in enumerate(group):
             cols = slice(k * ch, (k + 1) * ch)
-            store_tap(keep, send, 0, core, t, r[:ch, cols] + high[:, cols], ranks)
-            store_tap(keep, send, 0, core, 9 + t, r[ch : 2 * ch, cols], ranks)
-            store_tap(keep, send, 0, core, 18 + t, r[2 * ch :, cols] + low[:, cols], ranks)
-
+            sums = [r[a * ch : (a + 1) * ch, cols] + part[0, 9 * a + t] for a in range(3)]
+            store_tap(keep, send, 0, core, t, sums[0] + high[:, cols], ranks)
+            store_tap(keep, send, 0, core, 9 + t, sums[1], ranks)
+            store_tap(keep, send, 0, core, 18 + t, sums[2] + low[:, cols], ranks)
+
+    copies[8].wait()
     copies[9].wait()
     finish = grouped(firsts)
 
@@ -315,7 +353,7 @@
     finish()
     for a in range(3):
         outs += leave(9 * a + 8, 1 if a < 2 else keep.shape[1] - 26, 19 + 2 * a)
-    ext_out.wait()
+    rim_out.wait()
     for c in outs:
         c.wait()
 
@@ -325,33 +363,38 @@
     return (v * sigmoid(v)).astype(BF16)
 
 
-def input_kernel(ext_hbm, w_hbm, out_hbm, ext, w, tiles, out, var, sems):
+def input_kernel(hid_hbm, rim_hbm, w_hbm, out_hbm, ext, w, tiles, out, var, sems):
     depth, height, width, _ = out.shape
     copies = [
         pltpu.make_async_copy(a, b, sems.at[i])
-        for i, (a, b) in enumerate(((w_hbm, w), (ext_hbm, ext)))
+        for i, (a, b) in enumerate(
+            (
+                (w_hbm, w),
+                (rim_hbm.at[pl.ds(0, 2)], ext.at[pl.ds(0, 2)]),
+                (hid_hbm.at[pl.ds(2, depth - 2)], ext.at[pl.ds(2, depth - 2)]),
+                (rim_hbm.at[pl.ds(2, 2)], ext.at[pl.ds(depth, 2)]),
+            )
+        )
     ]
     for c in copies:
         c.start()
     clear_rows(var)
-    copies[0].wait()
-    loop(0, 9, functools.partial(fill_tile, tiles, w))
-    copies[1].wait()
-
-    @functools.partial(loop, 0, depth + 2)
-    def _(d):
-        fill_plane(var, d, ext[d])
-
-    step = step_of(depth)
-
-    @functools.partial(loop, 0, depth // step)
-    def _(i):
-        grad = back_planes(var, tiles, i * step, step).astype(BF16)
-        out[pl.ds(i * step, step)] = unpaired(grad, height, width)
-
-    c = pltpu.make_async_copy(out, out_hbm, sems.at[2])
-    c.start()
-    c.wait()
+    for c in copies:
+        c.wait()
+    for c in range(3):
+        fill_tiles(tiles, w, c)
+        for d in range(c, depth + 2, 3):
+            fill_plane(var, d, ext[d])
+    step = depth // 2 if depth % 4 == 0 else depth
+    outs = []
+    for i in range(depth // step):
+        grad = back_planes(var, tiles, i * step, step // 2).astype(BF16)
+        part = pl.ds(i * step, step)
+        out[part] = unpaired(grad, height, width)
+        outs.append(pltpu.make_async_copy(out.at[part], out_hbm.at[part], sems.at[4 + i]))
+        outs[-1].start()
+    for c in outs:
+        c.wait()
 
 
 def call(body, out_shape, operands, scratch, sems, flops, n_smem=0, limit=LIMIT, n_any=0):
@@ -479,9 +522,9 @@
     plane = (height, width, ch)
     many = lambda k: ((k,) + plane, BF16)
     shifted = lambda k: ((3, k, height + 2, width, ch), BF16)
-    tiles_of = ((9, 2, 2 * ch, 2 * ch), BF16)
+    tiles_of = ((21, 2 * ch, 2 * ch), BF16)
     weights_of = (weight_one.shape, BF16)
-    part_of = ((taps, ch, ch), F32)
+    part_of = ((2, taps, ch, ch), F32)
     keep_of = ((2, padded_taps, ch // 2, ch), F32)
     send_of = (keep_of[0], BF16)
 
@@ -491,25 +534,25 @@
         inner_kernel,
         (s(*many(depth + 2)), s(*part_of), s(*tiles_of), s(*turned)),
         (cot, pre, volume_in, weight_two),
-        [many(depth), many(depth), many(depth), weights_of, shifted(depth + 2), turned, turned,
+        [many(depth), many(depth), many(depth), weights_of, shifted(depth + 2), shifted(depth - 2), turned, turned,
          tiles_of, many(depth - 2), part_of],
-        8, 2 * sweep,
-    )
-    ext, keep, send = call(
+        9, 3 * sweep,
+    )
+    rim, keep, send = call(
         functools.partial(outer_kernel, ranks, taps),
         (s(*many(depth + 2)), s(*keep_of), s(*send_of)),
-        (where, far_a, far_b, cot, pre, hid, part, tiles2, in_t),
-        [many(3), many(3), many(4), many(4), many(depth + 2), part_of, tiles_of,
-         shifted(8), shifted(depth + 2), ((ch, 4 * n), BF16), turned, keep_of, send_of],
-        25, 3 * sweep // 2, 1, OUTER_LIMIT, 2,
+        (where, far_a, far_b, cot, pre, part, tiles2, in_t),
+        [many(3), many(3), many(4), many(4), many(4), part_of, tiles_of,
+         shifted(8), shifted(4), ((ch, 4 * n), BF16), turned, keep_of, send_of],
+        25, sweep, 1, OUTER_LIMIT, 2,
     )
     got = swap_cores(send)
     mine, others = slab_pieces(keep, got)
-    ext, weight_one, mine, *others = lax.optimization_barrier((ext, weight_one, mine, *others))
+    rim, weight_one, mine, *others = lax.optimization_barrier((rim, weight_one, mine, *others))
     arrived = trade_slab(others)
     input_grad = call(
-        input_kernel, s(*many(depth)), (ext, weight_one),
-        [many(depth + 2), weights_of, tiles_of, many(depth), shifted(depth + 2)], 3, sweep,
+        input_kernel, s(*many(depth)), (hid, rim, weight_one),
+        [many(depth + 2), weights_of, tiles_of, many(depth), shifted(depth + 2)], 6, sweep,
     )
     input_grad, *arrived = lax.optimization_barrier((input_grad, *arrived))
     for x in arrived:

time: 73.6 us -> 72.5 us (0.985)
  waiting for transfers between devices: 11.8 us -> 15.3 us
  Pallas kernels: 38.6 us -> 35.8 us
  starting transfers between devices: 19.3 us -> 17.5 us
    pallas_call x3, Pallas kernels: 36.6 us -> 33.8 us  [call(): pl.pallas_call(body, out_shape=out_shape, in_specs=[SMEM] * n_smem + [ANY...]
    ppermute x3, waiting for transfers between devices: 0.41 us -> 2.54 us  [trade_slab(): lax.ppermute(x, 'slab', [(i, partner(i, k, peers)) for i in range(peers)])]
    ppermute x3, starting transfers between devices: 7.42 us -> 5.73 us  [trade_slab(): lax.ppermute(x, 'slab', [(i, partner(i, k, peers)) for i in range(peers)])]
    ppermute x3, waiting for transfers between devices: 4.44 us -> 5.94 us  [scatter_ranks(): out = out + lax.ppermute(x, 'rep', perm).astype(F32)]
  transfers between devices with their start and end apart: 12 -> 12, of which waited for: 7 -> 8; matrix products, arithmetic and copies ran while one was open for 0% -> 0% of each run, Pallas kernels for 31% -> 33%
where the time goes in v3:
time: 72.5 us; the launch traced here: 72.3 us
  Pallas kernels  35.8 us (49%)
  starting transfers between devices  17.5 us (24%)
  waiting for transfers between devices  15.3 us (21%)
  other arithmetic  1.86 us (3%)
  local copies, waits for them, and re-layouts  0.89 us (1%)
  between operations  0.84 us (1%)
    pallas_call x3, Pallas kernels, call(): pl.pallas_call(body, out_shape=out_shape, in_specs=[SMEM] * n_smem + [ANY...  33.8 us
    ppermute x3, waiting for transfers between devices, scatter_ranks(): out = out + lax.ppermute(x, 'rep', perm).astype(F32)  5.94 us
    ppermute x3, starting transfers between devices, trade_slab(): lax.ppermute(x, 'slab', [(i, partner(i, k, peers)) for i in range(peers)])  5.73 us
    ppermute x3, starting transfers between devices, scatter_ranks(): out = out + lax.ppermute(x, 'rep', perm).astype(F32)  4.45 us
    ppermute x3, waiting for transfers between devices, gather_slab(): got = lax.ppermute(part, 'slab', perm)  4.44 us
    ppermute x2, starting transfers between devices, swap_faces(): return (lax.ppermute(to_a, 'slab', a), lax.ppermute(to_b, 'slab', b))  3.71 us
    ppermute x3, starting transfers between devices, gather_slab(): got = lax.ppermute(part, 'slab', perm)  3.55 us
    ppermute x3, waiting for transfers between devices, trade_slab(): lax.ppermute(x, 'slab', [(i, partner(i, k, peers)) for i in range(peers)])  2.54 us
  transfers between devices with their start and end apart: 12, of which 8 were waited for; matrix products, arithmetic and copies ran while one was open for 0% of the time, Pallas kernels for 33%

profile of v3, /device:TPU:0, one launch (start us, length us, event | category | flops | bytes accessed | tf_op | source)
XLA Modules:
  0.0 72.3 jit_solution(10112542451230913804)
XLA Ops:
  0.7 2.1 %shard_map.77 = (bf16[3,32,16,128]{3,2,1,0:T(8,128)(2,1)}, bf16[3,32,16,128]{3,2,1,0:T(8,128)(2,1)}) custom-call(s32[1]{0:T(128)} %bitcast.3.where_ref, bf16[8,32,16,128]{3,2,1,0:T(8,128)(2,1)} %bitcast.9, bf16[8,32,16,128]{3,2,1,0:T(8,128)(2,1)} %bitcast.12), custom_call_target="tpu_custom_call" | custom-call | tf_op jit(solution)/shard_map/pallas_call | solution.py:445
  2.7 3.0 %collective-permute-start = (bf16[3,32,16,128]{3,2,1,0:T(8,128)(2,1)}, bf16[3,32,16,128]{3,2,1,0:T(8,128)(2,1)S(1)}, u32[]{:S(2)}, u32[]{:S(2)}) collective-permute-start(bf16[3,32,16,128]{3,2,1,0:T(8,128)(2,1)} %get-tuple-element.26), channel_id=1, source_target_pairs={{0,1},{1,0},{2,3},{3,2},{4,5},{5,4},{6,7},{7,6},{8,9},{9,8},{10,11... | collective-permute-start | bytes 1179656 | tf_op jit(solution)/shard_map/ppermute | solution.py:453
  5.8 0.7 collective-permute-start.1
  6.4 16.9 %shard_map.76 = (bf16[10,32,16,128]{3,2,1,0:T(8,128)(2,1)}, f32[2,27,128,128]{3,2,1,0:T(8,128)}, bf16[21,256,256]{2,1,0:T(8,128)(2,1)}, bf16[128,5120]{1,0:T(8,128)(2,1)}) custom-call(bf16[8,32,16,128]{3,2,1,0:T(8,128)(2,1)} %bitcast.10, bf16[8,32,16,128]{3,2,1,0:T(8,128)(2,1)} %bitcast.13, bf16[8,32,16,128]{3,2,1,0:T(8,128)(2,1)} %bitcast.15, ...), custom_call_target="tpu_custom_call" | custom-call | flops 10871635968 | bytes 4030464 | tf_op jit(solution)/shard_map/pallas_call | solution.py:402
  23.3 0.0 collective-permute-done.far_a_hbm
  23.3 0.0 collective-permute-done.1.far_b_hbm
  23.4 10.0 %shard_map.78 = (bf16[10,32,16,128]{3,2,1,0:T(8,128)(2,1)}, f32[2,28,64,128]{3,2,1,0:T(8,128)}, bf16[2,28,64,128]{3,2,1,0:T(8,128)(2,1)S(1)}) custom-call(s32[1]{0:T(128)} %bitcast.3.where_ref, bf16[3,32,16,128]{3,2,1,0:T(8,128)(2,1)S(1)} %collective-permute-done.far_a_hbm, bf16[3,32,16,128]{3,2,1,0:T(8,128)(2,1)S(1)} %collective-permute-done.1.far_b_hbm, ...), custom_call_target="tpu_custom_call" | custom-call | flops 3623878656 | bytes 10485764 | tf_op jit(solution)/shard_map/pallas_call | solution.py:402
  33.4 0.1 collective-permute-start.2
  33.5 2.4 %collective-permute-done.2 = bf16[2,28,64,128]{3,2,1,0:T(8,128)(2,1)S(1)} collective-permute-done((bf16[2,28,64,128]{3,2,1,0:T(8,128)(2,1)S(1)}, bf16[2,28,64,128]{3,2,1,0:T(8,128)(2,1)S(1)}, u32[]{:S(2)}, u32[]{:S(2)}) %collective-permute-start.2) | collective-permute-done | bytes 917536 | tf_op jit(solution)/shard_map/ppermute | solution.py:458
  35.9 1.7 %add_convert_fusion = (bf16[2,7,64,128]{3,2,1,0:T(8,128)(2,1)S(1)}, bf16[2,7,64,128]{3,2,1,0:T(8,128)(2,1)S(1)}, bf16[2,7,64,128]{3,2,1,0:T(8,128)(2,1)S(1)}, f32[2,7,64,128]{3,2,1,0:T(8,128)S(1)}) fusion(f32[2,28,64,128]{3,2,1,0:T(8,128)} %get-tuple-element.32, s32[]{:T(128)S(6)} %select_n.55, bf16[2,28,64,128]{3,2,1,0:T(8,128)(2,1)S(1)} %collective-permute-done.2, ...), kind=kLoop, calls=%fused_computation.1 | loop fusion | flops 1261568 | bytes 3899408 | tf_op jit(solution)/shard_map/convert_element_type | solution.py:469
  37.7 1.6 %collective-permute-start.3 = (bf16[2,7,64,128]{3,2,1,0:T(8,128)(2,1)S(1)}, bf16[2,7,64,128]{3,2,1,0:T(8,128)(2,1)S(1)}, u32[]{:S(2)}, u32[]{:S(2)}) collective-permute-start(bf16[2,7,64,128]{3,2,1,0:T(8,128)(2,1)S(1)} %get-tuple-element.36), channel_id=1, source_target_pairs={{0,3},{1,2},{2,1},{3,0},{4,7},{5,6},{6,5},{7,4},{8,11},{9,10},{10,... | collective-permute-start | bytes 688136 | tf_op jit(solution)/shard_map/ppermute | solution.py:476
  39.2 4.2 %collective-permute-start.4 = (bf16[2,7,64,128]{3,2,1,0:T(8,128)(2,1)S(1)}, bf16[2,7,64,128]{3,2,1,0:T(8,128)(2,1)S(1)}, u32[]{:S(2)}, u32[]{:S(2)}) collective-permute-start(bf16[2,7,64,128]{3,2,1,0:T(8,128)(2,1)S(1)} %get-tuple-element.37), channel_id=1, source_target_pairs={{0,2},{1,3},{2,0},{3,1},{4,6},{5,7},{6,4},{7,5},{8,10},{9,11},{10,... | collective-permute-start | bytes 688136 | tf_op jit(solution)/shard_map/ppermute | solution.py:476
  43.4 0.0 collective-permute-start.5
  43.4 6.8 %shard_map.79 = bf16[8,32,16,128]{3,2,1,0:T(8,128)(2,1)} custom-call(bf16[10,32,16,128]{3,2,1,0:T(8,128)(2,1)} %get-tuple-element.25.hid_hbm, bf16[10,32,16,128]{3,2,1,0:T(8,128)(2,1)} %get-tuple-element.34.rim_hbm, bf16[27,128,128]{2,1,0:T(8,128)(2,1)} %w_hbm.2), custom_call_target="tpu_custom_call" | custom-call | flops 3623878656 | bytes 3506176 | tf_op jit(solution)/shard_map/pallas_call | solution.py:402
  50.2 0.0 collective-permute-done.3
  50.2 1.5 %collective-permute-done.4 = bf16[2,7,64,128]{3,2,1,0:T(8,128)(2,1)S(1)} collective-permute-done((bf16[2,7,64,128]{3,2,1,0:T(8,128)(2,1)S(1)}, bf16[2,7,64,128]{3,2,1,0:T(8,128)(2,1)S(1)}, u32[]{:S(2)}, u32[]{:S(2)}) %collective-permute-start.4) | collective-permute-done | bytes 229408 | tf_op jit(solution)/shard_map/ppermute | solution.py:476
  51.7 1.1 %collective-permute-done.5 = bf16[2,7,64,128]{3,2,1,0:T(8,128)(2,1)S(1)} collective-permute-done((bf16[2,7,64,128]{3,2,1,0:T(8,128)(2,1)S(1)}, bf16[2,7,64,128]{3,2,1,0:T(8,128)(2,1)S(1)}, u32[]{:S(2)}, u32[]{:S(2)}) %collective-permute-start.5) | collective-permute-done | bytes 229408 | tf_op jit(solution)/shard_map/ppermute | solution.py:476
  52.8 0.1 convert_add_fusion
  52.9 1.8 %collective-permute-start.8 = (bf16[2,7,16,128]{3,2,1,0:T(8,128)(2,1)S(1)}, bf16[2,7,16,128]{3,2,1,0:T(8,128)(2,1)S(1)}, u32[]{:S(2)}, u32[]{:S(2)}) collective-permute-start(bf16[2,7,16,128]{3,2,1,0:T(8,128)(2,1)S(1)} %get-tuple-element.46), channel_id=1, source_target_pairs={{0,8},{4,12},{8,0},{12,4},{16,24},{20,28},{24,16},{28,20},{1,9},{5... | collective-permute-start | bytes 172040 | tf_op jit(solution)/shard_map/ppermute | solution.py:492
  54.8 2.6 %collective-permute-start.7 = (bf16[2,7,16,128]{3,2,1,0:T(8,128)(2,1)S(1)}, bf16[2,7,16,128]{3,2,1,0:T(8,128)(2,1)S(1)}, u32[]{:S(2)}, u32[]{:S(2)}) collective-permute-start(bf16[2,7,16,128]{3,2,1,0:T(8,128)(2,1)S(1)} %get-tuple-element.45), channel_id=1, source_target_pairs={{0,16},{4,20},{8,24},{12,28},{16,0},{20,4},{24,8},{28,12},{1,17},{... | collective-permute-start | bytes 172040 | tf_op jit(solution)/shard_map/ppermute | solution.py:492
  57.4 0.0 collective-permute-start.6
  57.4 0.0 collective-permute-done.8
  57.4 3.1 %collective-permute-done.7 = bf16[2,7,16,128]{3,2,1,0:T(8,128)(2,1)S(1)} collective-permute-done((bf16[2,7,16,128]{3,2,1,0:T(8,128)(2,1)S(1)}, bf16[2,7,16,128]{3,2,1,0:T(8,128)(2,1)S(1)}, u32[]{:S(2)}, u32[]{:S(2)}) %collective-permute-start.7) | collective-permute-done | bytes 57376 | tf_op jit(solution)/shard_map/ppermute | solution.py:492
  60.5 2.9 %collective-permute-done.6 = bf16[2,7,16,128]{3,2,1,0:T(8,128)(2,1)S(1)} collective-permute-done((bf16[2,7,16,128]{3,2,1,0:T(8,128)(2,1)S(1)}, bf16[2,7,16,128]{3,2,1,0:T(8,128)(2,1)S(1)}, u32[]{:S(2)}, u32[]{:S(2)}) %collective-permute-start.6) | collective-permute-done | bytes 57376 | tf_op jit(solution)/shard_map/ppermute | solution.py:492
  63.4 2.5 %collective-permute-start.9 = (f32[2,7,16,128]{3,2,1,0:T(8,128)S(1)}, f32[2,7,16,128]{3,2,1,0:T(8,128)S(1)}, u32[]{:S(2)}, u32[]{:S(2)}) collective-permute-start(f32[2,7,16,128]{3,2,1,0:T(8,128)S(1)} %get-tuple-element.48), channel_id=1, source_target_pairs={{0,3},{1,2},{2,1},{3,0},{4,7},{5,6},{6,5},{7,4},{8,11},{9,10},{10,... | collective-permute-start | bytes 344072 | tf_op jit(solution)/shard_map/ppermute | solution.py:503
  65.9 0.7 collective-permute-start.10
  66.7 0.3 collective-permute-start.11
  67.0 2.5 %collective-permute-done.9 = f32[2,7,16,128]{3,2,1,0:T(8,128)S(1)} collective-permute-done((f32[2,7,16,128]{3,2,1,0:T(8,128)S(1)}, f32[2,7,16,128]{3,2,1,0:T(8,128)S(1)}, u32[]{:S(2)}, u32[]{:S(2)}) %collective-permute-start.9) | collective-permute-done | bytes 114720 | tf_op jit(solution)/shard_map/ppermute | solution.py:503
  69.5 1.3 %collective-permute-done.10 = f32[2,7,16,128]{3,2,1,0:T(8,128)S(1)} collective-permute-done((f32[2,7,16,128]{3,2,1,0:T(8,128)S(1)}, f32[2,7,16,128]{3,2,1,0:T(8,128)S(1)}, u32[]{:S(2)}, u32[]{:S(2)}) %collective-permute-start.10) | collective-permute-done | bytes 114720 | tf_op jit(solution)/shard_map/ppermute | solution.py:503
  70.8 0.7 collective-permute-done.11
  71.5 0.8 %slice_bitcast_fusion = (f32[27,16,128]{2,1,0:T(8,128)}, f32[27,16,128]{2,1,0:T(8,128)}) fusion(f32[2,28,16,128]{3,2,1,0:T(8,128)S(1)} %constant_dynamic-update-slice_fusion), kind=kLoop, calls=%fused_computation.5 | loop fusion | bytes 884736 | tf_op jit(solution)/shard_map/squeeze | solution.py:563
  (6 shorter events, 0.1 us)
Async XLA Ops:
  2.7 20.6 %collective-permute-start = (bf16[3,32,16,128]{3,2,1,0:T(8,128)(2,1)}, bf16[3,32,16,128]{3,2,1,0:T(8,128)(2,1)S(1)}, u32[]{:S(2)}, u32[]{:S(2)}) collective-permute-start(bf16[3,32,16,128]{3,2,1,0:T(8,128)(2,1)} %get-tuple-element.26), channel_id=1, source_target_pairs={{0,1},{1,0},{2,3},{3,2},{4,5},{5,4},{6,7},{7,6},{8,9},{9,8},{10,11... | collective-permute-start | bytes 1179656 | tf_op jit(solution)/shard_map/ppermute | solution.py:453
  5.8 17.6 %collective-permute-start.1 = (bf16[3,32,16,128]{3,2,1,0:T(8,128)(2,1)}, bf16[3,32,16,128]{3,2,1,0:T(8,128)(2,1)S(1)}, u32[]{:S(2)}, u32[]{:S(2)}) collective-permute-start(bf16[3,32,16,128]{3,2,1,0:T(8,128)(2,1)} %get-tuple-element.27), channel_id=1, source_target_pairs={{1,2},{2,1},{5,6},{6,5},{9,10},{10,9},{13,14},{14,13},{17,18},{18,... | collective-permute-start | bytes 1179656 | tf_op jit(solution)/shard_map/ppermute | solution.py:453
  33.4 2.5 %collective-permute-start.2 = (bf16[2,28,64,128]{3,2,1,0:T(8,128)(2,1)S(1)}, bf16[2,28,64,128]{3,2,1,0:T(8,128)(2,1)S(1)}, u32[]{:S(2)}, u32[]{:S(2)}) collective-permute-start(bf16[2,28,64,128]{3,2,1,0:T(8,128)(2,1)S(1)} %get-tuple-element.33), channel_id=1, source_target_pairs={{0,4},{4,0},{8,12},{12,8},{16,20},{20,16},{24,28},{28,24},{1,5},{5... | collective-permute-start | bytes 2752520 | tf_op jit(solution)/shard_map/ppermute | solution.py:458
  37.7 12.6 %collective-permute-start.3 = (bf16[2,7,64,128]{3,2,1,0:T(8,128)(2,1)S(1)}, bf16[2,7,64,128]{3,2,1,0:T(8,128)(2,1)S(1)}, u32[]{:S(2)}, u32[]{:S(2)}) collective-permute-start(bf16[2,7,64,128]{3,2,1,0:T(8,128)(2,1)S(1)} %get-tuple-element.36), channel_id=1, source_target_pairs={{0,3},{1,2},{2,1},{3,0},{4,7},{5,6},{6,5},{7,4},{8,11},{9,10},{10,... | collective-permute-start | bytes 688136 | tf_op jit(solution)/shard_map/ppermute | solution.py:476
  39.2 12.5 %collective-permute-start.4 = (bf16[2,7,64,128]{3,2,1,0:T(8,128)(2,1)S(1)}, bf16[2,7,64,128]{3,2,1,0:T(8,128)(2,1)S(1)}, u32[]{:S(2)}, u32[]{:S(2)}) collective-permute-start(bf16[2,7,64,128]{3,2,1,0:T(8,128)(2,1)S(1)} %get-tuple-element.37), channel_id=1, source_target_pairs={{0,2},{1,3},{2,0},{3,1},{4,6},{5,7},{6,4},{7,5},{8,10},{9,11},{10,... | collective-permute-start | bytes 688136 | tf_op jit(solution)/shard_map/ppermute | solution.py:476
  43.4 9.4 %collective-permute-start.5 = (bf16[2,7,64,128]{3,2,1,0:T(8,128)(2,1)S(1)}, bf16[2,7,64,128]{3,2,1,0:T(8,128)(2,1)S(1)}, u32[]{:S(2)}, u32[]{:S(2)}) collective-permute-start(bf16[2,7,64,128]{3,2,1,0:T(8,128)(2,1)S(1)} %get-tuple-element.38), channel_id=1, source_target_pairs={{0,1},{1,0},{2,3},{3,2},{4,5},{5,4},{6,7},{7,6},{8,9},{9,8},{10,11... | collective-permute-start | bytes 688136 | tf_op jit(solution)/shard_map/ppermute | solution.py:476
  52.9 4.5 %collective-permute-start.8 = (bf16[2,7,16,128]{3,2,1,0:T(8,128)(2,1)S(1)}, bf16[2,7,16,128]{3,2,1,0:T(8,128)(2,1)S(1)}, u32[]{:S(2)}, u32[]{:S(2)}) collective-permute-start(bf16[2,7,16,128]{3,2,1,0:T(8,128)(2,1)S(1)} %get-tuple-element.46), channel_id=1, source_target_pairs={{0,8},{4,12},{8,0},{12,4},{16,24},{20,28},{24,16},{28,20},{1,9},{5... | collective-permute-start | bytes 172040 | tf_op jit(solution)/shard_map/ppermute | solution.py:492
  54.8 5.7 %collective-permute-start.7 = (bf16[2,7,16,128]{3,2,1,0:T(8,128)(2,1)S(1)}, bf16[2,7,16,128]{3,2,1,0:T(8,128)(2,1)S(1)}, u32[]{:S(2)}, u32[]{:S(2)}) collective-permute-start(bf16[2,7,16,128]{3,2,1,0:T(8,128)(2,1)S(1)} %get-tuple-element.45), channel_id=1, source_target_pairs={{0,16},{4,20},{8,24},{12,28},{16,0},{20,4},{24,8},{28,12},{1,17},{... | collective-permute-start | bytes 172040 | tf_op jit(solution)/shard_map/ppermute | solution.py:492
  57.4 6.0 %collective-permute-start.6 = (bf16[2,7,16,128]{3,2,1,0:T(8,128)(2,1)S(1)}, bf16[2,7,16,128]{3,2,1,0:T(8,128)(2,1)S(1)}, u32[]{:S(2)}, u32[]{:S(2)}) collective-permute-start(bf16[2,7,16,128]{3,2,1,0:T(8,128)(2,1)S(1)} %get-tuple-element.44), channel_id=1, source_target_pairs={{0,24},{4,28},{8,16},{12,20},{16,8},{20,12},{24,0},{28,4},{1,25},{... | collective-permute-start | bytes 172040 | tf_op jit(solution)/shard_map/ppermute | solution.py:492
  63.4 6.0 %collective-permute-start.9 = (f32[2,7,16,128]{3,2,1,0:T(8,128)S(1)}, f32[2,7,16,128]{3,2,1,0:T(8,128)S(1)}, u32[]{:S(2)}, u32[]{:S(2)}) collective-permute-start(f32[2,7,16,128]{3,2,1,0:T(8,128)S(1)} %get-tuple-element.48), channel_id=1, source_target_pairs={{0,3},{1,2},{2,1},{3,0},{4,7},{5,6},{6,5},{7,4},{8,11},{9,10},{10,... | collective-permute-start | bytes 344072 | tf_op jit(solution)/shard_map/ppermute | solution.py:503
  65.9 4.8 %collective-permute-start.10 = (f32[2,7,16,128]{3,2,1,0:T(8,128)S(1)}, f32[2,7,16,128]{3,2,1,0:T(8,128)S(1)}, u32[]{:S(2)}, u32[]{:S(2)}) collective-permute-start(f32[2,7,16,128]{3,2,1,0:T(8,128)S(1)} %get-tuple-element.48), channel_id=1, source_target_pairs={{0,2},{1,3},{2,0},{3,1},{4,6},{5,7},{6,4},{7,5},{8,10},{9,11},{10,... | collective-permute-start | bytes 344072 | tf_op jit(solution)/shard_map/ppermute | solution.py:503
  66.7 4.8 %collective-permute-start.11 = (f32[2,7,16,128]{3,2,1,0:T(8,128)S(1)}, f32[2,7,16,128]{3,2,1,0:T(8,128)S(1)}, u32[]{:S(2)}, u32[]{:S(2)}) collective-permute-start(f32[2,7,16,128]{3,2,1,0:T(8,128)S(1)} %get-tuple-element.48), channel_id=1, source_target_pairs={{0,1},{1,0},{2,3},{3,2},{4,5},{5,4},{6,7},{7,6},{8,9},{9,8},{10,11... | collective-permute-start | bytes 344072 | tf_op jit(solution)/shard_map/ppermute | solution.py:503

commit v4 on v3

--- a/solution.py
+++ b/solution.py
@@ -187,9 +187,15 @@
     cot, pre, vol, w, var, hvar, act_t, in_t, tiles, hid, part, sems,
 ):
     depth, height, width, ch = cot.shape
+    half = depth // 2
+    pieces = [
+        (a.at[pl.ds(k * half, half)], b.at[pl.ds(k * half, half)])
+        for k in range(2)
+        for a, b in ((cot_hbm, cot), (pre_hbm, pre))
+    ]
     copies = [
         pltpu.make_async_copy(a, b, sems.at[i])
-        for i, (a, b) in enumerate(((cot_hbm, cot), (pre_hbm, pre), (w_hbm, w), (vol_hbm, vol)))
+        for i, (a, b) in enumerate(pieces + [(w_hbm, w), (vol_hbm, vol)])
     ]
     for c in copies:
         c.start()
@@ -200,23 +206,24 @@
     var[:, depth + 1] = edge
     clear_ends(act_t, depth)
     clear_ends(in_t, depth)
-    for c in copies[:2]:
-        c.wait()
-
-    @functools.partial(loop, 0, depth)
-    def _(d):
-        fill_plane(var, d + 1, cot[d])
-        transpose_plane(act_t, d + 1, silu_of(pre[d]))
-
-    for c in copies[2:]:
-        c.wait()
-
-    def terms(group, half):
+    for k in range(2):
+        for c in copies[2 * k : 2 * k + 2]:
+            c.wait()
+
+        @functools.partial(loop, k * half, (k + 1) * half)
+        def _(d):
+            fill_plane(var, d + 1, cot[d])
+            transpose_plane(act_t, d + 1, silu_of(pre[d]))
+
+    for c in copies[4:]:
+        c.wait()
+
+    def terms(group, step):
         r = depth_terms(act_t, depth, var, [(0, 1, depth)], group)
-        fill_tiles(tiles, w, 2 if half is None else half)
-        if half is not None:
-            for k in range(depth // 2):
-                d = half * (depth // 2) + k
+        fill_tiles(tiles, w, 2 if step is None else step)
+        if step is not None:
+            for k in range(half):
+                d = step * half + k
                 transpose_plane(in_t, d + 1, vol[d])
         for k, t in enumerate(group):
             for a in range(3):
@@ -224,7 +231,7 @@
 
     grouped(terms)()
     outs = [
-        pltpu.make_async_copy(a, b, sems.at[4 + i])
+        pltpu.make_async_copy(a, b, sems.at[6 + i])
         for i, (a, b) in enumerate(
             ((tiles, tiles_hbm), (part.at[1], part_hbm.at[1]), (in_t, in_t_hbm))
         )
@@ -234,7 +241,7 @@
     middle = depth - 2
     grad = hidden_plane(back_planes(var, tiles, 1, middle // 2), pre[1 : depth - 1])
     hid[...] = unpaired(grad, height, width)
-    outs.append(pltpu.make_async_copy(hid, hid_hbm.at[pl.ds(2, middle)], sems.at[7]))
+    outs.append(pltpu.make_async_copy(hid, hid_hbm.at[pl.ds(2, middle)], sems.at[9]))
     outs[-1].start()
 
     @functools.partial(loop, 0, middle)
@@ -247,9 +254,17 @@
             for a in range(3):
                 part[0, 9 * a + t] = r[a * ch : (a + 1) * ch, k * ch : (k + 1) * ch]
 
-    grouped(firsts)()
-    outs.append(pltpu.make_async_copy(part.at[0], part_hbm.at[0], sems.at[8]))
-    outs[-1].start()
+    def leave(first, count, sem):
+        rows = (0, pl.ds(first, count))
+        outs.append(pltpu.make_async_copy(part.at[rows], part_hbm.at[rows], sems.at[sem]))
+        outs[-1].start()
+
+    finish = grouped(firsts)
+    for a in range(3):
+        leave(9 * a, 8, 10 + a)
+    finish()
+    for a in range(3):
+        leave(9 * a + 8, 1, 13 + a)
     for c in outs:
         c.wait()
 
@@ -271,7 +286,7 @@
         (cot_hbm.at[pl.ds(0, 2)], cot.at[pl.ds(0, 2)]),
         (cot_hbm.at[pl.ds(depth - 2, 2)], cot.at[pl.ds(2, 2)]),
         (pre_hbm.at[0], pre.at[1]), (pre_hbm.at[depth - 1], pre.at[2]),
-        (tiles_hbm, tiles), (part_hbm.at[1], part.at[1]), (in_t_hbm, in_t), (part_hbm.at[0], part.at[0]),
+        (part_hbm.at[1], part.at[1]), (tiles_hbm, tiles), (in_t_hbm, in_t), (part_hbm.at[0], part.at[0]),
     )
     copies = [pltpu.make_async_copy(a, b, sems.at[i]) for i, (a, b) in enumerate(pairs)]
     for c in copies:
@@ -289,6 +304,28 @@
     pre[0] = jnp.where(even, far_b[2], far_a[2])
     pre[3] = jnp.where(even, far_a[2], far_b[2])
     copies[6].wait()
+
+    def seconds(group, _):
+        low, high = edge_terms(act_t, cvar, 1, 6, group)
+        for k, t in enumerate(group):
+            cols = slice(k * ch, (k + 1) * ch)
+            store_tap(keep, send, 1, core, t, part[1, t] + high[:, cols], ranks)
+            store_tap(keep, send, 1, core, 9 + t, part[1, 9 + t], ranks)
+            store_tap(keep, send, 1, core, 18 + t, part[1, 18 + t] + low[:, cols], ranks)
+
+    grouped(seconds)()
+    for t in range(taps, keep.shape[1]):
+        for conv in range(2):
+            keep[conv, t] = jnp.zeros(keep.shape[2:], keep.dtype)
+            send[conv, t] = jnp.zeros(send.shape[2:], send.dtype)
+    outs = [
+        pltpu.make_async_copy(a.at[1], b.at[1], sems.at[11 + i])
+        for i, (a, b) in enumerate(((send, send_hbm), (keep, keep_hbm)))
+    ]
+    for c in outs:
+        c.start()
+
+    copies[7].wait()
     for late in range(2):
         back = back_planes(cvar, tiles, 4 * late, 1)
         grad = hidden_plane(back, pre[2 * late : 2 * late + 2])
@@ -301,27 +338,6 @@
 
     rim_out = pltpu.make_async_copy(rim, rim_hbm.at[pl.ds(0, 4)], sems.at[10])
     rim_out.start()
-    copies[7].wait()
-
-    def seconds(group, _):
-        low, high = edge_terms(act_t, cvar, 1, 6, group)
-        for k, t in enumerate(group):
-            cols = slice(k * ch, (k + 1) * ch)
-            store_tap(keep, send, 1, core, t, part[1, t] + high[:, cols], ranks)
-            store_tap(keep, send, 1, core, 9 + t, part[1, 9 + t], ranks)
-            store_tap(keep, send, 1, core, 18 + t, part[1, 18 + t] + low[:, cols], ranks)
-
-    grouped(seconds)()
-    for t in range(taps, keep.shape[1]):
-        for conv in range(2):
-            keep[conv, t] = jnp.zeros(keep.shape[2:], keep.dtype)
-            send[conv, t] = jnp.zeros(send.shape[2:], send.dtype)
-    outs = [
-        pltpu.make_async_copy(a.at[1], b.at[1], sems.at[11 + i])
-        for i, (a, b) in enumerate(((send, send_hbm), (keep, keep_hbm)))
-    ]
-    for c in outs:
-        c.start()
 
     def firsts(group, _):
         r = depth_terms(in_t, depth, hvar, [(0, 1, 1), (depth - 1, 2, 1)], group)
@@ -536,7 +552,7 @@
         (cot, pre, volume_in, weight_two),
         [many(depth), many(depth), many(depth), weights_of, shifted(depth + 2), shifted(depth - 2), turned, turned,
          tiles_of, many(depth - 2), part_of],
-        9, 3 * sweep,
+        16, 3 * sweep,
     )
     rim, keep, send = call(
         functools.partial(outer_kernel, ranks, taps),
@@ -559,7 +575,7 @@
         mine = mine + x.astype(F32)
     factor = 1.0 / math.sqrt(ranks * slabs * depth * n)
     mine = scatter_ranks(mine) * factor
-    grads = gather_slab(mine)[:, :taps]
+    grads = gather_slab(lax.optimization_barrier(mine.astype(BF16)))[:, :taps].astype(F32)
     return (input_grad[None], grads[0], grads[1])
 
 

time: 72.5 us -> 71 us (0.979)
  Pallas kernels: 35.8 us -> 34.9 us
    pallas_call x3, Pallas kernels: 33.8 us -> 32.9 us  [call(): pl.pallas_call(body, out_shape=out_shape, in_specs=[SMEM] * n_smem + [ANY...]
  transfers between devices with their start and end apart: 12 -> 12, of which waited for: 8 -> 8; matrix products, arithmetic and copies ran while one was open for 0% -> 0% of each run, Pallas kernels for 33% -> 32%
where the time goes in v4:
time: 71 us; the launch traced here: 70.8 us
  Pallas kernels  34.9 us (49%)
  starting transfers between devices  17.5 us (25%)
  waiting for transfers between devices  14.7 us (21%)
  other arithmetic  1.9 us (3%)
  local copies, waits for them, and re-layouts  0.91 us (1%)
  between operations  0.84 us (1%)
    pallas_call x3, Pallas kernels, call(): pl.pallas_call(body, out_shape=out_shape, in_specs=[SMEM] * n_smem + [ANY...  32.9 us
    ppermute x3, waiting for transfers between devices, scatter_ranks(): out = out + lax.ppermute(x, 'rep', perm).astype(F32)  5.95 us
    ppermute x3, starting transfers between devices, trade_slab(): lax.ppermute(x, 'slab', [(i, partner(i, k, peers)) for i in range(peers)])  5.73 us
    ppermute x3, starting transfers between devices, scatter_ranks(): out = out + lax.ppermute(x, 'rep', perm).astype(F32)  4.45 us
    ppermute x3, waiting for transfers between devices, gather_slab(): got = lax.ppermute(part, 'slab', perm)  3.77 us
    ppermute x2, starting transfers between devices, swap_faces(): return (lax.ppermute(to_a, 'slab', a), lax.ppermute(to_b, 'slab', b))  3.71 us
    ppermute x3, starting transfers between devices, gather_slab(): got = lax.ppermute(part, 'slab', perm)  3.55 us
    ppermute x3, waiting for transfers between devices, trade_slab(): lax.ppermute(x, 'slab', [(i, partner(i, k, peers)) for i in range(peers)])  2.55 us
  transfers between devices with their start and end apart: 12, of which 8 were waited for; matrix products, arithmetic and copies ran while one was open for 0% of the time, Pallas kernels for 32%

profile of v4, /device:TPU:0, one launch (start us, length us, event | category | flops | bytes accessed | tf_op | source)
XLA Modules:
  0.0 70.8 jit_solution(8202203444587324813)
XLA Ops:
  0.7 2.1 %shard_map.77 = (bf16[3,32,16,128]{3,2,1,0:T(8,128)(2,1)}, bf16[3,32,16,128]{3,2,1,0:T(8,128)(2,1)}) custom-call(s32[1]{0:T(128)} %bitcast.3.where_ref, bf16[8,32,16,128]{3,2,1,0:T(8,128)(2,1)} %bitcast.9, bf16[8,32,16,128]{3,2,1,0:T(8,128)(2,1)} %bitcast.12), custom_call_target="tpu_custom_call" | custom-call | tf_op jit(solution)/shard_map/pallas_call | solution.py:461
  2.7 3.0 %collective-permute-start = (bf16[3,32,16,128]{3,2,1,0:T(8,128)(2,1)}, bf16[3,32,16,128]{3,2,1,0:T(8,128)(2,1)S(1)}, u32[]{:S(2)}, u32[]{:S(2)}) collective-permute-start(bf16[3,32,16,128]{3,2,1,0:T(8,128)(2,1)} %get-tuple-element.26), channel_id=1, source_target_pairs={{0,1},{1,0},{2,3},{3,2},{4,5},{5,4},{6,7},{7,6},{8,9},{9,8},{10,11... | collective-permute-start | bytes 1179656 | tf_op jit(solution)/shard_map/ppermute | solution.py:469
  5.8 0.7 collective-permute-start.1
  6.5 16.0 %shard_map.76 = (bf16[10,32,16,128]{3,2,1,0:T(8,128)(2,1)}, f32[2,27,128,128]{3,2,1,0:T(8,128)}, bf16[21,256,256]{2,1,0:T(8,128)(2,1)}, bf16[128,5120]{1,0:T(8,128)(2,1)}) custom-call(bf16[8,32,16,128]{3,2,1,0:T(8,128)(2,1)} %bitcast.10, bf16[8,32,16,128]{3,2,1,0:T(8,128)(2,1)} %bitcast.13, bf16[8,32,16,128]{3,2,1,0:T(8,128)(2,1)} %bitcast.15, ...), custom_call_target="tpu_custom_call" | custom-call | flops 10871635968 | bytes 4030464 | tf_op jit(solution)/shard_map/pallas_call | solution.py:418
  22.5 0.0 collective-permute-done.far_a_hbm
  22.5 0.0 collective-permute-done.1.far_b_hbm
  22.5 10.0 %shard_map.78 = (bf16[10,32,16,128]{3,2,1,0:T(8,128)(2,1)}, f32[2,28,64,128]{3,2,1,0:T(8,128)}, bf16[2,28,64,128]{3,2,1,0:T(8,128)(2,1)S(1)}) custom-call(s32[1]{0:T(128)} %bitcast.3.where_ref, bf16[3,32,16,128]{3,2,1,0:T(8,128)(2,1)S(1)} %collective-permute-done.far_a_hbm, bf16[3,32,16,128]{3,2,1,0:T(8,128)(2,1)S(1)} %collective-permute-done.1.far_b_hbm, ...), custom_call_target="tpu_custom_call" | custom-call | flops 3623878656 | bytes 10485764 | tf_op jit(solution)/shard_map/pallas_call | solution.py:418
  32.5 0.1 collective-permute-start.2
  32.7 2.4 %collective-permute-done.2 = bf16[2,28,64,128]{3,2,1,0:T(8,128)(2,1)S(1)} collective-permute-done((bf16[2,28,64,128]{3,2,1,0:T(8,128)(2,1)S(1)}, bf16[2,28,64,128]{3,2,1,0:T(8,128)(2,1)S(1)}, u32[]{:S(2)}, u32[]{:S(2)}) %collective-permute-start.2) | collective-permute-done | bytes 917536 | tf_op jit(solution)/shard_map/ppermute | solution.py:474
  35.1 1.7 %add_convert_fusion = (bf16[2,7,64,128]{3,2,1,0:T(8,128)(2,1)S(1)}, bf16[2,7,64,128]{3,2,1,0:T(8,128)(2,1)S(1)}, bf16[2,7,64,128]{3,2,1,0:T(8,128)(2,1)S(1)}, f32[2,7,64,128]{3,2,1,0:T(8,128)S(1)}) fusion(f32[2,28,64,128]{3,2,1,0:T(8,128)} %get-tuple-element.32, s32[]{:T(128)S(6)} %select_n.55, bf16[2,28,64,128]{3,2,1,0:T(8,128)(2,1)S(1)} %collective-permute-done.2, ...), kind=kLoop, calls=%fused_computation.1 | loop fusion | flops 1261568 | bytes 3899408 | tf_op jit(solution)/shard_map/convert_element_type | solution.py:485
  36.8 1.6 %collective-permute-start.3 = (bf16[2,7,64,128]{3,2,1,0:T(8,128)(2,1)S(1)}, bf16[2,7,64,128]{3,2,1,0:T(8,128)(2,1)S(1)}, u32[]{:S(2)}, u32[]{:S(2)}) collective-permute-start(bf16[2,7,64,128]{3,2,1,0:T(8,128)(2,1)S(1)} %get-tuple-element.36), channel_id=1, source_target_pairs={{0,3},{1,2},{2,1},{3,0},{4,7},{5,6},{6,5},{7,4},{8,11},{9,10},{10,... | collective-permute-start | bytes 688136 | tf_op jit(solution)/shard_map/ppermute | solution.py:492
  38.3 4.2 %collective-permute-start.4 = (bf16[2,7,64,128]{3,2,1,0:T(8,128)(2,1)S(1)}, bf16[2,7,64,128]{3,2,1,0:T(8,128)(2,1)S(1)}, u32[]{:S(2)}, u32[]{:S(2)}) collective-permute-start(bf16[2,7,64,128]{3,2,1,0:T(8,128)(2,1)S(1)} %get-tuple-element.37), channel_id=1, source_target_pairs={{0,2},{1,3},{2,0},{3,1},{4,6},{5,7},{6,4},{7,5},{8,10},{9,11},{10,... | collective-permute-start | bytes 688136 | tf_op jit(solution)/shard_map/ppermute | solution.py:492
  42.5 0.0 collective-permute-start.5
  42.5 6.8 %shard_map.79 = bf16[8,32,16,128]{3,2,1,0:T(8,128)(2,1)} custom-call(bf16[10,32,16,128]{3,2,1,0:T(8,128)(2,1)} %get-tuple-element.25.hid_hbm, bf16[10,32,16,128]{3,2,1,0:T(8,128)(2,1)} %get-tuple-element.34.rim_hbm, bf16[27,128,128]{2,1,0:T(8,128)(2,1)} %w_hbm.2), custom_call_target="tpu_custom_call" | custom-call | flops 3623878656 | bytes 3506176 | tf_op jit(solution)/shard_map/pallas_call | solution.py:418
  49.4 0.0 collective-permute-done.3
  49.4 1.5 %collective-permute-done.4 = bf16[2,7,64,128]{3,2,1,0:T(8,128)(2,1)S(1)} collective-permute-done((bf16[2,7,64,128]{3,2,1,0:T(8,128)(2,1)S(1)}, bf16[2,7,64,128]{3,2,1,0:T(8,128)(2,1)S(1)}, u32[]{:S(2)}, u32[]{:S(2)}) %collective-permute-start.4) | collective-permute-done | bytes 229408 | tf_op jit(solution)/shard_map/ppermute | solution.py:492
  50.9 1.1 %collective-permute-done.5 = bf16[2,7,64,128]{3,2,1,0:T(8,128)(2,1)S(1)} collective-permute-done((bf16[2,7,64,128]{3,2,1,0:T(8,128)(2,1)S(1)}, bf16[2,7,64,128]{3,2,1,0:T(8,128)(2,1)S(1)}, u32[]{:S(2)}, u32[]{:S(2)}) %collective-permute-start.5) | collective-permute-done | bytes 229408 | tf_op jit(solution)/shard_map/ppermute | solution.py:492
  51.9 0.1 convert_add_fusion
  52.1 1.8 %collective-permute-start.8 = (bf16[2,7,16,128]{3,2,1,0:T(8,128)(2,1)S(1)}, bf16[2,7,16,128]{3,2,1,0:T(8,128)(2,1)S(1)}, u32[]{:S(2)}, u32[]{:S(2)}) collective-permute-start(bf16[2,7,16,128]{3,2,1,0:T(8,128)(2,1)S(1)} %get-tuple-element.46), channel_id=1, source_target_pairs={{0,8},{4,12},{8,0},{12,4},{16,24},{20,28},{24,16},{28,20},{1,9},{5... | collective-permute-start | bytes 172040 | tf_op jit(solution)/shard_map/ppermute | solution.py:508
  53.9 2.6 %collective-permute-start.7 = (bf16[2,7,16,128]{3,2,1,0:T(8,128)(2,1)S(1)}, bf16[2,7,16,128]{3,2,1,0:T(8,128)(2,1)S(1)}, u32[]{:S(2)}, u32[]{:S(2)}) collective-permute-start(bf16[2,7,16,128]{3,2,1,0:T(8,128)(2,1)S(1)} %get-tuple-element.45), channel_id=1, source_target_pairs={{0,16},{4,20},{8,24},{12,28},{16,0},{20,4},{24,8},{28,12},{1,17},{... | collective-permute-start | bytes 172040 | tf_op jit(solution)/shard_map/ppermute | solution.py:508
  56.5 0.0 collective-permute-start.6
  56.5 0.0 collective-permute-done.8
  56.5 3.1 %collective-permute-done.7 = bf16[2,7,16,128]{3,2,1,0:T(8,128)(2,1)S(1)} collective-permute-done((bf16[2,7,16,128]{3,2,1,0:T(8,128)(2,1)S(1)}, bf16[2,7,16,128]{3,2,1,0:T(8,128)(2,1)S(1)}, u32[]{:S(2)}, u32[]{:S(2)}) %collective-permute-start.7) | collective-permute-done | bytes 57376 | tf_op jit(solution)/shard_map/ppermute | solution.py:508
  59.6 2.9 %collective-permute-done.6 = bf16[2,7,16,128]{3,2,1,0:T(8,128)(2,1)S(1)} collective-permute-done((bf16[2,7,16,128]{3,2,1,0:T(8,128)(2,1)S(1)}, bf16[2,7,16,128]{3,2,1,0:T(8,128)(2,1)S(1)}, u32[]{:S(2)}, u32[]{:S(2)}) %collective-permute-start.6) | collective-permute-done | bytes 57376 | tf_op jit(solution)/shard_map/ppermute | solution.py:508
  62.5 2.5 %collective-permute-start.9 = (bf16[2,7,16,128]{3,2,1,0:T(8,128)(2,1)S(1)}, bf16[2,7,16,128]{3,2,1,0:T(8,128)(2,1)S(1)}, u32[]{:S(2)}, u32[]{:S(2)}) collective-permute-start(bf16[2,7,16,128]{3,2,1,0:T(8,128)(2,1)S(1)} %multiply_convert_fusion), channel_id=1, source_target_pairs={{0,3},{1,2},{2,1},{3,0},{4,7},{5,6},{6,5},{7,4},{8,11},{9,10},{10,... | collective-permute-start | bytes 172040 | tf_op jit(solution)/shard_map/ppermute | solution.py:519
  65.0 0.7 %collective-permute-start.10 = (bf16[2,7,16,128]{3,2,1,0:T(8,128)(2,1)S(1)}, bf16[2,7,16,128]{3,2,1,0:T(8,128)(2,1)S(1)}, u32[]{:S(2)}, u32[]{:S(2)}) collective-permute-start(bf16[2,7,16,128]{3,2,1,0:T(8,128)(2,1)S(1)} %multiply_convert_fusion), channel_id=1, source_target_pairs={{0,2},{1,3},{2,0},{3,1},{4,6},{5,7},{6,4},{7,5},{8,10},{9,11},{10,... | collective-permute-start | bytes 172040 | tf_op jit(solution)/shard_map/ppermute | solution.py:519
  65.8 0.3 collective-permute-start.11
  66.1 1.5 %collective-permute-done.9 = bf16[2,7,16,128]{3,2,1,0:T(8,128)(2,1)S(1)} collective-permute-done((bf16[2,7,16,128]{3,2,1,0:T(8,128)(2,1)S(1)}, bf16[2,7,16,128]{3,2,1,0:T(8,128)(2,1)S(1)}, u32[]{:S(2)}, u32[]{:S(2)}) %collective-permute-start.9) | collective-permute-done | bytes 57376 | tf_op jit(solution)/shard_map/ppermute | solution.py:519
  67.7 1.5 %collective-permute-done.10 = bf16[2,7,16,128]{3,2,1,0:T(8,128)(2,1)S(1)} collective-permute-done((bf16[2,7,16,128]{3,2,1,0:T(8,128)(2,1)S(1)}, bf16[2,7,16,128]{3,2,1,0:T(8,128)(2,1)S(1)}, u32[]{:S(2)}, u32[]{:S(2)}) %collective-permute-start.10) | collective-permute-done | bytes 57376 | tf_op jit(solution)/shard_map/ppermute | solution.py:519
  69.2 0.7 %collective-permute-done.11 = bf16[2,7,16,128]{3,2,1,0:T(8,128)(2,1)S(1)} collective-permute-done((bf16[2,7,16,128]{3,2,1,0:T(8,128)(2,1)S(1)}, bf16[2,7,16,128]{3,2,1,0:T(8,128)(2,1)S(1)}, u32[]{:S(2)}, u32[]{:S(2)}) %collective-permute-start.11) | collective-permute-done | bytes 57376 | tf_op jit(solution)/shard_map/ppermute | solution.py:519
  70.0 0.8 %slice_bitcast_fusion = (f32[27,16,128]{2,1,0:T(8,128)}, f32[27,16,128]{2,1,0:T(8,128)}) fusion(f32[2,27,16,128]{3,2,1,0:T(8,128)S(1)} %slice_convert_fusion), kind=kLoop, calls=%fused_computation.5 | loop fusion | bytes 884736 | tf_op jit(solution)/shard_map/squeeze | solution.py:579
  (8 shorter events, 0.2 us)
Async XLA Ops:
  2.7 19.7 %collective-permute-start = (bf16[3,32,16,128]{3,2,1,0:T(8,128)(2,1)}, bf16[3,32,16,128]{3,2,1,0:T(8,128)(2,1)S(1)}, u32[]{:S(2)}, u32[]{:S(2)}) collective-permute-start(bf16[3,32,16,128]{3,2,1,0:T(8,128)(2,1)} %get-tuple-element.26), channel_id=1, source_target_pairs={{0,1},{1,0},{2,3},{3,2},{4,5},{5,4},{6,7},{7,6},{8,9},{9,8},{10,11... | collective-permute-start | bytes 1179656 | tf_op jit(solution)/shard_map/ppermute | solution.py:469
  5.8 16.7 %collective-permute-start.1 = (bf16[3,32,16,128]{3,2,1,0:T(8,128)(2,1)}, bf16[3,32,16,128]{3,2,1,0:T(8,128)(2,1)S(1)}, u32[]{:S(2)}, u32[]{:S(2)}) collective-permute-start(bf16[3,32,16,128]{3,2,1,0:T(8,128)(2,1)} %get-tuple-element.27), channel_id=1, source_target_pairs={{1,2},{2,1},{5,6},{6,5},{9,10},{10,9},{13,14},{14,13},{17,18},{18,... | collective-permute-start | bytes 1179656 | tf_op jit(solution)/shard_map/ppermute | solution.py:469
  32.5 2.5 %collective-permute-start.2 = (bf16[2,28,64,128]{3,2,1,0:T(8,128)(2,1)S(1)}, bf16[2,28,64,128]{3,2,1,0:T(8,128)(2,1)S(1)}, u32[]{:S(2)}, u32[]{:S(2)}) collective-permute-start(bf16[2,28,64,128]{3,2,1,0:T(8,128)(2,1)S(1)} %get-tuple-element.33), channel_id=1, source_target_pairs={{0,4},{4,0},{8,12},{12,8},{16,20},{20,16},{24,28},{28,24},{1,5},{5... | collective-permute-start | bytes 2752520 | tf_op jit(solution)/shard_map/ppermute | solution.py:474
  36.8 12.6 %collective-permute-start.3 = (bf16[2,7,64,128]{3,2,1,0:T(8,128)(2,1)S(1)}, bf16[2,7,64,128]{3,2,1,0:T(8,128)(2,1)S(1)}, u32[]{:S(2)}, u32[]{:S(2)}) collective-permute-start(bf16[2,7,64,128]{3,2,1,0:T(8,128)(2,1)S(1)} %get-tuple-element.36), channel_id=1, source_target_pairs={{0,3},{1,2},{2,1},{3,0},{4,7},{5,6},{6,5},{7,4},{8,11},{9,10},{10,... | collective-permute-start | bytes 688136 | tf_op jit(solution)/shard_map/ppermute | solution.py:492
  38.3 12.5 %collective-permute-start.4 = (bf16[2,7,64,128]{3,2,1,0:T(8,128)(2,1)S(1)}, bf16[2,7,64,128]{3,2,1,0:T(8,128)(2,1)S(1)}, u32[]{:S(2)}, u32[]{:S(2)}) collective-permute-start(bf16[2,7,64,128]{3,2,1,0:T(8,128)(2,1)S(1)} %get-tuple-element.37), channel_id=1, source_target_pairs={{0,2},{1,3},{2,0},{3,1},{4,6},{5,7},{6,4},{7,5},{8,10},{9,11},{10,... | collective-permute-start | bytes 688136 | tf_op jit(solution)/shard_map/ppermute | solution.py:492
  42.5 9.4 %collective-permute-start.5 = (bf16[2,7,64,128]{3,2,1,0:T(8,128)(2,1)S(1)}, bf16[2,7,64,128]{3,2,1,0:T(8,128)(2,1)S(1)}, u32[]{:S(2)}, u32[]{:S(2)}) collective-permute-start(bf16[2,7,64,128]{3,2,1,0:T(8,128)(2,1)S(1)} %get-tuple-element.38), channel_id=1, source_target_pairs={{0,1},{1,0},{2,3},{3,2},{4,5},{5,4},{6,7},{7,6},{8,9},{9,8},{10,11... | collective-permute-start | bytes 688136 | tf_op jit(solution)/shard_map/ppermute | solution.py:492
  52.1 4.5 %collective-permute-start.8 = (bf16[2,7,16,128]{3,2,1,0:T(8,128)(2,1)S(1)}, bf16[2,7,16,128]{3,2,1,0:T(8,128)(2,1)S(1)}, u32[]{:S(2)}, u32[]{:S(2)}) collective-permute-start(bf16[2,7,16,128]{3,2,1,0:T(8,128)(2,1)S(1)} %get-tuple-element.46), channel_id=1, source_target_pairs={{0,8},{4,12},{8,0},{12,4},{16,24},{20,28},{24,16},{28,20},{1,9},{5... | collective-permute-start | bytes 172040 | tf_op jit(solution)/shard_map/ppermute | solution.py:508
  53.9 5.7 %collective-permute-start.7 = (bf16[2,7,16,128]{3,2,1,0:T(8,128)(2,1)S(1)}, bf16[2,7,16,128]{3,2,1,0:T(8,128)(2,1)S(1)}, u32[]{:S(2)}, u32[]{:S(2)}) collective-permute-start(bf16[2,7,16,128]{3,2,1,0:T(8,128)(2,1)S(1)} %get-tuple-element.45), channel_id=1, source_target_pairs={{0,16},{4,20},{8,24},{12,28},{16,0},{20,4},{24,8},{28,12},{1,17},{... | collective-permute-start | bytes 172040 | tf_op jit(solution)/shard_map/ppermute | solution.py:508
  56.5 6.0 %collective-permute-start.6 = (bf16[2,7,16,128]{3,2,1,0:T(8,128)(2,1)S(1)}, bf16[2,7,16,128]{3,2,1,0:T(8,128)(2,1)S(1)}, u32[]{:S(2)}, u32[]{:S(2)}) collective-permute-start(bf16[2,7,16,128]{3,2,1,0:T(8,128)(2,1)S(1)} %get-tuple-element.44), channel_id=1, source_target_pairs={{0,24},{4,28},{8,16},{12,20},{16,8},{20,12},{24,0},{28,4},{1,25},{... | collective-permute-start | bytes 172040 | tf_op jit(solution)/shard_map/ppermute | solution.py:508
  62.5 5.1 %collective-permute-start.9 = (bf16[2,7,16,128]{3,2,1,0:T(8,128)(2,1)S(1)}, bf16[2,7,16,128]{3,2,1,0:T(8,128)(2,1)S(1)}, u32[]{:S(2)}, u32[]{:S(2)}) collective-permute-start(bf16[2,7,16,128]{3,2,1,0:T(8,128)(2,1)S(1)} %multiply_convert_fusion), channel_id=1, source_target_pairs={{0,3},{1,2},{2,1},{3,0},{4,7},{5,6},{6,5},{7,4},{8,11},{9,10},{10,... | collective-permute-start | bytes 172040 | tf_op jit(solution)/shard_map/ppermute | solution.py:519
  65.0 4.2 %collective-permute-start.10 = (bf16[2,7,16,128]{3,2,1,0:T(8,128)(2,1)S(1)}, bf16[2,7,16,128]{3,2,1,0:T(8,128)(2,1)S(1)}, u32[]{:S(2)}, u32[]{:S(2)}) collective-permute-start(bf16[2,7,16,128]{3,2,1,0:T(8,128)(2,1)S(1)} %multiply_convert_fusion), channel_id=1, source_target_pairs={{0,2},{1,3},{2,0},{3,1},{4,6},{5,7},{6,4},{7,5},{8,10},{9,11},{10,... | collective-permute-start | bytes 172040 | tf_op jit(solution)/shard_map/ppermute | solution.py:519
  65.8 4.2 %collective-permute-start.11 = (bf16[2,7,16,128]{3,2,1,0:T(8,128)(2,1)S(1)}, bf16[2,7,16,128]{3,2,1,0:T(8,128)(2,1)S(1)}, u32[]{:S(2)}, u32[]{:S(2)}) collective-permute-start(bf16[2,7,16,128]{3,2,1,0:T(8,128)(2,1)S(1)} %multiply_convert_fusion), channel_id=1, source_target_pairs={{0,1},{1,0},{2,3},{3,2},{4,5},{5,4},{6,7},{7,6},{8,9},{9,8},{10,11... | collective-permute-start | bytes 172040 | tf_op jit(solution)/shard_map/ppermute | solution.py:519

commit v5 on v4

--- a/solution.py
+++ b/solution.py
@@ -167,12 +167,12 @@
     return (back * (s * (1.0 + v * (1.0 - s)))).astype(BF16)
 
 
-def loop(start, stop, body):
+def loop(start, stop, body, unroll=1):
     def step(i, carry):
         body(i)
         return carry
 
-    lax.fori_loop(start, stop, step, 0)
+    lax.fori_loop(start, stop, step, 0, unroll=unroll)
 
 
 def clear_ends(left, depth):
@@ -210,7 +210,7 @@
         for c in copies[2 * k : 2 * k + 2]:
             c.wait()
 
-        @functools.partial(loop, k * half, (k + 1) * half)
+        @functools.partial(loop, k * half, (k + 1) * half, unroll=half)
         def _(d):
             fill_plane(var, d + 1, cot[d])
             transpose_plane(act_t, d + 1, silu_of(pre[d]))
@@ -244,7 +244,7 @@
     outs.append(pltpu.make_async_copy(hid, hid_hbm.at[pl.ds(2, middle)], sems.at[9]))
     outs[-1].start()
 
-    @functools.partial(loop, 0, middle)
+    @functools.partial(loop, 0, middle, unroll=middle)
     def _(d):
         fill_plane(hvar, d, hid[d])
 
@@ -434,22 +434,28 @@
     return i ^ k if n & (n - 1) == 0 else (i + k) % n
 
 
-def faces_kernel(where_ref, cot_hbm, pre_hbm, a_ref, b_ref, sems):
+def faces_kernel(where_ref, cot_hbm, pre_hbm, a_hbm, b_hbm, a, b, sems):
     depth = cot_hbm.shape[0]
     first = bit(where_ref[0], 0)
-    copies = []
-    for i, (out, low) in enumerate(((a_ref, first), (b_ref, 1 - first))):
-        for k, (x, count) in enumerate(((cot_hbm, 2), (pre_hbm, 1))):
-            start = (1 - low) * (depth - count)
-            copies.append(
-                pltpu.make_async_copy(
-                    x.at[pl.ds(start, count)], out.at[pl.ds(2 * k, count)], sems.at[2 * i + k]
+    moves = []
+    for out_hbm, out, low in ((a_hbm, a, first), (b_hbm, b, 1 - first)):
+        for at, x, count in ((0, cot_hbm, 2), (2, pre_hbm, 1)):
+            part = pl.ds(at, count)
+            here = x.at[pl.ds((1 - low) * (depth - count), count)]
+            k = 2 * len(moves)
+            moves.append(
+                (
+                    pltpu.make_async_copy(here, out.at[part], sems.at[k]),
+                    pltpu.make_async_copy(out.at[part], out_hbm.at[part], sems.at[k + 1]),
                 )
             )
-    for c in copies:
-        c.start()
-    for c in copies:
-        c.wait()
+    for take, _ in moves:
+        take.start()
+    for take, give in moves:
+        take.wait()
+        give.start()
+    for _, give in moves:
+        give.wait()
 
 
 def swap_faces(where, cot, pre):
@@ -457,13 +463,12 @@
     a = [(i, i ^ 1) for i in range(peers) if i ^ 1 < peers]
     b = [(i, j) for i in range(peers) for j in [((i + 1) ^ 1) - 1] if 0 <= j < peers]
     face = jax.ShapeDtypeStruct((3,) + cot.shape[1:], cot.dtype)
-    vmem = pl.BlockSpec(memory_space=pltpu.VMEM)
     to_a, to_b = pl.pallas_call(
         faces_kernel,
         out_shape=(face, face),
         in_specs=[SMEM, HBM, HBM],
-        out_specs=(vmem, vmem),
-        scratch_shapes=[pltpu.SemaphoreType.DMA((4,))],
+        out_specs=(ANY, ANY),
+        scratch_shapes=[pltpu.VMEM(face.shape, face.dtype)] * 2 + [pltpu.SemaphoreType.DMA((8,))],
         compiler_params=pltpu.CompilerParams(vmem_limit_bytes=LIMIT),
     )(where, cot, pre)
     return lax.ppermute(to_a, "slab", a), lax.ppermute(to_b, "slab", b)

time: 71 us -> 70.5 us (level)
  no operation moved by 1% of the time
where the time goes in v5:
time: 70.5 us; the launch traced here: 70.3 us
  Pallas kernels  34.5 us (49%)
  starting transfers between devices  17.5 us (25%)
  waiting for transfers between devices  14.7 us (21%)
  other arithmetic  1.9 us (3%)
  local copies, waits for them, and re-layouts  0.91 us (1%)
  between operations  0.84 us (1%)
    pallas_call x3, Pallas kernels, call(): pl.pallas_call(body, out_shape=out_shape, in_specs=[SMEM] * n_smem + [ANY...  32.6 us
    ppermute x3, waiting for transfers between devices, scatter_ranks(): out = out + lax.ppermute(x, 'rep', perm).astype(F32)  5.93 us
    ppermute x3, starting transfers between devices, trade_slab(): lax.ppermute(x, 'slab', [(i, partner(i, k, peers)) for i in range(peers)])  5.75 us
    ppermute x3, starting transfers between devices, scatter_ranks(): out = out + lax.ppermute(x, 'rep', perm).astype(F32)  4.45 us
    ppermute x3, waiting for transfers between devices, gather_slab(): got = lax.ppermute(part, 'slab', perm)  3.77 us
    ppermute x2, starting transfers between devices, swap_faces(): return (lax.ppermute(to_a, 'slab', a), lax.ppermute(to_b, 'slab', b))  3.71 us
    ppermute x3, starting transfers between devices, gather_slab(): got = lax.ppermute(part, 'slab', perm)  3.55 us
    ppermute x3, waiting for transfers between devices, trade_slab(): lax.ppermute(x, 'slab', [(i, partner(i, k, peers)) for i in range(peers)])  2.55 us
  transfers between devices with their start and end apart: 12, of which 8 were waited for; matrix products, arithmetic and copies ran while one was open for 0% of the time, Pallas kernels for 32%

profile of v5, /device:TPU:0, one launch (start us, length us, event | category | flops | bytes accessed | tf_op | source)
XLA Modules:
  0.0 70.3 jit_solution(5171235455036784357)
XLA Ops:
  0.7 1.9 %shard_map.77 = (bf16[3,32,16,128]{3,2,1,0:T(8,128)(2,1)}, bf16[3,32,16,128]{3,2,1,0:T(8,128)(2,1)}) custom-call(s32[1]{0:T(128)} %bitcast.3.where_ref, bf16[8,32,16,128]{3,2,1,0:T(8,128)(2,1)} %bitcast.9, bf16[8,32,16,128]{3,2,1,0:T(8,128)(2,1)} %bitcast.12), custom_call_target="tpu_custom_call" | custom-call | tf_op jit(solution)/shard_map/pallas_call | solution.py:466
  2.6 3.0 %collective-permute-start = (bf16[3,32,16,128]{3,2,1,0:T(8,128)(2,1)}, bf16[3,32,16,128]{3,2,1,0:T(8,128)(2,1)S(1)}, u32[]{:S(2)}, u32[]{:S(2)}) collective-permute-start(bf16[3,32,16,128]{3,2,1,0:T(8,128)(2,1)} %get-tuple-element.26), channel_id=1, source_target_pairs={{0,1},{1,0},{2,3},{3,2},{4,5},{5,4},{6,7},{7,6},{8,9},{9,8},{10,11... | collective-permute-start | bytes 1179656 | tf_op jit(solution)/shard_map/ppermute | solution.py:474
  5.6 0.7 collective-permute-start.1
  6.3 15.7 %shard_map.76 = (bf16[10,32,16,128]{3,2,1,0:T(8,128)(2,1)}, f32[2,27,128,128]{3,2,1,0:T(8,128)}, bf16[21,256,256]{2,1,0:T(8,128)(2,1)}, bf16[128,5120]{1,0:T(8,128)(2,1)}) custom-call(bf16[8,32,16,128]{3,2,1,0:T(8,128)(2,1)} %bitcast.10, bf16[8,32,16,128]{3,2,1,0:T(8,128)(2,1)} %bitcast.13, bf16[8,32,16,128]{3,2,1,0:T(8,128)(2,1)} %bitcast.15, ...), custom_call_target="tpu_custom_call" | custom-call | flops 10871635968 | bytes 4030464 | tf_op jit(solution)/shard_map/pallas_call | solution.py:418
  22.0 0.0 collective-permute-done.far_a_hbm
  22.0 0.0 collective-permute-done.1.far_b_hbm
  22.0 10.0 %shard_map.78 = (bf16[10,32,16,128]{3,2,1,0:T(8,128)(2,1)}, f32[2,28,64,128]{3,2,1,0:T(8,128)}, bf16[2,28,64,128]{3,2,1,0:T(8,128)(2,1)S(1)}) custom-call(s32[1]{0:T(128)} %bitcast.3.where_ref, bf16[3,32,16,128]{3,2,1,0:T(8,128)(2,1)S(1)} %collective-permute-done.far_a_hbm, bf16[3,32,16,128]{3,2,1,0:T(8,128)(2,1)S(1)} %collective-permute-done.1.far_b_hbm, ...), custom_call_target="tpu_custom_call" | custom-call | flops 3623878656 | bytes 10485764 | tf_op jit(solution)/shard_map/pallas_call | solution.py:418
  32.1 0.1 collective-permute-start.2
  32.2 2.4 %collective-permute-done.2 = bf16[2,28,64,128]{3,2,1,0:T(8,128)(2,1)S(1)} collective-permute-done((bf16[2,28,64,128]{3,2,1,0:T(8,128)(2,1)S(1)}, bf16[2,28,64,128]{3,2,1,0:T(8,128)(2,1)S(1)}, u32[]{:S(2)}, u32[]{:S(2)}) %collective-permute-start.2) | collective-permute-done | bytes 917536 | tf_op jit(solution)/shard_map/ppermute | solution.py:479
  34.6 1.7 %add_convert_fusion = (bf16[2,7,64,128]{3,2,1,0:T(8,128)(2,1)S(1)}, bf16[2,7,64,128]{3,2,1,0:T(8,128)(2,1)S(1)}, bf16[2,7,64,128]{3,2,1,0:T(8,128)(2,1)S(1)}, f32[2,7,64,128]{3,2,1,0:T(8,128)S(1)}) fusion(f32[2,28,64,128]{3,2,1,0:T(8,128)} %get-tuple-element.32, s32[]{:T(128)S(6)} %select_n.55, bf16[2,28,64,128]{3,2,1,0:T(8,128)(2,1)S(1)} %collective-permute-done.2, ...), kind=kLoop, calls=%fused_computation.1 | loop fusion | flops 1261568 | bytes 3899408 | tf_op jit(solution)/shard_map/convert_element_type | solution.py:490
  36.3 1.6 %collective-permute-start.3 = (bf16[2,7,64,128]{3,2,1,0:T(8,128)(2,1)S(1)}, bf16[2,7,64,128]{3,2,1,0:T(8,128)(2,1)S(1)}, u32[]{:S(2)}, u32[]{:S(2)}) collective-permute-start(bf16[2,7,64,128]{3,2,1,0:T(8,128)(2,1)S(1)} %get-tuple-element.36), channel_id=1, source_target_pairs={{0,3},{1,2},{2,1},{3,0},{4,7},{5,6},{6,5},{7,4},{8,11},{9,10},{10,... | collective-permute-start | bytes 688136 | tf_op jit(solution)/shard_map/ppermute | solution.py:497
  37.9 4.2 %collective-permute-start.4 = (bf16[2,7,64,128]{3,2,1,0:T(8,128)(2,1)S(1)}, bf16[2,7,64,128]{3,2,1,0:T(8,128)(2,1)S(1)}, u32[]{:S(2)}, u32[]{:S(2)}) collective-permute-start(bf16[2,7,64,128]{3,2,1,0:T(8,128)(2,1)S(1)} %get-tuple-element.37), channel_id=1, source_target_pairs={{0,2},{1,3},{2,0},{3,1},{4,6},{5,7},{6,4},{7,5},{8,10},{9,11},{10,... | collective-permute-start | bytes 688136 | tf_op jit(solution)/shard_map/ppermute | solution.py:497
  42.1 0.0 collective-permute-start.5
  42.1 6.8 %shard_map.79 = bf16[8,32,16,128]{3,2,1,0:T(8,128)(2,1)} custom-call(bf16[10,32,16,128]{3,2,1,0:T(8,128)(2,1)} %get-tuple-element.25.hid_hbm, bf16[10,32,16,128]{3,2,1,0:T(8,128)(2,1)} %get-tuple-element.34.rim_hbm, bf16[27,128,128]{2,1,0:T(8,128)(2,1)} %w_hbm.2), custom_call_target="tpu_custom_call" | custom-call | flops 3623878656 | bytes 3506176 | tf_op jit(solution)/shard_map/pallas_call | solution.py:418
  48.9 0.0 collective-permute-done.3
  48.9 1.5 %collective-permute-done.4 = bf16[2,7,64,128]{3,2,1,0:T(8,128)(2,1)S(1)} collective-permute-done((bf16[2,7,64,128]{3,2,1,0:T(8,128)(2,1)S(1)}, bf16[2,7,64,128]{3,2,1,0:T(8,128)(2,1)S(1)}, u32[]{:S(2)}, u32[]{:S(2)}) %collective-permute-start.4) | collective-permute-done | bytes 229408 | tf_op jit(solution)/shard_map/ppermute | solution.py:497
  50.4 1.1 %collective-permute-done.5 = bf16[2,7,64,128]{3,2,1,0:T(8,128)(2,1)S(1)} collective-permute-done((bf16[2,7,64,128]{3,2,1,0:T(8,128)(2,1)S(1)}, bf16[2,7,64,128]{3,2,1,0:T(8,128)(2,1)S(1)}, u32[]{:S(2)}, u32[]{:S(2)}) %collective-permute-start.5) | collective-permute-done | bytes 229408 | tf_op jit(solution)/shard_map/ppermute | solution.py:497
  51.5 0.1 convert_add_fusion
  51.6 1.8 %collective-permute-start.8 = (bf16[2,7,16,128]{3,2,1,0:T(8,128)(2,1)S(1)}, bf16[2,7,16,128]{3,2,1,0:T(8,128)(2,1)S(1)}, u32[]{:S(2)}, u32[]{:S(2)}) collective-permute-start(bf16[2,7,16,128]{3,2,1,0:T(8,128)(2,1)S(1)} %get-tuple-element.46), channel_id=1, source_target_pairs={{0,8},{4,12},{8,0},{12,4},{16,24},{20,28},{24,16},{28,20},{1,9},{5... | collective-permute-start | bytes 172040 | tf_op jit(solution)/shard_map/ppermute | solution.py:513
  53.5 2.6 %collective-permute-start.7 = (bf16[2,7,16,128]{3,2,1,0:T(8,128)(2,1)S(1)}, bf16[2,7,16,128]{3,2,1,0:T(8,128)(2,1)S(1)}, u32[]{:S(2)}, u32[]{:S(2)}) collective-permute-start(bf16[2,7,16,128]{3,2,1,0:T(8,128)(2,1)S(1)} %get-tuple-element.45), channel_id=1, source_target_pairs={{0,16},{4,20},{8,24},{12,28},{16,0},{20,4},{24,8},{28,12},{1,17},{... | collective-permute-start | bytes 172040 | tf_op jit(solution)/shard_map/ppermute | solution.py:513
  56.0 0.0 collective-permute-start.6
  56.1 0.0 collective-permute-done.8
  56.1 3.1 %collective-permute-done.7 = bf16[2,7,16,128]{3,2,1,0:T(8,128)(2,1)S(1)} collective-permute-done((bf16[2,7,16,128]{3,2,1,0:T(8,128)(2,1)S(1)}, bf16[2,7,16,128]{3,2,1,0:T(8,128)(2,1)S(1)}, u32[]{:S(2)}, u32[]{:S(2)}) %collective-permute-start.7) | collective-permute-done | bytes 57376 | tf_op jit(solution)/shard_map/ppermute | solution.py:513
  59.1 2.9 %collective-permute-done.6 = bf16[2,7,16,128]{3,2,1,0:T(8,128)(2,1)S(1)} collective-permute-done((bf16[2,7,16,128]{3,2,1,0:T(8,128)(2,1)S(1)}, bf16[2,7,16,128]{3,2,1,0:T(8,128)(2,1)S(1)}, u32[]{:S(2)}, u32[]{:S(2)}) %collective-permute-start.6) | collective-permute-done | bytes 57376 | tf_op jit(solution)/shard_map/ppermute | solution.py:513
  62.1 2.5 %collective-permute-start.9 = (bf16[2,7,16,128]{3,2,1,0:T(8,128)(2,1)S(1)}, bf16[2,7,16,128]{3,2,1,0:T(8,128)(2,1)S(1)}, u32[]{:S(2)}, u32[]{:S(2)}) collective-permute-start(bf16[2,7,16,128]{3,2,1,0:T(8,128)(2,1)S(1)} %multiply_convert_fusion), channel_id=1, source_target_pairs={{0,3},{1,2},{2,1},{3,0},{4,7},{5,6},{6,5},{7,4},{8,11},{9,10},{10,... | collective-permute-start | bytes 172040 | tf_op jit(solution)/shard_map/ppermute | solution.py:524
  64.6 0.7 %collective-permute-start.10 = (bf16[2,7,16,128]{3,2,1,0:T(8,128)(2,1)S(1)}, bf16[2,7,16,128]{3,2,1,0:T(8,128)(2,1)S(1)}, u32[]{:S(2)}, u32[]{:S(2)}) collective-permute-start(bf16[2,7,16,128]{3,2,1,0:T(8,128)(2,1)S(1)} %multiply_convert_fusion), channel_id=1, source_target_pairs={{0,2},{1,3},{2,0},{3,1},{4,6},{5,7},{6,4},{7,5},{8,10},{9,11},{10,... | collective-permute-start | bytes 172040 | tf_op jit(solution)/shard_map/ppermute | solution.py:524
  65.3 0.3 collective-permute-start.11
  65.7 1.5 %collective-permute-done.9 = bf16[2,7,16,128]{3,2,1,0:T(8,128)(2,1)S(1)} collective-permute-done((bf16[2,7,16,128]{3,2,1,0:T(8,128)(2,1)S(1)}, bf16[2,7,16,128]{3,2,1,0:T(8,128)(2,1)S(1)}, u32[]{:S(2)}, u32[]{:S(2)}) %collective-permute-start.9) | collective-permute-done | bytes 57376 | tf_op jit(solution)/shard_map/ppermute | solution.py:524
  67.2 1.5 %collective-permute-done.10 = bf16[2,7,16,128]{3,2,1,0:T(8,128)(2,1)S(1)} collective-permute-done((bf16[2,7,16,128]{3,2,1,0:T(8,128)(2,1)S(1)}, bf16[2,7,16,128]{3,2,1,0:T(8,128)(2,1)S(1)}, u32[]{:S(2)}, u32[]{:S(2)}) %collective-permute-start.10) | collective-permute-done | bytes 57376 | tf_op jit(solution)/shard_map/ppermute | solution.py:524
  68.8 0.7 collective-permute-done.11
  69.5 0.8 %slice_bitcast_fusion = (f32[27,16,128]{2,1,0:T(8,128)}, f32[27,16,128]{2,1,0:T(8,128)}) fusion(f32[2,27,16,128]{3,2,1,0:T(8,128)S(1)} %slice_convert_fusion), kind=kLoop, calls=%fused_computation.5 | loop fusion | bytes 884736 | tf_op jit(solution)/shard_map/squeeze | solution.py:584
  (8 shorter events, 0.2 us)
Async XLA Ops:
  2.6 19.5 %collective-permute-start = (bf16[3,32,16,128]{3,2,1,0:T(8,128)(2,1)}, bf16[3,32,16,128]{3,2,1,0:T(8,128)(2,1)S(1)}, u32[]{:S(2)}, u32[]{:S(2)}) collective-permute-start(bf16[3,32,16,128]{3,2,1,0:T(8,128)(2,1)} %get-tuple-element.26), channel_id=1, source_target_pairs={{0,1},{1,0},{2,3},{3,2},{4,5},{5,4},{6,7},{7,6},{8,9},{9,8},{10,11... | collective-permute-start | bytes 1179656 | tf_op jit(solution)/shard_map/ppermute | solution.py:474
  5.6 16.4 %collective-permute-start.1 = (bf16[3,32,16,128]{3,2,1,0:T(8,128)(2,1)}, bf16[3,32,16,128]{3,2,1,0:T(8,128)(2,1)S(1)}, u32[]{:S(2)}, u32[]{:S(2)}) collective-permute-start(bf16[3,32,16,128]{3,2,1,0:T(8,128)(2,1)} %get-tuple-element.27), channel_id=1, source_target_pairs={{1,2},{2,1},{5,6},{6,5},{9,10},{10,9},{13,14},{14,13},{17,18},{18,... | collective-permute-start | bytes 1179656 | tf_op jit(solution)/shard_map/ppermute | solution.py:474
  32.1 2.5 %collective-permute-start.2 = (bf16[2,28,64,128]{3,2,1,0:T(8,128)(2,1)S(1)}, bf16[2,28,64,128]{3,2,1,0:T(8,128)(2,1)S(1)}, u32[]{:S(2)}, u32[]{:S(2)}) collective-permute-start(bf16[2,28,64,128]{3,2,1,0:T(8,128)(2,1)S(1)} %get-tuple-element.33), channel_id=1, source_target_pairs={{0,4},{4,0},{8,12},{12,8},{16,20},{20,16},{24,28},{28,24},{1,5},{5... | collective-permute-start | bytes 2752520 | tf_op jit(solution)/shard_map/ppermute | solution.py:479
  36.3 12.6 %collective-permute-start.3 = (bf16[2,7,64,128]{3,2,1,0:T(8,128)(2,1)S(1)}, bf16[2,7,64,128]{3,2,1,0:T(8,128)(2,1)S(1)}, u32[]{:S(2)}, u32[]{:S(2)}) collective-permute-start(bf16[2,7,64,128]{3,2,1,0:T(8,128)(2,1)S(1)} %get-tuple-element.36), channel_id=1, source_target_pairs={{0,3},{1,2},{2,1},{3,0},{4,7},{5,6},{6,5},{7,4},{8,11},{9,10},{10,... | collective-permute-start | bytes 688136 | tf_op jit(solution)/shard_map/ppermute | solution.py:497
  37.9 12.5 %collective-permute-start.4 = (bf16[2,7,64,128]{3,2,1,0:T(8,128)(2,1)S(1)}, bf16[2,7,64,128]{3,2,1,0:T(8,128)(2,1)S(1)}, u32[]{:S(2)}, u32[]{:S(2)}) collective-permute-start(bf16[2,7,64,128]{3,2,1,0:T(8,128)(2,1)S(1)} %get-tuple-element.37), channel_id=1, source_target_pairs={{0,2},{1,3},{2,0},{3,1},{4,6},{5,7},{6,4},{7,5},{8,10},{9,11},{10,... | collective-permute-start | bytes 688136 | tf_op jit(solution)/shard_map/ppermute | solution.py:497
  42.1 9.4 %collective-permute-start.5 = (bf16[2,7,64,128]{3,2,1,0:T(8,128)(2,1)S(1)}, bf16[2,7,64,128]{3,2,1,0:T(8,128)(2,1)S(1)}, u32[]{:S(2)}, u32[]{:S(2)}) collective-permute-start(bf16[2,7,64,128]{3,2,1,0:T(8,128)(2,1)S(1)} %get-tuple-element.38), channel_id=1, source_target_pairs={{0,1},{1,0},{2,3},{3,2},{4,5},{5,4},{6,7},{7,6},{8,9},{9,8},{10,11... | collective-permute-start | bytes 688136 | tf_op jit(solution)/shard_map/ppermute | solution.py:497
  51.6 4.5 %collective-permute-start.8 = (bf16[2,7,16,128]{3,2,1,0:T(8,128)(2,1)S(1)}, bf16[2,7,16,128]{3,2,1,0:T(8,128)(2,1)S(1)}, u32[]{:S(2)}, u32[]{:S(2)}) collective-permute-start(bf16[2,7,16,128]{3,2,1,0:T(8,128)(2,1)S(1)} %get-tuple-element.46), channel_id=1, source_target_pairs={{0,8},{4,12},{8,0},{12,4},{16,24},{20,28},{24,16},{28,20},{1,9},{5... | collective-permute-start | bytes 172040 | tf_op jit(solution)/shard_map/ppermute | solution.py:513
  53.5 5.7 %collective-permute-start.7 = (bf16[2,7,16,128]{3,2,1,0:T(8,128)(2,1)S(1)}, bf16[2,7,16,128]{3,2,1,0:T(8,128)(2,1)S(1)}, u32[]{:S(2)}, u32[]{:S(2)}) collective-permute-start(bf16[2,7,16,128]{3,2,1,0:T(8,128)(2,1)S(1)} %get-tuple-element.45), channel_id=1, source_target_pairs={{0,16},{4,20},{8,24},{12,28},{16,0},{20,4},{24,8},{28,12},{1,17},{... | collective-permute-start | bytes 172040 | tf_op jit(solution)/shard_map/ppermute | solution.py:513
  56.0 6.0 %collective-permute-start.6 = (bf16[2,7,16,128]{3,2,1,0:T(8,128)(2,1)S(1)}, bf16[2,7,16,128]{3,2,1,0:T(8,128)(2,1)S(1)}, u32[]{:S(2)}, u32[]{:S(2)}) collective-permute-start(bf16[2,7,16,128]{3,2,1,0:T(8,128)(2,1)S(1)} %get-tuple-element.44), channel_id=1, source_target_pairs={{0,24},{4,28},{8,16},{12,20},{16,8},{20,12},{24,0},{28,4},{1,25},{... | collective-permute-start | bytes 172040 | tf_op jit(solution)/shard_map/ppermute | solution.py:513
  62.1 5.1 %collective-permute-start.9 = (bf16[2,7,16,128]{3,2,1,0:T(8,128)(2,1)S(1)}, bf16[2,7,16,128]{3,2,1,0:T(8,128)(2,1)S(1)}, u32[]{:S(2)}, u32[]{:S(2)}) collective-permute-start(bf16[2,7,16,128]{3,2,1,0:T(8,128)(2,1)S(1)} %multiply_convert_fusion), channel_id=1, source_target_pairs={{0,3},{1,2},{2,1},{3,0},{4,7},{5,6},{6,5},{7,4},{8,11},{9,10},{10,... | collective-permute-start | bytes 172040 | tf_op jit(solution)/shard_map/ppermute | solution.py:524
  64.6 4.2 %collective-permute-start.10 = (bf16[2,7,16,128]{3,2,1,0:T(8,128)(2,1)S(1)}, bf16[2,7,16,128]{3,2,1,0:T(8,128)(2,1)S(1)}, u32[]{:S(2)}, u32[]{:S(2)}) collective-permute-start(bf16[2,7,16,128]{3,2,1,0:T(8,128)(2,1)S(1)} %multiply_convert_fusion), channel_id=1, source_target_pairs={{0,2},{1,3},{2,0},{3,1},{4,6},{5,7},{6,4},{7,5},{8,10},{9,11},{10,... | collective-permute-start | bytes 172040 | tf_op jit(solution)/shard_map/ppermute | solution.py:524
  65.3 4.2 %collective-permute-start.11 = (bf16[2,7,16,128]{3,2,1,0:T(8,128)(2,1)S(1)}, bf16[2,7,16,128]{3,2,1,0:T(8,128)(2,1)S(1)}, u32[]{:S(2)}, u32[]{:S(2)}) collective-permute-start(bf16[2,7,16,128]{3,2,1,0:T(8,128)(2,1)S(1)} %multiply_convert_fusion), channel_id=1, source_target_pairs={{0,1},{1,0},{2,3},{3,2},{4,5},{5,4},{6,7},{7,6},{8,9},{9,8},{10,11... | collective-permute-start | bytes 172040 | tf_op jit(solution)/shard_map/ppermute | solution.py:524
